TPU v7x, 256 devices: a whole 4x4x8 slice. The times are simulated.
256 devices in a mesh: feat: 64 (over x, z, core), node: 4 (over y).
Axes of the slice: x: 4, y: 4, z: 8, core: 2. Of those that a mesh axis runs over, the one named last changes fastest.
Arguments:
- features: bfloat16 [32768, 1024], P(None, 'feat'), may hold values from -6 to 6
- w_self: bfloat16 [1024, 256], P('feat'), may hold values from -0.1875 to 0.1875
- w_neigh: bfloat16 [1024, 256], P('feat'), may hold values from -0.75 to 0.75
- bias: float32 [256], replicated, may hold values from -3 to 3
- d_out: bfloat16 [32768, 256], P(('node', 'feat')), may hold values from -6 to 6
- nbr_ids: int32 [256, 16], P('node'), may hold values from 0 to 255, as said below
- nbr_count: int32 [256], P('node'), may hold values from 1 to 16, as said below
- tiles: int32 [256, 16, 8, 128], P('node'), may hold values from 0 to 65535, as said below
Outputs:
- activated: bfloat16 [32768, 256], P(('node', 'feat'))
- grad_features: float32 [32768, 1024], P('node', 'feat')
- grad_self: float32 [1024, 256], P('feat')
- grad_neigh: float32 [1024, 256], P('feat')
Inputs may be any that keep to these rules, and one draw needn't show every extreme that they name: `nbr_ids`: the ids of one block row are distinct; only the first nbr_count slots of a row are live, the others hold ids and tiles that must be ignored. `nbr_count`: some block row of every draw has exactly 16 live slots. `tiles`: bits for destination rows 128 and above are zero; some destination nodes have no edges at all.
All inputs are finite; a program needn't handle non-finite values.
Results may differ from a plain program's by a relative error of at most 0.0075.
Values may be sent and summed in bfloat16 or wider, within the bound.
A program may use at most 64 MiB of HBM per device.

v0:
```python
import math

import jax
import jax.numpy as jnp
from jax import lax
from jax.sharding import PartitionSpec as P


def unpack(packed):
    shifts = jnp.arange(16, dtype=jnp.int32)
    bit_planes = jnp.bitwise_and(jnp.right_shift(packed[..., :, None, :], shifts[:, None]), 1)
    flat_shape = packed.shape[:-2] + (packed.shape[-2] * 16, packed.shape[-1])
    return bit_planes.reshape(flat_shape)


def shards(features, w_self, w_neigh, bias, d_out, nbr_ids, nbr_count, tiles):
    node_total = features.shape[0]
    feat_cols = features.shape[1]
    block_size = tiles.shape[3]
    blocks_here = nbr_ids.shape[0]
    group_rows = blocks_here * block_size
    all_blocks = node_total // block_size
    slot_total = nbr_ids.shape[1]
    node_group = lax.axis_index("node")
    blocked = features.reshape(all_blocks, block_size, feat_cols)

    def slot_tiles(slot_idx):
        packed = lax.dynamic_index_in_dim(tiles, slot_idx, 1, keepdims=False)
        block_ids = lax.dynamic_index_in_dim(nbr_ids, slot_idx, 1, keepdims=False)
        live_mask = (slot_idx < nbr_count).astype(jnp.float32)
        adjacency = unpack(packed).astype(jnp.bfloat16)
        return (adjacency, block_ids, live_mask)

    def forward_slot(slot_idx, state_pair):
        neigh_sum, degree = state_pair
        adjacency, block_ids, live_mask = slot_tiles(slot_idx)
        source = blocked[block_ids]
        product = jnp.einsum("bij,bjc->bic", adjacency, source, preferred_element_type=jnp.float32)
        neigh_sum = neigh_sum + product * live_mask[:, None, None]
        degree = degree + jnp.sum(adjacency, axis=2, dtype=jnp.float32) * live_mask[:, None]
        return (neigh_sum, degree)

    neigh_sum, degree = lax.fori_loop(
        0,
        slot_total,
        forward_slot,
        (
            jnp.zeros((blocks_here, block_size, feat_cols), jnp.float32),
            jnp.zeros((blocks_here, block_size), jnp.float32),
        ),
    )
    denom = jnp.maximum(degree, 1.0)
    neigh_mean = (neigh_sum / denom[..., None]).astype(jnp.bfloat16).reshape(group_rows, feat_cols)
    own_rows = lax.dynamic_slice_in_dim(features, node_group * group_rows, group_rows, 0)
    pre_act = (
        lax.psum_scatter(
            jnp.dot(own_rows, w_self, preferred_element_type=jnp.float32)
            + jnp.dot(neigh_mean, w_neigh, preferred_element_type=jnp.float32),
            "feat",
            scatter_dimension=0,
            tiled=True,
        )
        + bias
    )
    activated = jax.nn.elu(pre_act).astype(jnp.bfloat16)
    elu_slope = jnp.where(pre_act > 0, 1.0, jnp.exp(jnp.minimum(pre_act, 0.0)))
    dpre = (d_out.astype(jnp.float32) * elu_slope).astype(jnp.bfloat16)
    dpre_group = lax.all_gather(dpre, "feat", axis=0, tiled=True)
    part_self = lax.dot_general(
        own_rows, dpre_group, (((0,), (0,)), ((), ())), preferred_element_type=jnp.float32
    )
    part_neigh = lax.dot_general(
        neigh_mean, dpre_group, (((0,), (0,)), ((), ())), preferred_element_type=jnp.float32
    )
    sum_self, sum_neigh = lax.psum((part_self, part_neigh), "node")
    d_self = lax.dot_general(
        dpre_group, w_self, (((1,), (1,)), ((), ())), preferred_element_type=jnp.float32
    ).astype(jnp.bfloat16)
    d_neigh = lax.dot_general(
        dpre_group, w_neigh, (((1,), (1,)), ((), ())), preferred_element_type=jnp.float32
    ).astype(jnp.bfloat16)
    grad_scale = 1.0 / math.sqrt(node_total)
    grad_self = sum_self * grad_scale
    grad_neigh = sum_neigh * grad_scale
    d_scaled = (
        d_neigh.astype(jnp.float32).reshape(blocks_here, block_size, feat_cols) / denom[..., None]
    ).astype(jnp.bfloat16)

    def backward_slot(slot_idx, grad_all):
        adjacency, block_ids, live_mask = slot_tiles(slot_idx)
        product = jnp.einsum(
            "bij,bic->bjc", adjacency, d_scaled, preferred_element_type=jnp.float32
        )
        return grad_all.at[block_ids].add(product * live_mask[:, None, None])

    grad_all = lax.fori_loop(
        0, slot_total, backward_slot, jnp.zeros((all_blocks, block_size, feat_cols), jnp.float32)
    )
    flat_grad = grad_all.reshape(node_total, feat_cols)
    group_part = lax.dynamic_slice_in_dim(flat_grad, node_group * group_rows, group_rows, 0)
    flat_grad = lax.dynamic_update_slice_in_dim(
        flat_grad, group_part + d_self.astype(jnp.float32), node_group * group_rows, 0
    )
    grad_features = lax.psum_scatter(flat_grad, "node", scatter_dimension=0, tiled=True)
    return (activated, grad_features, grad_self, grad_neigh)


def solution(mesh):
    placed = (
        P(None, "feat"),
        P("feat", None),
        P("feat", None),
        P(),
        P(("node", "feat"), None),
        P("node", None),
        P("node"),
        P("node", None, None, None),
    )
    return jax.shard_map(
        shards,
        mesh=mesh,
        in_specs=placed,
        out_specs=(P(("node", "feat"), None), P("node", "feat"), P("feat", None), P("feat", None)),
        check_vma=False,
    )
```

profile of v0, /device:TPU:2, one launch (start us, length us, event | category | flops | bytes accessed | tf_op | source)
XLA Modules:
  0.0 585.1 jit_solution(15753192361563251253)
XLA Ops:
  8.6 4.6 copy.24
  13.2 101.6 %while.30 = (s32[]{:T(128)}, f32[64,128,16]{1,2,0:T(8,128)S(1)}, f32[64,128]{0,1:T(8,128)S(1)}, s32[64,16,8,128]{3,2,0,1:T(8,128)}, s32[64,16]{0,1:T(8,128)}, /*...) while((s32[]{:T(128)}, f32[64,128,16]{1,2,0:T(8,128)S(1)}, ...), condition=%wide.region_2.3_spmd.clone, body=%wide.region_0.2_spmd.clone.sunk | while | flops 42353984 | bytes 7282812 | solution.py:43
  116.2 4.5 convolution_add_fusion
  120.8 153.3 %reduce-scatter.3.cloned.1.call-done = f32[128,256]{1,0:T(8,128)} async-done(((f32[8192,256]{1,0:T(8,128)}), f32[128,256]{1,0:T(8,128)}) %reduce-scatter.3.cloned.1.call-update) | async-done | bytes 131088 | tf_op jit(solution)/shard_map/reduce_scatter | solution.py:56
  275.8 79.0 %all-gather.2.cloned.1.call-done = bf16[8192,256]{1,0:T(8,128)(2,1)} async-done(((bf16[128,256]{1,0:T(8,128)(2,1)}), bf16[8192,256]{1,0:T(8,128)(2,1)}) %all-gather.2.cloned.1.call-update) | async-done | bytes 4194320 | tf_op jit(solution)/shard_map/all_gather | solution.py:68
  359.7 181.3 %while.29 = (s32[]{:T(128)}, f32[256,128,16]{1,2,0:T(8,128)}, s32[64,16]{0,1:T(8,128)}, s32[64,16,8,128]{3,2,0,1:T(8,128)}, bf16[64,128,16]{1,2,0:T(8,128)(2,1)S(1)}, /*index=5*/s32[64]{0:T(128)}, s32[]{:T(128)}) while((s32[]{:T(128)}, f32[256,128,16]{1,2,0:T(8,128)}, s32[64,16]{0,1:T(8,128)}, s32[64,16,8,128]{3,2,0,1:T(8,128)}, ...), condition=%wide.region_6.7_spmd, body=%wide.region_4.6_spmd.sunk | while | flops 36962624 | bytes 7343713 | solution.py:96
  363.5 7.5 %scatter_fusion = f32[256,128,16]{1,2,0:T(8,128)} fusion(f32[256,128,16]{1,2,0:T(8,128)} %get-tuple-element.451, s32[64]{0:T(128)S(1)} %fusion.60, f32[64,128,16]{1,2,0:T(8,128)S(1)} %convolution_multiply_fusion.3), kind=kCustom, calls=%fused_computation.1.clone.1 | custom fusion | flops 131072 | bytes 1573120 | tf_op jit(solution)/shard_map/while/body/eval_jaxpr/scatter-add | solution.py:94
  374.9 7.5 %scatter_fusion = f32[256,128,16]{1,2,0:T(8,128)} fusion(f32[256,128,16]{1,2,0:T(8,128)} %get-tuple-element.451, s32[64]{0:T(128)S(1)} %fusion.60, f32[64,128,16]{1,2,0:T(8,128)S(1)} %convolution_multiply_fusion.3), kind=kCustom, calls=%fused_computation.1.clone.1 | custom fusion | flops 131072 | bytes 1573120 | tf_op jit(solution)/shard_map/while/body/eval_jaxpr/scatter-add | solution.py:94
  386.2 7.5 %scatter_fusion = f32[256,128,16]{1,2,0:T(8,128)} fusion(f32[256,128,16]{1,2,0:T(8,128)} %get-tuple-element.451, s32[64]{0:T(128)S(1)} %fusion.60, f32[64,128,16]{1,2,0:T(8,128)S(1)} %convolution_multiply_fusion.3), kind=kCustom, calls=%fused_computation.1.clone.1 | custom fusion | flops 131072 | bytes 1573120 | tf_op jit(solution)/shard_map/while/body/eval_jaxpr/scatter-add | solution.py:94
  397.5 7.5 %scatter_fusion = f32[256,128,16]{1,2,0:T(8,128)} fusion(f32[256,128,16]{1,2,0:T(8,128)} %get-tuple-element.451, s32[64]{0:T(128)S(1)} %fusion.60, f32[64,128,16]{1,2,0:T(8,128)S(1)} %convolution_multiply_fusion.3), kind=kCustom, calls=%fused_computation.1.clone.1 | custom fusion | flops 131072 | bytes 1573120 | tf_op jit(solution)/shard_map/while/body/eval_jaxpr/scatter-add | solution.py:94
  408.9 7.5 %scatter_fusion = f32[256,128,16]{1,2,0:T(8,128)} fusion(f32[256,128,16]{1,2,0:T(8,128)} %get-tuple-element.451, s32[64]{0:T(128)S(1)} %fusion.60, f32[64,128,16]{1,2,0:T(8,128)S(1)} %convolution_multiply_fusion.3), kind=kCustom, calls=%fused_computation.1.clone.1 | custom fusion | flops 131072 | bytes 1573120 | tf_op jit(solution)/shard_map/while/body/eval_jaxpr/scatter-add | solution.py:94
  420.2 7.5 %scatter_fusion = f32[256,128,16]{1,2,0:T(8,128)} fusion(f32[256,128,16]{1,2,0:T(8,128)} %get-tuple-element.451, s32[64]{0:T(128)S(1)} %fusion.60, f32[64,128,16]{1,2,0:T(8,128)S(1)} %convolution_multiply_fusion.3), kind=kCustom, calls=%fused_computation.1.clone.1 | custom fusion | flops 131072 | bytes 1573120 | tf_op jit(solution)/shard_map/while/body/eval_jaxpr/scatter-add | solution.py:94
  431.6 7.5 %scatter_fusion = f32[256,128,16]{1,2,0:T(8,128)} fusion(f32[256,128,16]{1,2,0:T(8,128)} %get-tuple-element.451, s32[64]{0:T(128)S(1)} %fusion.60, f32[64,128,16]{1,2,0:T(8,128)S(1)} %convolution_multiply_fusion.3), kind=kCustom, calls=%fused_computation.1.clone.1 | custom fusion | flops 131072 | bytes 1573120 | tf_op jit(solution)/shard_map/while/body/eval_jaxpr/scatter-add | solution.py:94
  442.9 7.5 %scatter_fusion = f32[256,128,16]{1,2,0:T(8,128)} fusion(f32[256,128,16]{1,2,0:T(8,128)} %get-tuple-element.451, s32[64]{0:T(128)S(1)} %fusion.60, f32[64,128,16]{1,2,0:T(8,128)S(1)} %convolution_multiply_fusion.3), kind=kCustom, calls=%fused_computation.1.clone.1 | custom fusion | flops 131072 | bytes 1573120 | tf_op jit(solution)/shard_map/while/body/eval_jaxpr/scatter-add | solution.py:94
  454.2 7.5 %scatter_fusion = f32[256,128,16]{1,2,0:T(8,128)} fusion(f32[256,128,16]{1,2,0:T(8,128)} %get-tuple-element.451, s32[64]{0:T(128)S(1)} %fusion.60, f32[64,128,16]{1,2,0:T(8,128)S(1)} %convolution_multiply_fusion.3), kind=kCustom, calls=%fused_computation.1.clone.1 | custom fusion | flops 131072 | bytes 1573120 | tf_op jit(solution)/shard_map/while/body/eval_jaxpr/scatter-add | solution.py:94
  465.6 7.5 %scatter_fusion = f32[256,128,16]{1,2,0:T(8,128)} fusion(f32[256,128,16]{1,2,0:T(8,128)} %get-tuple-element.451, s32[64]{0:T(128)S(1)} %fusion.60, f32[64,128,16]{1,2,0:T(8,128)S(1)} %convolution_multiply_fusion.3), kind=kCustom, calls=%fused_computation.1.clone.1 | custom fusion | flops 131072 | bytes 1573120 | tf_op jit(solution)/shard_map/while/body/eval_jaxpr/scatter-add | solution.py:94
  476.9 7.5 %scatter_fusion = f32[256,128,16]{1,2,0:T(8,128)} fusion(f32[256,128,16]{1,2,0:T(8,128)} %get-tuple-element.451, s32[64]{0:T(128)S(1)} %fusion.60, f32[64,128,16]{1,2,0:T(8,128)S(1)} %convolution_multiply_fusion.3), kind=kCustom, calls=%fused_computation.1.clone.1 | custom fusion | flops 131072 | bytes 1573120 | tf_op jit(solution)/shard_map/while/body/eval_jaxpr/scatter-add | solution.py:94
  488.2 7.5 %scatter_fusion = f32[256,128,16]{1,2,0:T(8,128)} fusion(f32[256,128,16]{1,2,0:T(8,128)} %get-tuple-element.451, s32[64]{0:T(128)S(1)} %fusion.60, f32[64,128,16]{1,2,0:T(8,128)S(1)} %convolution_multiply_fusion.3), kind=kCustom, calls=%fused_computation.1.clone.1 | custom fusion | flops 131072 | bytes 1573120 | tf_op jit(solution)/shard_map/while/body/eval_jaxpr/scatter-add | solution.py:94
  499.5 7.5 %scatter_fusion = f32[256,128,16]{1,2,0:T(8,128)} fusion(f32[256,128,16]{1,2,0:T(8,128)} %get-tuple-element.451, s32[64]{0:T(128)S(1)} %fusion.60, f32[64,128,16]{1,2,0:T(8,128)S(1)} %convolution_multiply_fusion.3), kind=kCustom, calls=%fused_computation.1.clone.1 | custom fusion | flops 131072 | bytes 1573120 | tf_op jit(solution)/shard_map/while/body/eval_jaxpr/scatter-add | solution.py:94
  510.9 7.5 %scatter_fusion = f32[256,128,16]{1,2,0:T(8,128)} fusion(f32[256,128,16]{1,2,0:T(8,128)} %get-tuple-element.451, s32[64]{0:T(128)S(1)} %fusion.60, f32[64,128,16]{1,2,0:T(8,128)S(1)} %convolution_multiply_fusion.3), kind=kCustom, calls=%fused_computation.1.clone.1 | custom fusion | flops 131072 | bytes 1573120 | tf_op jit(solution)/shard_map/while/body/eval_jaxpr/scatter-add | solution.py:94
  522.2 7.5 %scatter_fusion = f32[256,128,16]{1,2,0:T(8,128)} fusion(f32[256,128,16]{1,2,0:T(8,128)} %get-tuple-element.451, s32[64]{0:T(128)S(1)} %fusion.60, f32[64,128,16]{1,2,0:T(8,128)S(1)} %convolution_multiply_fusion.3), kind=kCustom, calls=%fused_computation.1.clone.1 | custom fusion | flops 131072 | bytes 1573120 | tf_op jit(solution)/shard_map/while/body/eval_jaxpr/scatter-add | solution.py:94
  533.5 7.5 %scatter_fusion = f32[256,128,16]{1,2,0:T(8,128)} fusion(f32[256,128,16]{1,2,0:T(8,128)} %get-tuple-element.451, s32[64]{0:T(128)S(1)} %fusion.60, f32[64,128,16]{1,2,0:T(8,128)S(1)} %convolution_multiply_fusion.3), kind=kCustom, calls=%fused_computation.1.clone.1 | custom fusion | flops 131072 | bytes 1573120 | tf_op jit(solution)/shard_map/while/body/eval_jaxpr/scatter-add | solution.py:94
  551.4 17.6 %all-reduce = (f32[16,256]{1,0:T(8,128)S(1)}, f32[16,256]{1,0:T(8,128)S(1)}) all-reduce(f32[16,256]{1,0:T(8,128)S(1)} %fusion.20, f32[16,256]{1,0:T(8,128)S(1)} %fusion.14), channel_id=1, replica_groups=mesh['feat'=64,'node'=4] {'node'}, use_global_device_ids=true, to_apply=%region_8.9 | all-reduce | flops 8192 | bytes 65536 | tf_op jit(solution)/shard_map/psum | solution.py:75
  569.7 8.9 %reduce-scatter.5.cloned.1.call-done = f32[8192,16]{0,1:T(8,128)} async-done(((f32[32768,16]{0,1:T(8,128)}), f32[8192,16]{0,1:T(8,128)}) %reduce-scatter.5.cloned.1.call-update) | async-done | bytes 524304 | tf_op jit(solution)/shard_map/reduce_scatter | solution.py:104
  (339 shorter events, 182.3 us)
Async XLA Ops:
  7.2 1.2 copy-start
  7.2 266.9 %reduce-scatter.3.cloned.1.call-start = ((), (), s32[]{:S(2)}) async-start(), calls=%async_computation.2 | async-start | bytes 8519680 | tf_op jit(solution)/shard_map/reduce_scatter | solution.py:56
  13.2 101.7 %copy-start.5 = (bf16[16,256]{1,0:T(8,128)(2,1)S(1)}, bf16[16,256]{1,0:T(8,128)(2,1)}, u32[]{:S(2)}) copy-start(bf16[16,256]{1,0:T(8,128)(2,1)} %param.13) | copy-start | bytes 24580
  114.9 1.3 copy-start.4
  120.7 153.4 %copy-start.3 = (bf16[128,256]{1,0:T(8,128)(2,1)S(1)}, bf16[128,256]{1,0:T(8,128)(2,1)}, u32[]{:S(2)}) copy-start(bf16[128,256]{1,0:T(8,128)(2,1)} %param.16) | copy-start | bytes 196612
  120.7 153.4 %copy-start.6 = (f32[256]{0:T(256)S(1)}, f32[256]{0:T(256)}, u32[]{:S(2)}) copy-start(f32[256]{0:T(256)} %param.15) | copy-start | bytes 3076
  120.8 234.0 %all-gather.2.cloned.1.call-start = ((), (), s32[]{:S(2)}) async-start(), calls=%async_computation.3 | async-start | bytes 4259840 | tf_op jit(solution)/shard_map/all_gather | solution.py:68
  275.8 302.8 %reduce-scatter.5.cloned.1.call-start = ((), (), s32[]{:S(2)}) async-start(), calls=%async_computation.4 | async-start | bytes 2621440 | tf_op jit(solution)/shard_map/reduce_scatter | solution.py:104
  541.0 3.2 copy-start.1
  547.3 3.5 copy-start.2
Sparse Core Ops, SparseCore 0:
  120.9 153.1 reduce-scatter.2
  277.8 76.9 all-gather.1
  547.4 31.0 reduce-scatter.4
where the time goes:
time: 592 us; the launch traced here: 585 us
  waiting for transfers between devices  241 us (41%)
  other arithmetic  209 us (35%)
  local copies, waits for them, and re-layouts  57 us (10%)
  matrix products  45.7 us (8%)
  blocking collectives  17.6 us (3%)
  between operations  13.8 us (2%)
    reduce_scatter x1, waiting for transfers between devices, shards(): lax.psum_scatter(jnp.dot(own_rows, w_self, preferred_element_type=jnp.flo...  153 us
    scatter-add x16, other arithmetic, backward_slot(): return grad_all.at[block_ids].add(product * live_mask[:, None, None])  120 us
    all_gather x1, waiting for transfers between devices, shards(): dpre_group = lax.all_gather(dpre, 'feat', axis=0, tiled=True)  79 us
    shift_right_arithmetic x96, local copies, waits for them, and re-layouts, unpack(): jnp.right_shift(packed[..., :, None, :], shifts[:, None])  33.8 us
    convert_element_type x32, other arithmetic, slot_tiles(): adjacency = unpack(packed).astype(jnp.bfloat16)  23.8 us
    convert_element_type x32, other arithmetic, slot_tiles(): live_mask = (slot_idx < nbr_count).astype(jnp.float32)  21.2 us
    dot_general x16, matrix products, forward_slot(): jnp.einsum('bij,bjc->bic', adjacency, source, preferred_element_type=jnp....  19.2 us
    reduce_sum x16, other arithmetic, forward_slot(): jnp.sum(adjacency, axis=2, dtype=jnp.float32) * live_mask[:, None]  18.5 us
  transfers between devices with their start and end apart: 3, of which 3 were waited for; matrix products, arithmetic and copies ran while one was open for 1% of the time, Pallas kernels for 0%

commit v1 on v0

v1 whole, which is shorter than its diff:
```python
import math

import jax
import jax.numpy as jnp
from jax import lax
from jax.experimental import pallas as pl
from jax.experimental.pallas import tpu as pltpu
from jax.sharding import PartitionSpec as P


def unpack_tile(words):
    nwords, width = words.shape
    shifts = lax.broadcasted_iota(jnp.int32, (16, width), 0)
    rows = [
        jnp.bitwise_and(jnp.right_shift(jnp.broadcast_to(words[w : w + 1, :], (16, width)), shifts), 1)
        for w in range(nwords)
    ]
    return jnp.concatenate(rows, axis=0).astype(jnp.float32).astype(jnp.bfloat16)


def forward_kernel(ids_ref, cnt_ref, feat_ref, tiles_ref, nm_ref, deg_ref):
    b = pl.program_id(0)
    slots = tiles_ref.shape[1]
    cols, width = feat_ref.shape[1], feat_ref.shape[2]
    ones = jnp.ones((16, width), jnp.bfloat16)

    def body(s, acc):
        adj = unpack_tile(tiles_ref[0, s])
        src = feat_ref[ids_ref[b * slots + s]]
        lhs = jnp.concatenate([src, ones], axis=0)
        return acc + lax.dot_general(
            lhs, adj, (((1,), (1,)), ((), ())), preferred_element_type=jnp.float32
        )

    acc = lax.fori_loop(0, cnt_ref[b], body, jnp.zeros((cols + 16, width), jnp.float32))
    deg = acc[cols : cols + 1, :]
    nm_ref[0] = (acc[:cols, :] / jnp.maximum(deg, 1.0)).astype(nm_ref.dtype)
    deg_ref[0] = deg


def backward_kernel(ids_ref, cnt_ref, ds_ref, tiles_ref, g_ref):
    b = pl.program_id(0)
    slots = tiles_ref.shape[1]

    @pl.when(b == 0)
    def _():
        g_ref[...] = jnp.zeros_like(g_ref)

    d = ds_ref[0]

    def body(s, carry):
        adj = unpack_tile(tiles_ref[0, s])
        prod = jnp.dot(d, adj, preferred_element_type=jnp.float32)
        t = ids_ref[b * slots + s]
        g_ref[t] = g_ref[t] + prod
        return carry

    lax.fori_loop(0, cnt_ref[b], body, 0)


def aggregate_forward(ids_flat, counts, feat_blocks, tiles):
    blocks_here, slots, nwords, width = tiles.shape
    all_blocks, cols, _ = feat_blocks.shape
    return pl.pallas_call(
        forward_kernel,
        grid_spec=pltpu.PrefetchScalarGridSpec(
            num_scalar_prefetch=2,
            grid=(blocks_here,),
            in_specs=[
                pl.BlockSpec((all_blocks, cols, width), lambda b, *_: (0, 0, 0)),
                pl.BlockSpec((1, slots, nwords, width), lambda b, *_: (b, 0, 0, 0)),
            ],
            out_specs=[
                pl.BlockSpec((1, cols, width), lambda b, *_: (b, 0, 0)),
                pl.BlockSpec((1, 1, width), lambda b, *_: (b, 0, 0)),
            ],
        ),
        out_shape=[
            jax.ShapeDtypeStruct((blocks_here, cols, width), jnp.bfloat16),
            jax.ShapeDtypeStruct((blocks_here, 1, width), jnp.float32),
        ],
        compiler_params=pltpu.CompilerParams(dimension_semantics=("arbitrary",)),
    )(ids_flat, counts, feat_blocks, tiles)


def aggregate_backward(ids_flat, counts, ds_blocks, tiles, all_blocks):
    blocks_here, slots, nwords, width = tiles.shape
    cols = ds_blocks.shape[1]
    return pl.pallas_call(
        backward_kernel,
        grid_spec=pltpu.PrefetchScalarGridSpec(
            num_scalar_prefetch=2,
            grid=(blocks_here,),
            in_specs=[
                pl.BlockSpec((1, cols, width), lambda b, *_: (b, 0, 0)),
                pl.BlockSpec((1, slots, nwords, width), lambda b, *_: (b, 0, 0, 0)),
            ],
            out_specs=pl.BlockSpec((all_blocks, cols, width), lambda b, *_: (0, 0, 0)),
        ),
        out_shape=jax.ShapeDtypeStruct((all_blocks, cols, width), jnp.float32),
        compiler_params=pltpu.CompilerParams(dimension_semantics=("arbitrary",)),
    )(ids_flat, counts, ds_blocks, tiles)


def shards(features, w_self, w_neigh, bias, d_out, nbr_ids, nbr_count, tiles):
    node_total, cols = features.shape
    block_size = tiles.shape[3]
    blocks_here = nbr_ids.shape[0]
    all_blocks = node_total // block_size
    node_group = lax.axis_index("node")
    feat_index = lax.axis_index("feat")

    feat_blocks = features.reshape(all_blocks, block_size, cols).transpose(0, 2, 1)
    ids_flat = nbr_ids.reshape(-1)

    nm_blocks, deg_blocks = aggregate_forward(ids_flat, nbr_count, feat_blocks, tiles)

    w_self_all = lax.all_gather(w_self, "feat", axis=0, tiled=True)
    w_neigh_all = lax.all_gather(w_neigh, "feat", axis=0, tiled=True)

    feat_parts = lax.axis_size("feat")
    per = blocks_here // feat_parts
    group_feat = lax.dynamic_slice_in_dim(feat_blocks, node_group * blocks_here, blocks_here, 0)
    sent = jnp.stack([group_feat, nm_blocks], axis=1).reshape(feat_parts, per, 2, cols, block_size)
    got = lax.all_to_all(sent, "feat", 0, 0, tiled=True)
    own_t = got.transpose(2, 0, 3, 1, 4).reshape(2, feat_parts * cols, per * block_size)
    own_feat_t = own_t[0]
    own_nm_t = own_t[1]

    contract_rows = (((0,), (0,)), ((), ()))
    pre_act = (
        lax.dot_general(own_feat_t, w_self_all, contract_rows, preferred_element_type=jnp.float32)
        + lax.dot_general(own_nm_t, w_neigh_all, contract_rows, preferred_element_type=jnp.float32)
        + bias
    )
    activated = jax.nn.elu(pre_act).astype(jnp.bfloat16)
    elu_slope = jnp.where(pre_act > 0, 1.0, jnp.exp(jnp.minimum(pre_act, 0.0)))
    dpre = (d_out.astype(jnp.float32) * elu_slope).astype(jnp.bfloat16)

    contract_cols = (((1,), (1,)), ((), ()))
    d_self_t = lax.dot_general(
        w_self_all, dpre, contract_cols, preferred_element_type=jnp.float32
    ).astype(jnp.bfloat16)
    d_neigh_t = lax.dot_general(
        w_neigh_all, dpre, contract_cols, preferred_element_type=jnp.float32
    ).astype(jnp.bfloat16)
    own_deg = lax.dynamic_slice_in_dim(deg_blocks, feat_index * per, per, 0).reshape(1, -1)
    d_scaled_t = (d_neigh_t.astype(jnp.float32) / jnp.maximum(own_deg, 1.0)).astype(jnp.bfloat16)

    back = (
        jnp.stack([d_self_t, d_scaled_t], axis=0)
        .reshape(2, feat_parts, cols, per, block_size)
        .transpose(1, 3, 0, 2, 4)
    )
    got_back = lax.all_to_all(back, "feat", 0, 0, tiled=True).reshape(blocks_here, 2, cols, block_size)
    d_self_blocks = got_back[:, 0]
    d_scaled_blocks = got_back[:, 1]

    part = jnp.concatenate(
        [
            jnp.dot(own_feat_t, dpre, preferred_element_type=jnp.float32),
            jnp.dot(own_nm_t, dpre, preferred_element_type=jnp.float32),
        ],
        axis=1,
    )
    grads = lax.psum(lax.psum_scatter(part, "feat", scatter_dimension=0, tiled=True), "node")
    grad_scale = 1.0 / math.sqrt(node_total)
    hidden = w_self.shape[1]
    grad_self = grads[:, :hidden] * grad_scale
    grad_neigh = grads[:, hidden:] * grad_scale

    grad_all = aggregate_backward(ids_flat, nbr_count, d_scaled_blocks, tiles, all_blocks)
    grad_group = lax.psum_scatter(grad_all, "node", scatter_dimension=0, tiled=True)
    grad_group = grad_group + d_self_blocks.astype(jnp.float32)
    grad_features = grad_group.transpose(0, 2, 1).reshape(-1, cols)
    return (activated, grad_features, grad_self, grad_neigh)


def solution(mesh):
    placed = (
        P(None, "feat"),
        P("feat", None),
        P("feat", None),
        P(),
        P(("node", "feat"), None),
        P("node", None),
        P("node"),
        P("node", None, None, None),
    )
    return jax.shard_map(
        shards,
        mesh=mesh,
        in_specs=placed,
        out_specs=(P(("node", "feat"), None), P("node", "feat"), P("feat", None), P("feat", None)),
        check_vma=False,
    )
```

time: 592 us -> 490 us (0.83)
  other arithmetic: 209 us -> 3.86 us
  blocking collectives: 17.6 us -> 176 us
  Pallas kernels: 0 us -> 121 us
  waiting for transfers between devices: 241 us -> 146 us
  local copies, waits for them, and re-layouts: 57 us -> 9.12 us
  matrix products: 45.7 us -> 2.53 us
  starting transfers between devices: 0.12 us -> 12.2 us
    reduce_scatter x2 -> x1, waiting for transfers between devices: 162 us -> 7.31 us  [shards(): lax.psum_scatter(grad_all, 'node', scatter_dimension=0, tiled=True)]
    unnamed x3, waiting for transfers between devices: 0.05 us -> 138 us
    pallas_call x0 -> x2, Pallas kernels: none -> 121 us  [the longest x1 62.9 us: aggregate_forward(): pl.pallas_call(forward_kernel, grid_spec=pltpu.PrefetchScalarGridSpec(num...]
    scatter-add x16 -> x0, other arithmetic: 120 us -> none  [backward_slot(): return grad_all.at[block_ids].add(product * live_mask[:, None, None])]
    all_gather x0 -> x2, blocking collectives: none -> 105 us  [the longest x1 56.9 us: shards(): w_self_all = lax.all_gather(w_self, 'feat', axis=0, tiled=True)]
    all_gather x1 -> x0, waiting for transfers between devices: 79 us -> none  [shards(): dpre_group = lax.all_gather(dpre, 'feat', axis=0, tiled=True)]
    convert_element_type x66 -> x0, other arithmetic: 46.7 us -> none  [the longest x32 23.8 us: slot_tiles(): adjacency = unpack(packed).astype(jnp.bfloat16)]
    dot_general x38 -> x6, matrix products: 45.7 us -> 2.53 us  [the longest x1 0.98 us: shards(): lax.dot_general(own_nm_t, w_neigh_all, contract_rows, preferred_element_t...]
  transfers between devices with their start and end apart: 3 -> 3, of which waited for: 3 -> 2; matrix products, arithmetic and copies ran while one was open for 1% -> 1% of each run, Pallas kernels for 0% -> 12%
where the time goes in v1:
time: 490 us; the launch traced here: 485 us
  blocking collectives  176 us (36%)
  waiting for transfers between devices  146 us (30%)
  Pallas kernels  121 us (25%)
  between operations  14.2 us (3%)
  starting transfers between devices  12.2 us (2%)
  local copies, waits for them, and re-layouts  9.12 us (2%)
    unnamed x3, waiting for transfers between devices  138 us
    pallas_call x1, Pallas kernels, aggregate_forward(): pl.pallas_call(forward_kernel, grid_spec=pltpu.PrefetchScalarGridSpec(num...  62.9 us
    pallas_call x1, Pallas kernels, aggregate_backward(): pl.pallas_call(backward_kernel, grid_spec=pltpu.PrefetchScalarGridSpec(nu...  58.2 us
    all_gather x1, blocking collectives, shards(): w_self_all = lax.all_gather(w_self, 'feat', axis=0, tiled=True)  56.9 us
    all_gather x1, blocking collectives, shards(): w_neigh_all = lax.all_gather(w_neigh, 'feat', axis=0, tiled=True)  48.3 us
    psum x1, blocking collectives, shards(): lax.psum(lax.psum_scatter(part, 'feat', scatter_dimension=0, tiled=True),...  45.4 us
    all_to_all x1, blocking collectives, shards(): lax.all_to_all(back, 'feat', 0, 0, tiled=True)  25.8 us
    all_to_all x1, starting transfers between devices, shards(): got = lax.all_to_all(sent, 'feat', 0, 0, tiled=True)  12.2 us
  transfers between devices with their start and end apart: 3, of which 2 were waited for; matrix products, arithmetic and copies ran while one was open for 1% of the time, Pallas kernels for 12%

profile of v1, /device:TPU:2, one launch (start us, length us, event | category | flops | bytes accessed | tf_op | source)
XLA Modules:
  0.0 485.3 jit_solution(2912785797961351779)
XLA Ops:
  7.2 0.9 copy.35
  8.1 0.7 reshape.47.ids_ref
  8.7 1.2 copy_bitcast_fusion
  10.0 62.9 %shard_map.111 = (bf16[64,16,128]{2,1,0:T(8,128)(2,1)}, f32[64,1,128]{2,1,0:T(1,128)}) custom-call(s32[1024]{0:T(1024)} %reshape.47.ids_ref, s32[64]{0:T(128)} %cnt_ref.3, bf16[256,16,128]{2,1,0:T(8,128)(2,1)} %get-tuple-element.25.feat_ref, s32[64,16,8,128]{3,2,1,0:T(8,128)} %tiles_ref.3), custom_call_target="tpu_custom_call" | custom-call | tf_op jit(solution)/shard_map/pallas_call | solution.py:64
  72.9 1.0 maximum_bitcast_fusion
  73.9 0.8 copy.37
  74.8 12.2 %all-to-all-start = ((bf16[64,1,2,16,128]{4,3,2,1,0:T(8,128)(2,1)}), bf16[64,1,2,16,128]{4,3,2,1,0:T(8,128)(2,1)S(1)}, u32[]{:S(2)}, u32[]{:S(2)}) async-start(bf16[64,1,2,16,128]{4,3,2,1,0:T(8,128)(2,1)} %copy.37), calls=%async_computation | async-start | bytes 1048576 | tf_op jit(solution)/shard_map/all_to_all | solution.py:125
  87.0 56.9 %all_gather.6 = bf16[1024,256]{1,0:T(8,128)(2,1)S(1)} all-gather(bf16[16,256]{1,0:T(8,128)(2,1)S(1)} %copy-done.6), channel_id=1, replica_groups=mesh['feat'=64,'node'=4] {'feat'}, dimensions={0}, use_global_device_ids=true | all-gather | bytes 532480 | tf_op jit(solution)/shard_map/all_gather | solution.py:118
  143.9 48.3 %all_gather.7 = bf16[1024,256]{1,0:T(8,128)(2,1)S(1)} all-gather(bf16[16,256]{1,0:T(8,128)(2,1)S(1)} %copy-done.7), channel_id=1, replica_groups=mesh['feat'=64,'node'=4] {'feat'}, dimensions={0}, use_global_device_ids=true | all-gather | bytes 532480 | tf_op jit(solution)/shard_map/all_gather | solution.py:119
  192.5 1.0 fusion.10
  193.5 0.3 fusion.15
  193.9 0.3 fusion.14
  194.3 1.8 copy.45
  196.3 0.7 maximum_bitcast_fusion.2
  198.3 25.8 %all_to_all.10 = bf16[64,1,2,16,128]{4,3,2,1,0:T(8,128)(2,1)S(1)} all-to-all(bf16[64,1,2,16,128]{4,3,2,1,0:T(8,128)(2,1)S(1)} %copy.40), channel_id=1, replica_groups=mesh['feat'=64,'node'=4] {'feat'}, dimensions={0} | all-to-all | bytes 1048576 | tf_op jit(solution)/shard_map/all_to_all | solution.py:155
  224.1 0.7 slice_bitcast_fusion.1.ds_ref
  224.9 58.2 %shard_map.112 = f32[256,16,128]{2,1,0:T(8,128)} custom-call(s32[1024]{0:T(1024)} %reshape.47.ids_ref, s32[64]{0:T(128)} %cnt_ref.3, bf16[64,16,128]{2,1,0:T(8,128)(2,1)} %slice_bitcast_fusion.1.ds_ref, s32[64,16,8,128]{3,2,1,0:T(8,128)} %tiles_ref.3), custom_call_target="tpu_custom_call" | custom-call | tf_op jit(solution)/shard_map/pallas_call | solution.py:89
  283.1 138.4 %reduce-scatter.7.cloned.1.call-done = f32[16,512]{1,0:T(8,128)} async-done(((f32[1024,512]{1,0:T(8,128)}), f32[16,512]{1,0:T(8,128)}) %reduce-scatter.7.cloned.1.call-update) | async-done | bytes 32784
  421.6 0.9 copy.46
  422.4 45.4 %psum.7 = f32[16,512]{0,1:T(8,128)S(1)} all-reduce(f32[16,512]{0,1:T(8,128)S(1)} %copy.46), channel_id=1, replica_groups=mesh['feat'=64,'node'=4] {'node'}, use_global_device_ids=true, to_apply=%region_2.3 | all-reduce | flops 8192 | bytes 65536 | tf_op jit(solution)/shard_map/psum | solution.py:166
  467.9 0.7 copy.43
  468.6 0.7 copy.44
  469.3 7.3 %reduce-scatter.5.cloned.1.call-done = f32[64,16,128]{2,1,0:T(8,128)} async-done(((f32[256,16,128]{2,1,0:T(8,128)}), f32[64,16,128]{2,1,0:T(8,128)}) %reduce-scatter.5.cloned.1.call-update) | async-done | bytes 524304 | tf_op jit(solution)/shard_map/reduce_scatter | solution.py:173
  476.6 1.9 copy_bitcast_fusion.1
  (35 shorter events, 1.9 us)
Async XLA Ops:
  7.2 1.6 copy-start
  72.9 14.1 %copy-start.6 = (bf16[16,256]{1,0:T(8,128)(2,1)S(1)}, bf16[16,256]{1,0:T(8,128)(2,1)}, u32[]{:S(2)}) copy-start(bf16[16,256]{1,0:T(8,128)(2,1)} %param.9) | copy-start | bytes 24580
  72.9 71.0 %copy-start.7 = (bf16[16,256]{1,0:T(8,128)(2,1)S(1)}, bf16[16,256]{1,0:T(8,128)(2,1)}, u32[]{:S(2)}) copy-start(bf16[16,256]{1,0:T(8,128)(2,1)} %param.10) | copy-start | bytes 24580
  74.8 117.7 %copy-start.5 = (bf16[128,256]{1,0:T(8,128)(2,1)S(1)}, bf16[128,256]{1,0:T(8,128)(2,1)}, u32[]{:S(2)}) copy-start(bf16[128,256]{1,0:T(8,128)(2,1)} %param.12) | copy-start | bytes 196612
  74.8 117.7 %copy-start.8 = (f32[256]{0:T(256)S(1)}, f32[256]{0:T(256)}, u32[]{:S(2)}) copy-start(f32[256]{0:T(256)} %param.11) | copy-start | bytes 3076
  74.8 117.4 %all-to-all-start = ((bf16[64,1,2,16,128]{4,3,2,1,0:T(8,128)(2,1)}), bf16[64,1,2,16,128]{4,3,2,1,0:T(8,128)(2,1)S(1)}, u32[]{:S(2)}, u32[]{:S(2)}) async-start(bf16[64,1,2,16,128]{4,3,2,1,0:T(8,128)(2,1)} %copy.37), calls=%async_computation | async-start | bytes 1048576 | tf_op jit(solution)/shard_map/all_to_all | solution.py:125
  86.9 334.6 %reduce-scatter.7.cloned.1.call-start = ((), (), s32[]{:S(2)}) async-start(), calls=%async_computation.5 | async-start | bytes 2129920
  143.9 49.9 %copy-start.1 = (bf16[1024,256]{1,0:T(8,128)(2,1)}, bf16[1024,256]{1,0:T(8,128)(2,1)S(1)}, u32[]{:S(2)}) copy-start(bf16[1024,256]{1,0:T(8,128)(2,1)S(1)} %all_gather.6) | copy-start | bytes 1572868
  192.2 1.7 copy-start.3
  196.2 1.0 copy-start.4
  196.2 1.5 copy-start.2
  196.2 280.4 %reduce-scatter.5.cloned.1.call-start = ((), (), s32[]{:S(2)}) async-start(), calls=%async_computation.4 | async-start | bytes 2621440 | tf_op jit(solution)/shard_map/reduce_scatter | solution.py:173
Sparse Core Ops, SparseCore 0:
  196.3 225.1 reduce-scatter.6
  424.3 52.2 reduce-scatter.4

commit v2 on v1

v2 whole, which is shorter than its diff:
```python
import math

import jax
import jax.numpy as jnp
from jax import lax
from jax.experimental import pallas as pl
from jax.experimental.pallas import tpu as pltpu
from jax.sharding import PartitionSpec as P

ROWS_PER_STEP = 8


def unpack_tile(words):
    nwords, width = words.shape
    shifts = lax.broadcasted_iota(jnp.int32, (16, width), 0)
    rows = [
        jnp.bitwise_and(jnp.right_shift(jnp.broadcast_to(words[w : w + 1, :], (16, width)), shifts), 1)
        for w in range(nwords)
    ]
    return jnp.concatenate(rows, axis=0).astype(jnp.float32).astype(jnp.bfloat16)


def forward_kernel(ids_ref, cnt_ref, feat_ref, tiles_ref, nm_ref, deg_ref):
    step = pl.program_id(0)
    rows_here, slots = tiles_ref.shape[0], tiles_ref.shape[1]
    cols = nm_ref.shape[2]

    def row(r, carry):
        b = step * rows_here + r
        cnt = cnt_ref[b]
        adjs, srcs = [], []
        for s in range(slots):
            live = jnp.where(s < cnt, 1.0, 0.0)
            adjs.append(unpack_tile(tiles_ref[r, s]))
            src = feat_ref[ids_ref[b * slots + s]]
            srcs.append((src.astype(jnp.float32) * live).astype(jnp.bfloat16))
        out = jnp.dot(
            jnp.concatenate(adjs, axis=1),
            jnp.concatenate(srcs, axis=0),
            preferred_element_type=jnp.float32,
        )
        deg = out[:, cols : cols + 1]
        nm_ref[r] = (out[:, :cols] / jnp.maximum(deg, 1.0)).astype(nm_ref.dtype)
        deg_ref[r] = deg
        return carry

    lax.fori_loop(0, rows_here, row, 0)


def backward_kernel(ids_ref, cnt_ref, ds_ref, tiles_ref, g_ref):
    step = pl.program_id(0)
    rows_here, slots = tiles_ref.shape[0], tiles_ref.shape[1]
    width = tiles_ref.shape[3]

    @pl.when(step == 0)
    def _():
        g_ref[...] = jnp.zeros_like(g_ref)

    def row(r, carry):
        b = step * rows_here + r
        cnt = cnt_ref[b]
        adjcat = jnp.concatenate([unpack_tile(tiles_ref[r, s]) for s in range(slots)], axis=1)
        res = jnp.dot(ds_ref[r], adjcat, preferred_element_type=jnp.float32)
        for s in range(slots):
            live = jnp.where(s < cnt, 1.0, 0.0)
            t = ids_ref[b * slots + s]
            g_ref[t] = g_ref[t] + res[:, s * width : (s + 1) * width] * live
        return carry

    lax.fori_loop(0, rows_here, row, 0)


def aggregate_forward(ids_flat, counts, feat_aug, tiles, cols):
    blocks_here, slots, nwords, width = tiles.shape
    all_blocks, block_size, aug = feat_aug.shape
    rows = ROWS_PER_STEP
    return pl.pallas_call(
        forward_kernel,
        grid_spec=pltpu.PrefetchScalarGridSpec(
            num_scalar_prefetch=2,
            grid=(blocks_here // rows,),
            in_specs=[
                pl.BlockSpec((all_blocks, block_size, aug), lambda i, *_: (0, 0, 0)),
                pl.BlockSpec((rows, slots, nwords, width), lambda i, *_: (i, 0, 0, 0)),
            ],
            out_specs=[
                pl.BlockSpec((rows, block_size, cols), lambda i, *_: (i, 0, 0)),
                pl.BlockSpec((rows, block_size, 1), lambda i, *_: (i, 0, 0)),
            ],
        ),
        out_shape=[
            jax.ShapeDtypeStruct((blocks_here, block_size, cols), jnp.bfloat16),
            jax.ShapeDtypeStruct((blocks_here, block_size, 1), jnp.float32),
        ],
        compiler_params=pltpu.CompilerParams(dimension_semantics=("arbitrary",)),
    )(ids_flat, counts, feat_aug, tiles)


def aggregate_backward(ids_flat, counts, ds_blocks, tiles, all_blocks):
    blocks_here, slots, nwords, width = tiles.shape
    cols = ds_blocks.shape[1]
    rows = ROWS_PER_STEP
    return pl.pallas_call(
        backward_kernel,
        grid_spec=pltpu.PrefetchScalarGridSpec(
            num_scalar_prefetch=2,
            grid=(blocks_here // rows,),
            in_specs=[
                pl.BlockSpec((rows, cols, width), lambda i, *_: (i, 0, 0)),
                pl.BlockSpec((rows, slots, nwords, width), lambda i, *_: (i, 0, 0, 0)),
            ],
            out_specs=pl.BlockSpec((all_blocks, cols, width), lambda i, *_: (0, 0, 0)),
        ),
        out_shape=jax.ShapeDtypeStruct((all_blocks, cols, width), jnp.float32),
        compiler_params=pltpu.CompilerParams(dimension_semantics=("arbitrary",)),
    )(ids_flat, counts, ds_blocks, tiles)


def shards(features, w_self, w_neigh, bias, d_out, nbr_ids, nbr_count, tiles):
    node_total, cols = features.shape
    hidden = w_self.shape[1]
    block_size = tiles.shape[3]
    blocks_here = nbr_ids.shape[0]
    all_blocks = node_total // block_size
    node_group = lax.axis_index("node")
    feat_index = lax.axis_index("feat")
    feat_parts = lax.axis_size("feat")
    per = blocks_here // feat_parts

    feat_nat = features.reshape(all_blocks, block_size, cols)
    feat_aug = jnp.concatenate([feat_nat, jnp.ones_like(feat_nat)], axis=2)
    ids_flat = nbr_ids.reshape(-1)

    nm_blocks, deg_blocks = aggregate_forward(ids_flat, nbr_count, feat_aug, tiles, cols)

    w_both = jnp.concatenate([w_self, w_neigh], axis=1)
    w_all = lax.all_to_all(
        jnp.broadcast_to(w_both[None], (feat_parts,) + w_both.shape), "feat", 0, 0, tiled=True
    ).reshape(feat_parts * cols, 2 * hidden)
    w_self_all = w_all[:, :hidden]
    w_neigh_all = w_all[:, hidden:]

    group_feat = lax.dynamic_slice_in_dim(feat_nat, node_group * blocks_here, blocks_here, 0)
    sent = jnp.stack([group_feat, nm_blocks], axis=1).reshape(feat_parts, per, 2, block_size, cols)
    got = lax.all_to_all(sent, "feat", 0, 0, tiled=True)
    own = got.transpose(2, 1, 3, 0, 4).reshape(2, per * block_size, feat_parts * cols)
    own_feat = own[0]
    own_nm = own[1]

    pre_act = (
        jnp.dot(own_feat, w_self_all, preferred_element_type=jnp.float32)
        + jnp.dot(own_nm, w_neigh_all, preferred_element_type=jnp.float32)
        + bias
    )
    activated = jax.nn.elu(pre_act).astype(jnp.bfloat16)
    elu_slope = jnp.where(pre_act > 0, 1.0, jnp.exp(jnp.minimum(pre_act, 0.0)))
    dpre = (d_out.astype(jnp.float32) * elu_slope).astype(jnp.bfloat16)

    contract_cols = (((1,), (1,)), ((), ()))
    d_self = lax.dot_general(
        dpre, w_self_all, contract_cols, preferred_element_type=jnp.float32
    ).astype(jnp.bfloat16)
    d_neigh = lax.dot_general(
        dpre, w_neigh_all, contract_cols, preferred_element_type=jnp.float32
    ).astype(jnp.bfloat16)
    own_deg = lax.dynamic_slice_in_dim(deg_blocks, feat_index * per, per, 0).reshape(-1, 1)
    d_scaled = (d_neigh.astype(jnp.float32) / jnp.maximum(own_deg, 1.0)).astype(jnp.bfloat16)

    contract_rows = (((0,), (0,)), ((), ()))
    part = jnp.concatenate(
        [
            lax.dot_general(own_feat, dpre, contract_rows, preferred_element_type=jnp.float32),
            lax.dot_general(own_nm, dpre, contract_rows, preferred_element_type=jnp.float32),
        ],
        axis=1,
    )
    part_got = lax.all_to_all(part.reshape(feat_parts, cols, 2 * hidden), "feat", 0, 0, tiled=True)
    grads = lax.psum(jnp.sum(part_got, axis=0), "node")
    grad_scale = 1.0 / math.sqrt(node_total)
    grad_self = grads[:, :hidden] * grad_scale
    grad_neigh = grads[:, hidden:] * grad_scale

    back = (
        jnp.stack([d_self, d_scaled], axis=0)
        .reshape(2, per, block_size, feat_parts, cols)
        .transpose(3, 1, 0, 2, 4)
    )
    got_back = lax.all_to_all(back, "feat", 0, 0, tiled=True).reshape(blocks_here, 2, block_size, cols)
    d_self_blocks = got_back[:, 0]
    d_scaled_t = got_back[:, 1].transpose(0, 2, 1)

    grad_all = aggregate_backward(ids_flat, nbr_count, d_scaled_t, tiles, all_blocks)
    grad_group = lax.psum_scatter(grad_all, "node", scatter_dimension=0, tiled=True)
    grad_features = (
        grad_group.transpose(0, 2, 1) + d_self_blocks.astype(jnp.float32)
    ).reshape(-1, cols)
    return (activated, grad_features, grad_self, grad_neigh)


def solution(mesh):
    placed = (
        P(None, "feat"),
        P("feat", None),
        P("feat", None),
        P(),
        P(("node", "feat"), None),
        P("node", None),
        P("node"),
        P("node", None, None, None),
    )
    return jax.shard_map(
        shards,
        mesh=mesh,
        in_specs=placed,
        out_specs=(P(("node", "feat"), None), P("node", "feat"), P("feat", None), P("feat", None)),
        check_vma=False,
    )
```

time: 490 us -> 240 us (0.49)
  blocking collectives: 176 us -> 17.3 us
  Pallas kernels: 121 us -> 52.4 us
  waiting for transfers between devices: 146 us -> 86.5 us
  starting transfers between devices: 12.2 us -> 33.7 us
  local copies, waits for them, and re-layouts: 9.12 us -> 27.8 us
    unnamed x3 -> x1, waiting for transfers between devices: 138 us -> 0.02 us
    all_gather x2 -> x0, blocking collectives: 105 us -> none  [the longest x1 56.9 us: shards(): w_self_all = lax.all_gather(w_self, 'feat', axis=0, tiled=True)]
    all_to_all x0 -> x3, waiting for transfers between devices: none -> 69.8 us  [the longest x1 29.7 us: shards(): lax.all_to_all(part.reshape(feat_parts, cols, 2 * hidden), 'feat', 0, 0,...]
    pallas_call x1, Pallas kernels: 58.2 us -> 19 us  [aggregate_backward(): pl.pallas_call(backward_kernel, grid_spec=pltpu.PrefetchScalarGridSpec(nu...]
    pallas_call x1, Pallas kernels: 62.9 us -> 33.4 us  [aggregate_forward(): pl.pallas_call(forward_kernel, grid_spec=pltpu.PrefetchScalarGridSpec(num...]
    psum x1, blocking collectives: 45.4 us -> 17.3 us  [shards(): grads = lax.psum(jnp.sum(part_got, axis=0), 'node')]
    all_to_all x1 -> x0, blocking collectives: 25.8 us -> none  [shards(): lax.all_to_all(back, 'feat', 0, 0, tiled=True)]
    all_to_all x0 -> x3, starting transfers between devices: none -> 21.6 us  [the longest x1 7.62 us: shards(): lax.all_to_all(back, 'feat', 0, 0, tiled=True)]
  transfers between devices with their start and end apart: 3 -> 5, of which waited for: 2 -> 4; matrix products, arithmetic and copies ran while one was open for 1% -> 2% of each run, Pallas kernels for 12% -> 8%
where the time goes in v2:
time: 240 us; the launch traced here: 239 us
  waiting for transfers between devices  86.5 us (36%)
  Pallas kernels  52.4 us (22%)
  starting transfers between devices  33.7 us (14%)
  local copies, waits for them, and re-layouts  27.8 us (12%)
  blocking collectives  17.3 us (7%)
  between operations  14.2 us (6%)
  other arithmetic  4.62 us (2%)
  matrix products  2.52 us (1%)
    pallas_call x1, Pallas kernels, aggregate_forward(): pl.pallas_call(forward_kernel, grid_spec=pltpu.PrefetchScalarGridSpec(num...  33.4 us
    all_to_all x1, waiting for transfers between devices, shards(): lax.all_to_all(part.reshape(feat_parts, cols, 2 * hidden), 'feat', 0, 0,...  29.7 us
    all_to_all x1, waiting for transfers between devices, shards(): lax.all_to_all(jnp.broadcast_to(w_both[None], (feat_parts,) + w_both.shap...  26.1 us
    pallas_call x1, Pallas kernels, aggregate_backward(): pl.pallas_call(backward_kernel, grid_spec=pltpu.PrefetchScalarGridSpec(nu...  19 us
    psum x1, blocking collectives, shards(): grads = lax.psum(jnp.sum(part_got, axis=0), 'node')  17.3 us
    all_to_all x1, waiting for transfers between devices, shards(): got = lax.all_to_all(sent, 'feat', 0, 0, tiled=True)  16.7 us
    all_to_all x1, waiting for transfers between devices, shards(): lax.all_to_all(back, 'feat', 0, 0, tiled=True)  14 us
    all_to_all x1, starting transfers between devices, shards(): got = lax.all_to_all(sent, 'feat', 0, 0, tiled=True)  12.1 us
  transfers between devices with their start and end apart: 5, of which 4 were waited for; matrix products, arithmetic and copies ran while one was open for 2% of the time, Pallas kernels for 8%

profile of v2, /device:TPU:2, one launch (start us, length us, event | category | flops | bytes accessed | tf_op | source)
XLA Modules:
  0.0 239.0 jit_solution(5263011673257375024)
XLA Ops:
  7.2 7.2 %copy.32 = bf16[32768,16]{1,0:T(8,128)(2,1)} copy(bf16[32768,16]{0,1:T(8,128)(2,1)} %param.8) | data formatting | bytes 2097152 | tf_op args[0]
  14.3 1.7 constant_dynamic-slice_fusion
  16.1 0.8 copy.33
  16.9 10.5 %concatenate.10.feat_ref = bf16[256,128,32]{2,1,0:T(8,128)(2,1)} pad(bf16[256,128,16]{2,1,0:T(8,128)(2,1)} %bitcast.46, bf16[]{:T(256)} %constant.5.clone.1), padding=0_0x0_0x0_16 | pad | bytes 3145730 | tf_op jit(solution)/shard_map/concatenate | solution.py:131
  28.1 33.4 %shard_map.111 = (bf16[64,128,16]{2,1,0:T(8,128)(2,1)}, f32[64,128,1]{2,1,0:T(8,128)}) custom-call(s32[1024]{0:T(1024)} %reshape.54.ids_ref, s32[64]{0:T(128)} %cnt_ref.3, bf16[256,128,32]{2,1,0:T(8,128)(2,1)} %concatenate.10.feat_ref, s32[64,16,8,128]{3,2,1,0:T(8,128)} %tiles_ref.3), custom_call_target="tpu_custom_call" | custom-call | tf_op jit(solution)/shard_map/pallas_call | solution.py:77
  61.5 1.9 copy.35
  63.4 0.8 maximum_bitcast_fusion
  64.3 12.1 %all-to-all-start = ((bf16[64,1,2,128,16]{3,4,2,1,0:T(8,128)(2,1)}), bf16[64,1,2,128,16]{3,4,2,1,0:T(8,128)(2,1)S(1)}, u32[]{:S(2)}, u32[]{:S(2)}) async-start(bf16[64,1,2,128,16]{3,4,2,1,0:T(8,128)(2,1)} %maximum_bitcast_fusion), calls=%async_computation | async-start | bytes 1048576 | tf_op jit(solution)/shard_map/all_to_all | solution.py:145
  76.3 16.7 %all-to-all-done = bf16[64,1,2,128,16]{3,4,2,1,0:T(8,128)(2,1)S(1)} async-done(((bf16[64,1,2,128,16]{3,4,2,1,0:T(8,128)(2,1)}), bf16[64,1,2,128,16]{3,4,2,1,0:T(8,128)(2,1)S(1)}, u32[]{:S(2)}, u32[]{:S(2)}) %all-to-all-start) | async-done | bytes 524320 | tf_op jit(solution)/shard_map/all_to_all | solution.py:145
  93.0 1.1 broadcast_in_dim.14
  94.1 7.0 %all-to-all-start.1 = ((bf16[64,16,512]{2,1,0:T(8,128)(2,1)}), bf16[64,16,512]{2,1,0:T(8,128)(2,1)S(1)}, u32[]{:S(2)}, u32[]{:S(2)}) async-start(bf16[64,16,512]{2,1,0:T(8,128)(2,1)} %broadcast_in_dim.14), calls=%async_computation.1 | async-start | bytes 2097152 | tf_op jit(solution)/shard_map/all_to_all | solution.py:137
  101.2 0.9 maximum_reduce_fusion
  102.2 26.1 %all-to-all-done.1 = bf16[64,16,512]{2,1,0:T(8,128)(2,1)S(1)} async-done(((bf16[64,16,512]{2,1,0:T(8,128)(2,1)}), bf16[64,16,512]{2,1,0:T(8,128)(2,1)S(1)}, u32[]{:S(2)}, u32[]{:S(2)}) %all-to-all-start.1) | async-done | bytes 1048608 | tf_op jit(solution)/shard_map/all_to_all | solution.py:137
  128.6 1.0 fusion.13
  130.6 0.8 copy.39
  131.4 7.6 %all-to-all-start.2 = ((bf16[64,1,2,128,16]{3,4,2,1,0:T(8,128)(2,1)}), bf16[64,1,2,128,16]{3,4,2,1,0:T(8,128)(2,1)S(1)}, u32[]{:S(2)}, u32[]{:S(2)}) async-start(bf16[64,1,2,128,16]{3,4,2,1,0:T(8,128)(2,1)} %copy.39), calls=%async_computation.2 | async-start | bytes 1048576 | tf_op jit(solution)/shard_map/all_to_all | solution.py:188
  139.9 1.8 copy.42
  141.7 14.0 %all-to-all-done.2 = bf16[64,1,2,128,16]{3,4,2,1,0:T(8,128)(2,1)S(1)} async-done(((bf16[64,1,2,128,16]{3,4,2,1,0:T(8,128)(2,1)}), bf16[64,1,2,128,16]{3,4,2,1,0:T(8,128)(2,1)S(1)}, u32[]{:S(2)}, u32[]{:S(2)}) %all-to-all-start.2) | async-done | bytes 524320 | tf_op jit(solution)/shard_map/all_to_all | solution.py:188
  155.7 6.9 %all-to-all-start.3 = ((f32[64,16,512]{2,1,0:T(8,128)}), f32[64,16,512]{2,1,0:T(8,128)S(1)}, u32[]{:S(2)}, u32[]{:S(2)}) async-start(f32[64,16,512]{2,1,0:T(8,128)} %bitcast.16), calls=%async_computation.4 | async-start | bytes 4194304 | tf_op jit(solution)/shard_map/all_to_all | solution.py:177
  162.8 0.7 slice_bitcast_fusion.1.ds_ref
  163.5 19.0 %shard_map.112 = f32[256,16,128]{2,1,0:T(8,128)} custom-call(s32[1024]{0:T(1024)} %reshape.54.ids_ref, s32[64]{0:T(128)} %cnt_ref.3, bf16[64,16,128]{2,1,0:T(8,128)(2,1)} %slice_bitcast_fusion.1.ds_ref, s32[64,16,8,128]{3,2,1,0:T(8,128)} %tiles_ref.3), custom_call_target="tpu_custom_call" | custom-call | tf_op jit(solution)/shard_map/pallas_call | solution.py:103
  182.5 29.7 %all-to-all-done.3 = f32[64,16,512]{2,1,0:T(8,128)S(1)} async-done(((f32[64,16,512]{2,1,0:T(8,128)}), f32[64,16,512]{2,1,0:T(8,128)S(1)}, u32[]{:S(2)}, u32[]{:S(2)}) %all-to-all-start.3) | async-done | bytes 2097184 | tf_op jit(solution)/shard_map/all_to_all | solution.py:177
  212.3 17.3 %psum.7 = f32[16,512]{1,0:T(8,128)S(1)} all-reduce(f32[16,512]{1,0:T(8,128)S(1)} %reduce_sum.9), channel_id=1, replica_groups=mesh['feat'=64,'node'=4] {'node'}, use_global_device_ids=true, to_apply=%region_2.3 | all-reduce | flops 8192 | bytes 65536 | tf_op jit(solution)/shard_map/psum | solution.py:178
  230.3 1.9 copy_bitcast_fusion
  (30 shorter events, 3.8 us)
Async XLA Ops:
  16.9 10.5 %copy-start = (s32[64,16]{0,1:T(8,128)S(1)}, s32[64,16]{0,1:T(8,128)}, u32[]{:S(2)}) copy-start(s32[64,16]{0,1:T(8,128)} %param.13) | copy-start | bytes 12292
  61.5 14.8 %copy-start.1 = (bf16[16,256]{1,0:T(8,128)(2,1)S(1)}, bf16[16,256]{1,0:T(8,128)(2,1)}, u32[]{:S(2)}) copy-start(bf16[16,256]{1,0:T(8,128)(2,1)} %param.10) | copy-start | bytes 24580
  61.5 14.8 %copy-start.2 = (bf16[16,256]{1,0:T(8,128)(2,1)S(1)}, bf16[16,256]{1,0:T(8,128)(2,1)}, u32[]{:S(2)}) copy-start(bf16[16,256]{1,0:T(8,128)(2,1)} %param.9) | copy-start | bytes 24580
  64.3 28.8 %all-to-all-start = ((bf16[64,1,2,128,16]{3,4,2,1,0:T(8,128)(2,1)}), bf16[64,1,2,128,16]{3,4,2,1,0:T(8,128)(2,1)S(1)}, u32[]{:S(2)}, u32[]{:S(2)}) async-start(bf16[64,1,2,128,16]{3,4,2,1,0:T(8,128)(2,1)} %maximum_bitcast_fusion), calls=%async_computation | async-start | bytes 1048576 | tf_op jit(solution)/shard_map/all_to_all | solution.py:145
  94.1 34.5 %copy-start.3 = (bf16[128,256]{1,0:T(8,128)(2,1)S(1)}, bf16[128,256]{1,0:T(8,128)(2,1)}, u32[]{:S(2)}) copy-start(bf16[128,256]{1,0:T(8,128)(2,1)} %param.12) | copy-start | bytes 196612
  94.1 34.5 %copy-start.4 = (f32[256]{0:T(256)S(1)}, f32[256]{0:T(256)}, u32[]{:S(2)}) copy-start(f32[256]{0:T(256)} %param.11) | copy-start | bytes 3076
  94.1 34.2 %all-to-all-start.1 = ((bf16[64,16,512]{2,1,0:T(8,128)(2,1)}), bf16[64,16,512]{2,1,0:T(8,128)(2,1)S(1)}, u32[]{:S(2)}, u32[]{:S(2)}) async-start(bf16[64,16,512]{2,1,0:T(8,128)(2,1)} %broadcast_in_dim.14), calls=%async_computation.1 | async-start | bytes 2097152 | tf_op jit(solution)/shard_map/all_to_all | solution.py:137
  131.4 24.3 %all-to-all-start.2 = ((bf16[64,1,2,128,16]{3,4,2,1,0:T(8,128)(2,1)}), bf16[64,1,2,128,16]{3,4,2,1,0:T(8,128)(2,1)S(1)}, u32[]{:S(2)}, u32[]{:S(2)}) async-start(bf16[64,1,2,128,16]{3,4,2,1,0:T(8,128)(2,1)} %copy.39), calls=%async_computation.2 | async-start | bytes 1048576 | tf_op jit(solution)/shard_map/all_to_all | solution.py:188
  155.7 56.5 %all-to-all-start.3 = ((f32[64,16,512]{2,1,0:T(8,128)}), f32[64,16,512]{2,1,0:T(8,128)S(1)}, u32[]{:S(2)}, u32[]{:S(2)}) async-start(f32[64,16,512]{2,1,0:T(8,128)} %bitcast.16), calls=%async_computation.4 | async-start | bytes 4194304 | tf_op jit(solution)/shard_map/all_to_all | solution.py:177
  162.7 67.6 %reduce-scatter.2.cloned.1.call-start = ((), (), s32[]{:S(2)}) async-start(), calls=%async_computation.5 | async-start | bytes 2621440 | tf_op jit(solution)/shard_map/reduce_scatter | solution.py:193
Sparse Core Ops, SparseCore 0:
  182.7 33.4 reduce-scatter.1

commit v3 on v2

--- a/solution.py
+++ b/solution.py
@@ -23,24 +23,29 @@
 def forward_kernel(ids_ref, cnt_ref, feat_ref, tiles_ref, nm_ref, deg_ref):
     step = pl.program_id(0)
     rows_here, slots = tiles_ref.shape[0], tiles_ref.shape[1]
-    cols = nm_ref.shape[2]
+    cols, width = feat_ref.shape[1], feat_ref.shape[2]
 
     def row(r, carry):
         b = step * rows_here + r
         cnt = cnt_ref[b]
-        adjs, srcs = [], []
+        adjs, lhs = [], []
         for s in range(slots):
             live = jnp.where(s < cnt, 1.0, 0.0)
             adjs.append(unpack_tile(tiles_ref[r, s]))
-            src = feat_ref[ids_ref[b * slots + s]]
-            srcs.append((src.astype(jnp.float32) * live).astype(jnp.bfloat16))
-        out = jnp.dot(
+            src = feat_ref[ids_ref[b * slots + s]].astype(jnp.float32) * live
+            lhs.append(
+                jnp.concatenate([src, jnp.full((cols, width), live, jnp.float32)], axis=0).astype(
+                    jnp.bfloat16
+                )
+            )
+        out = lax.dot_general(
+            jnp.concatenate(lhs, axis=1),
             jnp.concatenate(adjs, axis=1),
-            jnp.concatenate(srcs, axis=0),
+            (((1,), (1,)), ((), ())),
             preferred_element_type=jnp.float32,
         )
-        deg = out[:, cols : cols + 1]
-        nm_ref[r] = (out[:, :cols] / jnp.maximum(deg, 1.0)).astype(nm_ref.dtype)
+        deg = out[cols : cols + 1, :]
+        nm_ref[r] = (out[:cols, :] / jnp.maximum(deg, 1.0)).astype(nm_ref.dtype)
         deg_ref[r] = deg
         return carry
 
@@ -70,9 +75,9 @@
     lax.fori_loop(0, rows_here, row, 0)
 
 
-def aggregate_forward(ids_flat, counts, feat_aug, tiles, cols):
+def aggregate_forward(ids_flat, counts, feat_t, tiles):
     blocks_here, slots, nwords, width = tiles.shape
-    all_blocks, block_size, aug = feat_aug.shape
+    all_blocks, cols, _ = feat_t.shape
     rows = ROWS_PER_STEP
     return pl.pallas_call(
         forward_kernel,
@@ -80,20 +85,20 @@
             num_scalar_prefetch=2,
             grid=(blocks_here // rows,),
             in_specs=[
-                pl.BlockSpec((all_blocks, block_size, aug), lambda i, *_: (0, 0, 0)),
+                pl.BlockSpec((all_blocks, cols, width), lambda i, *_: (0, 0, 0)),
                 pl.BlockSpec((rows, slots, nwords, width), lambda i, *_: (i, 0, 0, 0)),
             ],
             out_specs=[
-                pl.BlockSpec((rows, block_size, cols), lambda i, *_: (i, 0, 0)),
-                pl.BlockSpec((rows, block_size, 1), lambda i, *_: (i, 0, 0)),
+                pl.BlockSpec((rows, cols, width), lambda i, *_: (i, 0, 0)),
+                pl.BlockSpec((rows, 1, width), lambda i, *_: (i, 0, 0)),
             ],
         ),
         out_shape=[
-            jax.ShapeDtypeStruct((blocks_here, block_size, cols), jnp.bfloat16),
-            jax.ShapeDtypeStruct((blocks_here, block_size, 1), jnp.float32),
+            jax.ShapeDtypeStruct((blocks_here, cols, width), jnp.bfloat16),
+            jax.ShapeDtypeStruct((blocks_here, 1, width), jnp.float32),
         ],
         compiler_params=pltpu.CompilerParams(dimension_semantics=("arbitrary",)),
-    )(ids_flat, counts, feat_aug, tiles)
+    )(ids_flat, counts, feat_t, tiles)
 
 
 def aggregate_backward(ids_flat, counts, ds_blocks, tiles, all_blocks):
@@ -126,26 +131,36 @@
     feat_index = lax.axis_index("feat")
     feat_parts = lax.axis_size("feat")
     per = blocks_here // feat_parts
-
-    feat_nat = features.reshape(all_blocks, block_size, cols)
-    feat_aug = jnp.concatenate([feat_nat, jnp.ones_like(feat_nat)], axis=2)
+    own_nodes = per * block_size
+
+    feat_t = features.reshape(all_blocks, block_size, cols).transpose(0, 2, 1)
     ids_flat = nbr_ids.reshape(-1)
 
-    nm_blocks, deg_blocks = aggregate_forward(ids_flat, nbr_count, feat_aug, tiles, cols)
-
-    w_both = jnp.concatenate([w_self, w_neigh], axis=1)
-    w_all = lax.all_to_all(
-        jnp.broadcast_to(w_both[None], (feat_parts,) + w_both.shape), "feat", 0, 0, tiled=True
-    ).reshape(feat_parts * cols, 2 * hidden)
+    nm_t, deg_blocks = aggregate_forward(ids_flat, nbr_count, feat_t, tiles)
+
+    group_t = lax.dynamic_slice_in_dim(feat_t, node_group * blocks_here, blocks_here, 0)
+    w_both = jnp.concatenate([w_self, w_neigh], axis=1).reshape(1, -1)
+    sent = jnp.concatenate(
+        [
+            group_t.reshape(feat_parts, -1),
+            nm_t.reshape(feat_parts, -1),
+            jnp.broadcast_to(w_both, (feat_parts, w_both.shape[1])),
+        ],
+        axis=1,
+    )
+    got = lax.all_to_all(sent, "feat", 0, 0, tiled=True)
+    span = own_nodes * cols
+    own = (
+        got[:, : 2 * span]
+        .reshape(feat_parts, 2, per, cols, block_size)
+        .transpose(1, 2, 4, 0, 3)
+        .reshape(2, own_nodes, feat_parts * cols)
+    )
+    own_feat = own[0]
+    own_nm = own[1]
+    w_all = got[:, 2 * span :].reshape(feat_parts * cols, 2 * hidden)
     w_self_all = w_all[:, :hidden]
     w_neigh_all = w_all[:, hidden:]
-
-    group_feat = lax.dynamic_slice_in_dim(feat_nat, node_group * blocks_here, blocks_here, 0)
-    sent = jnp.stack([group_feat, nm_blocks], axis=1).reshape(feat_parts, per, 2, block_size, cols)
-    got = lax.all_to_all(sent, "feat", 0, 0, tiled=True)
-    own = got.transpose(2, 1, 3, 0, 4).reshape(2, per * block_size, feat_parts * cols)
-    own_feat = own[0]
-    own_nm = own[1]
 
     pre_act = (
         jnp.dot(own_feat, w_self_all, preferred_element_type=jnp.float32)
@@ -157,14 +172,14 @@
     dpre = (d_out.astype(jnp.float32) * elu_slope).astype(jnp.bfloat16)
 
     contract_cols = (((1,), (1,)), ((), ()))
-    d_self = lax.dot_general(
-        dpre, w_self_all, contract_cols, preferred_element_type=jnp.float32
+    d_self_t = lax.dot_general(
+        w_self_all, dpre, contract_cols, preferred_element_type=jnp.float32
     ).astype(jnp.bfloat16)
-    d_neigh = lax.dot_general(
-        dpre, w_neigh_all, contract_cols, preferred_element_type=jnp.float32
+    d_neigh_t = lax.dot_general(
+        w_neigh_all, dpre, contract_cols, preferred_element_type=jnp.float32
     ).astype(jnp.bfloat16)
-    own_deg = lax.dynamic_slice_in_dim(deg_blocks, feat_index * per, per, 0).reshape(-1, 1)
-    d_scaled = (d_neigh.astype(jnp.float32) / jnp.maximum(own_deg, 1.0)).astype(jnp.bfloat16)
+    own_deg = lax.dynamic_slice_in_dim(deg_blocks, feat_index * per, per, 0).reshape(1, -1)
+    d_scaled_t = (d_neigh_t.astype(jnp.float32) / jnp.maximum(own_deg, 1.0)).astype(jnp.bfloat16)
 
     contract_rows = (((0,), (0,)), ((), ()))
     part = jnp.concatenate(
@@ -174,26 +189,35 @@
         ],
         axis=1,
     )
-    part_got = lax.all_to_all(part.reshape(feat_parts, cols, 2 * hidden), "feat", 0, 0, tiled=True)
-    grads = lax.psum(jnp.sum(part_got, axis=0), "node")
+    part_hi = part.astype(jnp.bfloat16)
+    part_lo = (part - part_hi.astype(jnp.float32)).astype(jnp.bfloat16)
+
+    def per_peer(x_t):
+        return x_t.reshape(feat_parts, cols, per, block_size).transpose(0, 2, 1, 3).reshape(feat_parts, -1)
+
+    back = jnp.concatenate(
+        [
+            per_peer(d_self_t),
+            per_peer(d_scaled_t),
+            part_hi.reshape(feat_parts, -1),
+            part_lo.reshape(feat_parts, -1),
+        ],
+        axis=1,
+    )
+    got_back = lax.all_to_all(back, "feat", 0, 0, tiled=True)
+    d_t = got_back[:, : 2 * span].reshape(feat_parts, 2, per, cols, block_size)
+    d_self_blocks = d_t[:, 0].reshape(blocks_here, cols, block_size)
+    d_scaled_blocks = d_t[:, 1].reshape(blocks_here, cols, block_size)
+    halves = got_back[:, 2 * span :].reshape(feat_parts, 2, cols, 2 * hidden).astype(jnp.float32)
+    grads = lax.psum(jnp.sum(halves[:, 0] + halves[:, 1], axis=0), "node")
     grad_scale = 1.0 / math.sqrt(node_total)
     grad_self = grads[:, :hidden] * grad_scale
     grad_neigh = grads[:, hidden:] * grad_scale
 
-    back = (
-        jnp.stack([d_self, d_scaled], axis=0)
-        .reshape(2, per, block_size, feat_parts, cols)
-        .transpose(3, 1, 0, 2, 4)
-    )
-    got_back = lax.all_to_all(back, "feat", 0, 0, tiled=True).reshape(blocks_here, 2, block_size, cols)
-    d_self_blocks = got_back[:, 0]
-    d_scaled_t = got_back[:, 1].transpose(0, 2, 1)
-
-    grad_all = aggregate_backward(ids_flat, nbr_count, d_scaled_t, tiles, all_blocks)
+    grad_all = aggregate_backward(ids_flat, nbr_count, d_scaled_blocks, tiles, all_blocks)
     grad_group = lax.psum_scatter(grad_all, "node", scatter_dimension=0, tiled=True)
-    grad_features = (
-        grad_group.transpose(0, 2, 1) + d_self_blocks.astype(jnp.float32)
-    ).reshape(-1, cols)
+    grad_group = grad_group + d_self_blocks.astype(jnp.float32)
+    grad_features = grad_group.transpose(0, 2, 1).reshape(-1, cols)
     return (activated, grad_features, grad_self, grad_neigh)
 
 

time: 240 us -> 269 us (1.12)
  blocking collectives: 17.3 us -> 86.5 us
  waiting for transfers between devices: 86.5 us -> 47.3 us
  local copies, waits for them, and re-layouts: 27.8 us -> 51.7 us
  starting transfers between devices: 33.7 us -> 12.2 us
  Pallas kernels: 52.4 us -> 40 us
  other arithmetic: 4.62 us -> 12.5 us
    all_to_all x3 -> x0, waiting for transfers between devices: 69.8 us -> none  [the longest x1 29.7 us: shards(): lax.all_to_all(part.reshape(feat_parts, cols, 2 * hidden), 'feat', 0, 0,...]
    all_to_all x0 -> x1, blocking collectives: none -> 68.7 us  [shards(): got_back = lax.all_to_all(back, 'feat', 0, 0, tiled=True)]
    unnamed x12 -> x25, local copies, waits for them, and re-layouts: 7.28 us -> 42.8 us
    all_to_all x3 -> x0, starting transfers between devices: 21.6 us -> none  [the longest x1 7.62 us: shards(): lax.all_to_all(back, 'feat', 0, 0, tiled=True)]
    all_to_all x1, waiting for transfers between devices: 16.7 us -> 37.8 us  [shards(): got = lax.all_to_all(sent, 'feat', 0, 0, tiled=True)]
    pallas_call x1, Pallas kernels: 33.4 us -> 20.9 us  [aggregate_forward(): pl.pallas_call(forward_kernel, grid_spec=pltpu.PrefetchScalarGridSpec(num...]
    concatenate x1, local copies, waits for them, and re-layouts: 10.5 us -> 0.01 us  [shards(): jnp.concatenate([group_t.reshape(feat_parts, -1), nm_t.reshape(feat_parts...]
    reduce_scatter x1, waiting for transfers between devices: 0.01 us -> 9.47 us  [shards(): lax.psum_scatter(grad_all, 'node', scatter_dimension=0, tiled=True)]
  transfers between devices with their start and end apart: 5 -> 2, of which waited for: 4 -> 2; matrix products, arithmetic and copies ran while one was open for 2% -> 2% of each run, Pallas kernels for 8% -> 0%
where the time goes in v3:
time: 269 us; the launch traced here: 267 us
  blocking collectives  86.5 us (32%)
  local copies, waits for them, and re-layouts  51.7 us (19%)
  waiting for transfers between devices  47.3 us (18%)
  Pallas kernels  40 us (15%)
  between operations  14.3 us (5%)
  other arithmetic  12.5 us (5%)
  starting transfers between devices  12.2 us (5%)
    all_to_all x1, blocking collectives, shards(): got_back = lax.all_to_all(back, 'feat', 0, 0, tiled=True)  68.7 us
    unnamed x25, local copies, waits for them, and re-layouts  42.8 us
    all_to_all x1, waiting for transfers between devices, shards(): got = lax.all_to_all(sent, 'feat', 0, 0, tiled=True)  37.8 us
    pallas_call x1, Pallas kernels, aggregate_forward(): pl.pallas_call(forward_kernel, grid_spec=pltpu.PrefetchScalarGridSpec(num...  20.9 us
    pallas_call x1, Pallas kernels, aggregate_backward(): pl.pallas_call(backward_kernel, grid_spec=pltpu.PrefetchScalarGridSpec(nu...  19 us
    psum x1, blocking collectives, shards(): grads = lax.psum(jnp.sum(halves[:, 0] + halves[:, 1], axis=0), 'node')  17.7 us
    all_to_all x1, starting transfers between devices, shards(): got = lax.all_to_all(sent, 'feat', 0, 0, tiled=True)  12.2 us
    reduce_scatter x1, waiting for transfers between devices, shards(): lax.psum_scatter(grad_all, 'node', scatter_dimension=0, tiled=True)  9.47 us
  transfers between devices with their start and end apart: 2, of which 2 were waited for; matrix products, arithmetic and copies ran while one was open for 2% of the time, Pallas kernels for 0%

profile of v3, /device:TPU:2, one launch (start us, length us, event | category | flops | bytes accessed | tf_op | source)
XLA Modules:
  0.0 267.0 jit_solution(18281532993347453211)
XLA Ops:
  8.6 2.4 bitcast_bitcast_fusion.feat_ref
  11.0 20.9 %shard_map.111 = (bf16[64,16,128]{2,1,0:T(8,128)(2,1)}, f32[64,1,128]{2,1,0:T(1,128)}) custom-call(s32[1024]{0:T(1024)} %reshape.66.ids_ref, s32[64]{0:T(128)} %cnt_ref.3, bf16[256,16,128]{2,1,0:T(8,128)(2,1)} %bitcast_bitcast_fusion.feat_ref, s32[64,16,8,128]{3,2,1,0:T(8,128)} %tiles_ref.3), custom_call_target="tpu_custom_call" | custom-call | tf_op jit(solution)/shard_map/pallas_call | solution.py:82
  31.9 1.0 copy.63
  34.0 1.9 reduce.1
  35.9 2.1 reshape.75
  37.9 12.2 %all-to-all-start = ((bf16[64,2,6144]{2,1,0:T(2,128)(2,1)}), bf16[64,2,6144]{2,1,0:T(2,128)(2,1)}, u32[]{:S(2)}, u32[]{:S(2)}) async-start(bf16[64,2,6144]{2,1,0:T(2,128)(2,1)} %reshape.75), calls=%async_computation | async-start | bytes 3145728 | tf_op jit(solution)/shard_map/all_to_all | solution.py:151
  50.8 37.8 %all-to-all-done = bf16[64,2,6144]{2,1,0:T(2,128)(2,1)} async-done(((bf16[64,2,6144]{2,1,0:T(2,128)(2,1)}), bf16[64,2,6144]{2,1,0:T(2,128)(2,1)}, u32[]{:S(2)}, u32[]{:S(2)}) %all-to-all-start) | async-done | bytes 1572896 | tf_op jit(solution)/shard_map/all_to_all | solution.py:151
  88.7 9.1 %reshape.76 = bf16[64,1,12288]{2,1,0:T(2,128)(2,1)S(1)} reshape(bf16[64,2,6144]{2,1,0:T(2,128)(2,1)} %all-to-all-done) | data formatting | bytes 3145728
  97.8 1.7 copy.62
  100.6 1.0 fusion.14
  102.7 1.9 copy.37
  104.5 1.7 concatenate.17
  106.3 1.6 subtract_convert_fusion
  108.5 1.6 maximum_bitcast_fusion
  110.1 3.4 %reduce.2 = bf16[64,20480]{1,0:T(8,128)(2,1)} reduce(bf16[64,1,20480]{2,0,1:T(8,128)(2,1)S(1)} %maximum_bitcast_fusion, bf16[]{:T(256)} %broadcast.19), dimensions={1}, to_apply=%copy.38.reduce_sub_computation | reduce | bytes 5242882 | tf_op jit(solution)/shard_map/all_to_all | solution.py:207
  113.5 3.7 %reshape.77 = bf16[64,2,10240]{2,1,0:T(2,128)(2,1)S(1)} reshape(bf16[64,20480]{1,0:T(8,128)(2,1)} %reduce.2) | data formatting | bytes 5242880
  117.2 68.7 %all_to_all.24 = bf16[64,2,10240]{2,1,0:T(2,128)(2,1)} all-to-all(bf16[64,2,10240]{2,1,0:T(2,128)(2,1)S(1)} %reshape.77), channel_id=1, replica_groups=mesh['feat'=64,'node'=4] {'feat'}, dimensions={0} | all-to-all | bytes 5242880 | tf_op jit(solution)/shard_map/all_to_all | solution.py:207
  185.9 16.3 %reshape.78 = bf16[64,1,20480]{2,1,0:T(2,128)(2,1)} reshape(bf16[64,2,10240]{2,1,0:T(2,128)(2,1)} %all_to_all.24) | data formatting | bytes 5242880
  202.2 5.3 %copy.61 = bf16[64,1,20480]{2,0,1:T(8,128)(2,1)S(1)} copy(bf16[64,1,20480]{2,1,0:T(2,128)(2,1)} %reshape.78) | data formatting | bytes 5242880
  208.4 19.0 %shard_map.112 = f32[256,16,128]{2,1,0:T(8,128)} custom-call(s32[1024]{0:T(1024)} %reshape.66.ids_ref, s32[64]{0:T(128)} %cnt_ref.3, bf16[64,16,128]{2,1,0:T(8,128)(2,1)} %slice_bitcast_fusion.3.ds_ref, s32[64,16,8,128]{3,2,1,0:T(8,128)} %tiles_ref.3), custom_call_target="tpu_custom_call" | custom-call | tf_op jit(solution)/shard_map/pallas_call | solution.py:108
  227.7 2.4 copy.54
  230.4 17.7 %psum.7 = f32[16,512]{1,0:T(8,128)S(1)} all-reduce(f32[16,512]{1,0:T(8,128)S(1)} %fusion), channel_id=1, replica_groups=mesh['feat'=64,'node'=4] {'node'}, use_global_device_ids=true, to_apply=%region_2.3 | all-reduce | flops 8192 | bytes 65536 | tf_op jit(solution)/shard_map/psum | solution.py:212
  248.8 9.5 %reduce-scatter.2.cloned.1.call-done = f32[64,16,128]{2,1,0:T(8,128)} async-done(((f32[256,16,128]{2,1,0:T(8,128)}), f32[64,16,128]{2,1,0:T(8,128)}) %reduce-scatter.2.cloned.1.call-update) | async-done | bytes 524304 | tf_op jit(solution)/shard_map/reduce_scatter | solution.py:218
  258.2 1.9 copy_bitcast_fusion.2
  (41 shorter events, 7.8 us)
Async XLA Ops:
  11.0 22.0 %copy-start = (bf16[32768,16]{0,1:T(8,128)(2,1)S(1)}, bf16[32768,16]{0,1:T(8,128)(2,1)}, u32[]{:S(2)}) copy-start(bf16[32768,16]{0,1:T(8,128)(2,1)} %param.8) | copy-start | bytes 3145732
  31.9 1.3 copy-start.1
  31.9 1.3 copy-start.2
  37.9 50.7 %all-to-all-start = ((bf16[64,2,6144]{2,1,0:T(2,128)(2,1)}), bf16[64,2,6144]{2,1,0:T(2,128)(2,1)}, u32[]{:S(2)}, u32[]{:S(2)}) async-start(bf16[64,2,6144]{2,1,0:T(2,128)(2,1)} %reshape.75), calls=%async_computation | async-start | bytes 3145728 | tf_op jit(solution)/shard_map/all_to_all | solution.py:151
  50.1 208.1 %reduce-scatter.2.cloned.1.call-start = ((), (), s32[]{:S(2)}) async-start(), calls=%async_computation.3 | async-start | bytes 2621440 | tf_op jit(solution)/shard_map/reduce_scatter | solution.py:218
  99.6 1.0 copy-start.3
  99.6 1.0 copy-start.4
Sparse Core Ops, SparseCore 0:
  227.5 30.6 reduce-scatter.1

commit v4 on v3

--- a/solution.py
+++ b/solution.py
@@ -138,29 +138,19 @@
 
     nm_t, deg_blocks = aggregate_forward(ids_flat, nbr_count, feat_t, tiles)
 
+    w_both = jnp.concatenate([w_self, w_neigh], axis=1)
+    w_all = lax.all_to_all(
+        jnp.broadcast_to(w_both[None], (feat_parts,) + w_both.shape), "feat", 0, 0, tiled=True
+    ).reshape(feat_parts * cols, 2 * hidden)
+    w_self_all = w_all[:, :hidden]
+    w_neigh_all = w_all[:, hidden:]
+
     group_t = lax.dynamic_slice_in_dim(feat_t, node_group * blocks_here, blocks_here, 0)
-    w_both = jnp.concatenate([w_self, w_neigh], axis=1).reshape(1, -1)
-    sent = jnp.concatenate(
-        [
-            group_t.reshape(feat_parts, -1),
-            nm_t.reshape(feat_parts, -1),
-            jnp.broadcast_to(w_both, (feat_parts, w_both.shape[1])),
-        ],
-        axis=1,
-    )
+    sent = jnp.stack([group_t, nm_t], axis=1).reshape(feat_parts, per, 2, cols, block_size)
     got = lax.all_to_all(sent, "feat", 0, 0, tiled=True)
-    span = own_nodes * cols
-    own = (
-        got[:, : 2 * span]
-        .reshape(feat_parts, 2, per, cols, block_size)
-        .transpose(1, 2, 4, 0, 3)
-        .reshape(2, own_nodes, feat_parts * cols)
-    )
+    own = got.transpose(2, 1, 4, 0, 3).reshape(2, own_nodes, feat_parts * cols)
     own_feat = own[0]
     own_nm = own[1]
-    w_all = got[:, 2 * span :].reshape(feat_parts * cols, 2 * hidden)
-    w_self_all = w_all[:, :hidden]
-    w_neigh_all = w_all[:, hidden:]
 
     pre_act = (
         jnp.dot(own_feat, w_self_all, preferred_element_type=jnp.float32)
@@ -189,30 +179,20 @@
         ],
         axis=1,
     )
-    part_hi = part.astype(jnp.bfloat16)
-    part_lo = (part - part_hi.astype(jnp.float32)).astype(jnp.bfloat16)
-
-    def per_peer(x_t):
-        return x_t.reshape(feat_parts, cols, per, block_size).transpose(0, 2, 1, 3).reshape(feat_parts, -1)
-
-    back = jnp.concatenate(
-        [
-            per_peer(d_self_t),
-            per_peer(d_scaled_t),
-            part_hi.reshape(feat_parts, -1),
-            part_lo.reshape(feat_parts, -1),
-        ],
-        axis=1,
-    )
-    got_back = lax.all_to_all(back, "feat", 0, 0, tiled=True)
-    d_t = got_back[:, : 2 * span].reshape(feat_parts, 2, per, cols, block_size)
-    d_self_blocks = d_t[:, 0].reshape(blocks_here, cols, block_size)
-    d_scaled_blocks = d_t[:, 1].reshape(blocks_here, cols, block_size)
-    halves = got_back[:, 2 * span :].reshape(feat_parts, 2, cols, 2 * hidden).astype(jnp.float32)
-    grads = lax.psum(jnp.sum(halves[:, 0] + halves[:, 1], axis=0), "node")
+    part_got = lax.all_to_all(part.reshape(feat_parts, cols, 2 * hidden), "feat", 0, 0, tiled=True)
+    grads = lax.psum(jnp.sum(part_got, axis=0), "node")
     grad_scale = 1.0 / math.sqrt(node_total)
     grad_self = grads[:, :hidden] * grad_scale
     grad_neigh = grads[:, hidden:] * grad_scale
+
+    back = (
+        jnp.stack([d_self_t, d_scaled_t], axis=0)
+        .reshape(2, feat_parts, cols, per, block_size)
+        .transpose(1, 3, 0, 2, 4)
+    )
+    got_back = lax.all_to_all(back, "feat", 0, 0, tiled=True).reshape(blocks_here, 2, cols, block_size)
+    d_self_blocks = got_back[:, 0]
+    d_scaled_blocks = got_back[:, 1]
 
     grad_all = aggregate_backward(ids_flat, nbr_count, d_scaled_blocks, tiles, all_blocks)
     grad_group = lax.psum_scatter(grad_all, "node", scatter_dimension=0, tiled=True)

time: 269 us -> 208 us (0.77)
  blocking collectives: 86.5 us -> 17.3 us
  local copies, waits for them, and re-layouts: 51.7 us -> 9.21 us
  waiting for transfers between devices: 47.3 us -> 84.9 us
  starting transfers between devices: 12.2 us -> 33.8 us
  other arithmetic: 12.5 us -> 5.37 us
    all_to_all x1 -> x0, blocking collectives: 68.7 us -> none  [shards(): got_back = lax.all_to_all(back, 'feat', 0, 0, tiled=True)]
    all_to_all x0 -> x3, waiting for transfers between devices: none -> 68.2 us  [the longest x1 27.9 us: shards(): lax.all_to_all(part.reshape(feat_parts, cols, 2 * hidden), 'feat', 0, 0,...]
    unnamed x25 -> x13, local copies, waits for them, and re-layouts: 42.8 us -> 1.67 us
    all_to_all x0 -> x3, starting transfers between devices: none -> 21.8 us  [the longest x1 7.81 us: shards(): lax.all_to_all(back, 'feat', 0, 0, tiled=True)]
    all_to_all x1, waiting for transfers between devices: 37.8 us -> 16.7 us  [shards(): got = lax.all_to_all(sent, 'feat', 0, 0, tiled=True)]
    reduce_scatter x1, waiting for transfers between devices: 9.47 us -> 0.01 us  [shards(): lax.psum_scatter(grad_all, 'node', scatter_dimension=0, tiled=True)]
    all_to_all x4 -> x0, other arithmetic: 7.02 us -> none  [the longest x2 4.99 us: shards(): got_back = lax.all_to_all(back, 'feat', 0, 0, tiled=True)]
  transfers between devices with their start and end apart: 2 -> 5, of which waited for: 2 -> 4; matrix products, arithmetic and copies ran while one was open for 2% -> 3% of each run, Pallas kernels for 0% -> 9%
where the time goes in v4:
time: 208 us; the launch traced here: 207 us
  waiting for transfers between devices  84.9 us (41%)
  Pallas kernels  39.8 us (19%)
  starting transfers between devices  33.8 us (16%)
  blocking collectives  17.3 us (8%)
  between operations  14.2 us (7%)
  local copies, waits for them, and re-layouts  9.21 us (4%)
  other arithmetic  5.37 us (3%)
  matrix products  2.49 us (1%)
    all_to_all x1, waiting for transfers between devices, shards(): lax.all_to_all(part.reshape(feat_parts, cols, 2 * hidden), 'feat', 0, 0,...  27.9 us
    all_to_all x1, waiting for transfers between devices, shards(): lax.all_to_all(jnp.broadcast_to(w_both[None], (feat_parts,) + w_both.shap...  26.4 us
    pallas_call x1, Pallas kernels, aggregate_forward(): pl.pallas_call(forward_kernel, grid_spec=pltpu.PrefetchScalarGridSpec(num...  20.8 us
    pallas_call x1, Pallas kernels, aggregate_backward(): pl.pallas_call(backward_kernel, grid_spec=pltpu.PrefetchScalarGridSpec(nu...  19 us
    psum x1, blocking collectives, shards(): grads = lax.psum(jnp.sum(part_got, axis=0), 'node')  17.3 us
    all_to_all x1, waiting for transfers between devices, shards(): got = lax.all_to_all(sent, 'feat', 0, 0, tiled=True)  16.7 us
    all_to_all x1, waiting for transfers between devices, shards(): lax.all_to_all(back, 'feat', 0, 0, tiled=True)  13.9 us
    all_to_all x1, starting transfers between devices, shards(): got = lax.all_to_all(sent, 'feat', 0, 0, tiled=True)  12 us
  transfers between devices with their start and end apart: 5, of which 4 were waited for; matrix products, arithmetic and copies ran while one was open for 3% of the time, Pallas kernels for 9%

profile of v4, /device:TPU:2, one launch (start us, length us, event | category | flops | bytes accessed | tf_op | source)
XLA Modules:
  0.0 207.1 jit_solution(1829604867783927469)
XLA Ops:
  7.2 0.9 copy.18
  8.1 0.7 reshape.54.ids_ref
  8.7 1.2 copy_bitcast_fusion
  10.0 20.8 %shard_map.111 = (bf16[64,16,128]{2,1,0:T(8,128)(2,1)}, f32[64,1,128]{2,1,0:T(1,128)}) custom-call(s32[1024]{0:T(1024)} %reshape.54.ids_ref, s32[64]{0:T(128)} %cnt_ref.3, bf16[256,16,128]{2,1,0:T(8,128)(2,1)} %get-tuple-element.9.feat_ref, s32[64,16,8,128]{3,2,1,0:T(8,128)} %tiles_ref.3), custom_call_target="tpu_custom_call" | custom-call | tf_op jit(solution)/shard_map/pallas_call | solution.py:82
  30.8 1.0 maximum_bitcast_fusion
  31.8 0.8 copy.20
  32.6 12.0 %all-to-all-start = ((bf16[64,1,2,16,128]{4,3,2,1,0:T(8,128)(2,1)}), bf16[64,1,2,16,128]{4,3,2,1,0:T(8,128)(2,1)S(1)}, u32[]{:S(2)}, u32[]{:S(2)}) async-start(bf16[64,1,2,16,128]{4,3,2,1,0:T(8,128)(2,1)} %copy.20), calls=%async_computation | async-start | bytes 1048576 | tf_op jit(solution)/shard_map/all_to_all | solution.py:150
  44.7 16.7 %all-to-all-done = bf16[64,1,2,16,128]{4,3,2,1,0:T(8,128)(2,1)S(1)} async-done(((bf16[64,1,2,16,128]{4,3,2,1,0:T(8,128)(2,1)}), bf16[64,1,2,16,128]{4,3,2,1,0:T(8,128)(2,1)S(1)}, u32[]{:S(2)}, u32[]{:S(2)}) %all-to-all-start) | async-done | bytes 524320 | tf_op jit(solution)/shard_map/all_to_all | solution.py:150
  61.4 1.1 broadcast_in_dim.13
  62.5 7.0 %all-to-all-start.1 = ((bf16[64,16,512]{2,1,0:T(8,128)(2,1)}), bf16[64,16,512]{2,1,0:T(8,128)(2,1)S(1)}, u32[]{:S(2)}, u32[]{:S(2)}) async-start(bf16[64,16,512]{2,1,0:T(8,128)(2,1)} %broadcast_in_dim.13), calls=%async_computation.1 | async-start | bytes 2097152 | tf_op jit(solution)/shard_map/all_to_all | solution.py:142
  70.2 26.4 %all-to-all-done.1 = bf16[64,16,512]{2,1,0:T(8,128)(2,1)S(1)} async-done(((bf16[64,16,512]{2,1,0:T(8,128)(2,1)}), bf16[64,16,512]{2,1,0:T(8,128)(2,1)S(1)}, u32[]{:S(2)}, u32[]{:S(2)}) %all-to-all-start.1) | async-done | bytes 1048608 | tf_op jit(solution)/shard_map/all_to_all | solution.py:142
  96.9 1.0 fusion.13
  98.5 0.8 maximum_bitcast_fusion.1
  99.4 7.8 %all-to-all-start.2 = ((bf16[64,1,2,16,128]{4,3,2,1,0:T(8,128)(2,1)}), bf16[64,1,2,16,128]{4,3,2,1,0:T(8,128)(2,1)}, u32[]{:S(2)}, u32[]{:S(2)}) async-start(bf16[64,1,2,16,128]{4,3,2,1,0:T(8,128)(2,1)} %maximum_bitcast_fusion.1), calls=%async_computation.2 | async-start | bytes 1048576 | tf_op jit(solution)/shard_map/all_to_all | solution.py:193
  108.0 1.8 copy.25
  109.8 13.9 %all-to-all-done.2 = bf16[64,1,2,16,128]{4,3,2,1,0:T(8,128)(2,1)} async-done(((bf16[64,1,2,16,128]{4,3,2,1,0:T(8,128)(2,1)}), bf16[64,1,2,16,128]{4,3,2,1,0:T(8,128)(2,1)}, u32[]{:S(2)}, u32[]{:S(2)}) %all-to-all-start.2) | async-done | bytes 524320 | tf_op jit(solution)/shard_map/all_to_all | solution.py:193
  123.8 6.9 %all-to-all-start.3 = ((f32[64,16,512]{2,1,0:T(8,128)}), f32[64,16,512]{2,1,0:T(8,128)S(1)}, u32[]{:S(2)}, u32[]{:S(2)}) async-start(f32[64,16,512]{2,1,0:T(8,128)} %bitcast.19), calls=%async_computation.4 | async-start | bytes 4194304 | tf_op jit(solution)/shard_map/all_to_all | solution.py:182
  130.7 1.1 copy.33
  131.8 0.8 copy-done.1
  132.6 0.7 slice_bitcast_fusion.1.ds_ref
  133.3 19.0 %shard_map.112 = f32[256,16,128]{2,1,0:T(8,128)} custom-call(s32[1024]{0:T(1024)} %reshape.54.ids_ref, s32[64]{0:T(128)} %cnt_ref.3, bf16[64,16,128]{2,1,0:T(8,128)(2,1)} %slice_bitcast_fusion.1.ds_ref, s32[64,16,8,128]{3,2,1,0:T(8,128)} %tiles_ref.3), custom_call_target="tpu_custom_call" | custom-call | tf_op jit(solution)/shard_map/pallas_call | solution.py:108
  152.4 27.9 %all-to-all-done.3 = f32[64,16,512]{2,1,0:T(8,128)S(1)} async-done(((f32[64,16,512]{2,1,0:T(8,128)}), f32[64,16,512]{2,1,0:T(8,128)S(1)}, u32[]{:S(2)}, u32[]{:S(2)}) %all-to-all-start.3) | async-done | bytes 2097184 | tf_op jit(solution)/shard_map/all_to_all | solution.py:182
  180.4 17.3 %psum.7 = f32[16,512]{1,0:T(8,128)S(1)} all-reduce(f32[16,512]{1,0:T(8,128)S(1)} %reduce_sum.9), channel_id=1, replica_groups=mesh['feat'=64,'node'=4] {'node'}, use_global_device_ids=true, to_apply=%region_2.3 | all-reduce | flops 8192 | bytes 65536 | tf_op jit(solution)/shard_map/psum | solution.py:183
  198.3 1.9 copy_bitcast_fusion.1
  (26 shorter events, 3.2 us)
Async XLA Ops:
  7.2 1.6 copy-start
  30.8 13.9 %copy-start.2 = (bf16[16,256]{1,0:T(8,128)(2,1)S(1)}, bf16[16,256]{1,0:T(8,128)(2,1)}, u32[]{:S(2)}) copy-start(bf16[16,256]{1,0:T(8,128)(2,1)} %param.10) | copy-start | bytes 24580
  30.8 13.9 %copy-start.3 = (bf16[16,256]{1,0:T(8,128)(2,1)S(1)}, bf16[16,256]{1,0:T(8,128)(2,1)}, u32[]{:S(2)}) copy-start(bf16[16,256]{1,0:T(8,128)(2,1)} %param.9) | copy-start | bytes 24580
  32.6 28.7 %all-to-all-start = ((bf16[64,1,2,16,128]{4,3,2,1,0:T(8,128)(2,1)}), bf16[64,1,2,16,128]{4,3,2,1,0:T(8,128)(2,1)S(1)}, u32[]{:S(2)}, u32[]{:S(2)}) async-start(bf16[64,1,2,16,128]{4,3,2,1,0:T(8,128)(2,1)} %copy.20), calls=%async_computation | async-start | bytes 1048576 | tf_op jit(solution)/shard_map/all_to_all | solution.py:150
  62.5 34.5 %copy-start.4 = (bf16[128,256]{1,0:T(8,128)(2,1)S(1)}, bf16[128,256]{1,0:T(8,128)(2,1)}, u32[]{:S(2)}) copy-start(bf16[128,256]{1,0:T(8,128)(2,1)} %param.12) | copy-start | bytes 196612
  62.5 34.5 %copy-start.5 = (f32[256]{0:T(256)S(1)}, f32[256]{0:T(256)}, u32[]{:S(2)}) copy-start(f32[256]{0:T(256)} %param.11) | copy-start | bytes 3076
  62.5 34.2 %all-to-all-start.1 = ((bf16[64,16,512]{2,1,0:T(8,128)(2,1)}), bf16[64,16,512]{2,1,0:T(8,128)(2,1)S(1)}, u32[]{:S(2)}, u32[]{:S(2)}) async-start(bf16[64,16,512]{2,1,0:T(8,128)(2,1)} %broadcast_in_dim.13), calls=%async_computation.1 | async-start | bytes 2097152 | tf_op jit(solution)/shard_map/all_to_all | solution.py:142
  99.4 24.4 %all-to-all-start.2 = ((bf16[64,1,2,16,128]{4,3,2,1,0:T(8,128)(2,1)}), bf16[64,1,2,16,128]{4,3,2,1,0:T(8,128)(2,1)}, u32[]{:S(2)}, u32[]{:S(2)}) async-start(bf16[64,1,2,16,128]{4,3,2,1,0:T(8,128)(2,1)} %maximum_bitcast_fusion.1), calls=%async_computation.2 | async-start | bytes 1048576 | tf_op jit(solution)/shard_map/all_to_all | solution.py:193
  123.8 56.5 %all-to-all-start.3 = ((f32[64,16,512]{2,1,0:T(8,128)}), f32[64,16,512]{2,1,0:T(8,128)S(1)}, u32[]{:S(2)}, u32[]{:S(2)}) async-start(f32[64,16,512]{2,1,0:T(8,128)} %bitcast.19), calls=%async_computation.4 | async-start | bytes 4194304 | tf_op jit(solution)/shard_map/all_to_all | solution.py:182
  130.7 67.6 %reduce-scatter.2.cloned.1.call-start = ((), (), s32[]{:S(2)}) async-start(), calls=%async_computation.5 | async-start | bytes 2621440 | tf_op jit(solution)/shard_map/reduce_scatter | solution.py:198
  131.8 0.8 copy-start.1
Sparse Core Ops, SparseCore 0:
  152.5 33.4 reduce-scatter.1

commit v5 on v4

--- a/solution.py
+++ b/solution.py
@@ -1,3 +1,4 @@
+import functools
 import math
 
 import jax
@@ -121,6 +122,71 @@
     )(ids_flat, counts, ds_blocks, tiles)
 
 
+def exchange_kernel(parts, kinds, *refs):
+    n_in = len(kinds)
+    ins, outs = refs[:n_in], refs[n_in : 2 * n_in]
+    send_sems, recv_sems = refs[2 * n_in :]
+    me = lax.axis_index("feat")
+    mesh_id = pl.DeviceIdType.MESH
+
+    barrier = pltpu.get_barrier_semaphore()
+
+    def greet(k, carry):
+        peer = lax.rem(me + k, parts)
+        pl.semaphore_signal(barrier, 1, device_id={"feat": peer}, device_id_type=mesh_id)
+        return carry
+
+    lax.fori_loop(1, parts, greet, 0)
+    pl.semaphore_wait(barrier, parts - 1)
+
+    def copy(i, k):
+        peer = lax.rem(me + k, parts)
+        src = ins[i] if kinds[i] else ins[i].at[peer]
+        return pltpu.make_async_remote_copy(
+            src_ref=src,
+            dst_ref=outs[i].at[me],
+            send_sem=send_sems.at[i, k],
+            recv_sem=recv_sems.at[i, k],
+            device_id={"feat": peer},
+            device_id_type=mesh_id,
+        )
+
+    def start(k, carry):
+        for i in range(n_in):
+            copy(i, k).start()
+        return carry
+
+    lax.fori_loop(1, parts, start, 0)
+    for i in range(n_in):
+        outs[i][me] = ins[i][...] if kinds[i] else ins[i][me]
+
+    def finish(k, carry):
+        for i in range(n_in):
+            copy(i, k).wait()
+        return carry
+
+    lax.fori_loop(1, parts, finish, 0)
+
+
+def exchange(arrays, kinds, parts, cid):
+    out_shapes = [
+        jax.ShapeDtypeStruct(((parts,) + x.shape) if kind else x.shape, x.dtype)
+        for x, kind in zip(arrays, kinds)
+    ]
+    vmem = pl.BlockSpec(memory_space=pltpu.VMEM)
+    return pl.pallas_call(
+        functools.partial(exchange_kernel, parts, tuple(kinds)),
+        out_shape=out_shapes,
+        in_specs=[vmem] * len(arrays),
+        out_specs=[vmem] * len(arrays),
+        scratch_shapes=[
+            pltpu.SemaphoreType.DMA((len(arrays), parts)),
+            pltpu.SemaphoreType.DMA((len(arrays), parts)),
+        ],
+        compiler_params=pltpu.CompilerParams(collective_id=cid, has_side_effects=True),
+    )(*arrays)
+
+
 def shards(features, w_self, w_neigh, bias, d_out, nbr_ids, nbr_count, tiles):
     node_total, cols = features.shape
     hidden = w_self.shape[1]
@@ -139,15 +205,13 @@
     nm_t, deg_blocks = aggregate_forward(ids_flat, nbr_count, feat_t, tiles)
 
     w_both = jnp.concatenate([w_self, w_neigh], axis=1)
-    w_all = lax.all_to_all(
-        jnp.broadcast_to(w_both[None], (feat_parts,) + w_both.shape), "feat", 0, 0, tiled=True
-    ).reshape(feat_parts * cols, 2 * hidden)
+    group_t = lax.dynamic_slice_in_dim(feat_t, node_group * blocks_here, blocks_here, 0)
+    sent = jnp.stack([group_t, nm_t], axis=1).reshape(feat_parts, per, 2, cols, block_size)
+    got, w_all = exchange([sent, w_both], [False, True], feat_parts, 0)
+    w_all = w_all.reshape(feat_parts * cols, 2 * hidden)
     w_self_all = w_all[:, :hidden]
     w_neigh_all = w_all[:, hidden:]
 
-    group_t = lax.dynamic_slice_in_dim(feat_t, node_group * blocks_here, blocks_here, 0)
-    sent = jnp.stack([group_t, nm_t], axis=1).reshape(feat_parts, per, 2, cols, block_size)
-    got = lax.all_to_all(sent, "feat", 0, 0, tiled=True)
     own = got.transpose(2, 1, 4, 0, 3).reshape(2, own_nodes, feat_parts * cols)
     own_feat = own[0]
     own_nm = own[1]
@@ -179,20 +243,21 @@
         ],
         axis=1,
     )
-    part_got = lax.all_to_all(part.reshape(feat_parts, cols, 2 * hidden), "feat", 0, 0, tiled=True)
+    back = (
+        jnp.stack([d_self_t, d_scaled_t], axis=0)
+        .reshape(2, feat_parts, cols, per, block_size)
+        .transpose(1, 3, 0, 2, 4)
+    )
+    got_back, part_got = exchange(
+        [back, part.reshape(feat_parts, cols, 2 * hidden)], [False, False], feat_parts, 1
+    )
+    got_back = got_back.reshape(blocks_here, 2, cols, block_size)
+    d_self_blocks = got_back[:, 0]
+    d_scaled_blocks = got_back[:, 1]
     grads = lax.psum(jnp.sum(part_got, axis=0), "node")
     grad_scale = 1.0 / math.sqrt(node_total)
     grad_self = grads[:, :hidden] * grad_scale
     grad_neigh = grads[:, hidden:] * grad_scale
-
-    back = (
-        jnp.stack([d_self_t, d_scaled_t], axis=0)
-        .reshape(2, feat_parts, cols, per, block_size)
-        .transpose(1, 3, 0, 2, 4)
-    )
-    got_back = lax.all_to_all(back, "feat", 0, 0, tiled=True).reshape(blocks_here, 2, cols, block_size)
-    d_self_blocks = got_back[:, 0]
-    d_scaled_blocks = got_back[:, 1]
 
     grad_all = aggregate_backward(ids_flat, nbr_count, d_scaled_blocks, tiles, all_blocks)
     grad_group = lax.psum_scatter(grad_all, "node", scatter_dimension=0, tiled=True)

time: 208 us -> 233 us (1.12)
  Pallas kernels: 39.8 us -> 162 us
  waiting for transfers between devices: 84.9 us -> 12.3 us
  starting transfers between devices: 33.8 us -> 0.04 us
  matrix products: 2.49 us -> 7.27 us
  other arithmetic: 5.37 us -> 7.82 us
    pallas_call x0 -> x2, Pallas kernels: none -> 123 us  [exchange(): pl.pallas_call(functools.partial(exchange_kernel, parts, tuple(kinds)), o...]
    all_to_all x4 -> x0, waiting for transfers between devices: 84.9 us -> none  [the longest x1 27.9 us: shards(): lax.all_to_all(part.reshape(feat_parts, cols, 2 * hidden), 'feat', 0, 0,...]
    all_to_all x4 -> x0, starting transfers between devices: 33.8 us -> none  [the longest x1 12 us: shards(): got = lax.all_to_all(sent, 'feat', 0, 0, tiled=True)]
    reduce_scatter x1, waiting for transfers between devices: 0.01 us -> 12.3 us  [shards(): lax.psum_scatter(grad_all, 'node', scatter_dimension=0, tiled=True)]
  transfers between devices with their start and end apart: 5 -> 1, of which waited for: 4 -> 1; matrix products, arithmetic and copies ran while one was open for 3% -> 0% of each run, Pallas kernels for 9% -> 0%
where the time goes in v5:
time: 233 us; the launch traced here: 232 us
  Pallas kernels  162 us (70%)
  blocking collectives  17.5 us (8%)
  between operations  14.2 us (6%)
  waiting for transfers between devices  12.3 us (5%)
  local copies, waits for them, and re-layouts  9.98 us (4%)
  other arithmetic  7.82 us (3%)
  matrix products  7.27 us (3%)
    pallas_call x2, Pallas kernels, exchange(): pl.pallas_call(functools.partial(exchange_kernel, parts, tuple(kinds)), o...  123 us
    pallas_call x1, Pallas kernels, aggregate_forward(): pl.pallas_call(forward_kernel, grid_spec=pltpu.PrefetchScalarGridSpec(num...  20.8 us
    pallas_call x1, Pallas kernels, aggregate_backward(): pl.pallas_call(backward_kernel, grid_spec=pltpu.PrefetchScalarGridSpec(nu...  19 us
    psum x1, blocking collectives, shards(): grads = lax.psum(jnp.sum(part_got, axis=0), 'node')  17.5 us
    reduce_scatter x1, waiting for transfers between devices, shards(): lax.psum_scatter(grad_all, 'node', scatter_dimension=0, tiled=True)  12.3 us
  transfers between devices with their start and end apart: 1, of which 1 were waited for; matrix products, arithmetic and copies ran while one was open for 0% of the time, Pallas kernels for 0%

profile of v5, /device:TPU:2, one launch (start us, length us, event | category | flops | bytes accessed | tf_op | source)
XLA Modules:
  0.0 231.5 jit_solution(12570574456392901091)
XLA Ops:
  7.3 0.9 copy.15
  8.1 0.7 reshape.53.ids_ref
  8.8 1.2 copy_bitcast_fusion
  10.7 20.8 %shard_map.111 = (bf16[64,16,128]{2,1,0:T(8,128)(2,1)}, f32[64,1,128]{2,1,0:T(1,128)}) custom-call(s32[1024]{0:T(1024)} %reshape.53.ids_ref, s32[64]{0:T(128)} %cnt_ref.3, bf16[256,16,128]{2,1,0:T(8,128)(2,1)} %get-tuple-element.17.feat_ref, s32[64,16,8,128]{3,2,1,0:T(8,128)} %tiles_ref.3), custom_call_target="tpu_custom_call" | custom-call | tf_op jit(solution)/shard_map/pallas_call | solution.py:83
  31.5 1.8 maximum_bitcast_fusion.refs_0_
  33.3 48.8 %shard_map.112 = (bf16[64,1,2,16,128]{4,3,2,1,0:T(8,128)(2,1)}, bf16[64,16,512]{2,1,0:T(8,128)(2,1)}) custom-call(bf16[64,1,2,16,128]{4,3,2,1,0:T(8,128)(2,1)} %maximum_bitcast_fusion.refs_0_, bf16[16,512]{1,0:T(8,128)(2,1)} %pad_maximum_fusion.1.refs_1_), custom_call_target="tpu_custom_call" | custom-call | tf_op jit(solution)/shard_map/pallas_call | solution.py:177
  82.1 1.2 fusion.15
  83.3 1.3 fusion.8
  84.6 2.0 fusion.13
  87.0 1.3 fusion.17
  88.3 1.3 fusion.16
  89.6 0.8 maximum_bitcast_fusion.2
  90.4 1.0 fusion.2
  91.5 1.8 copy.17
  93.4 1.8 maximum_bitcast_fusion.1.refs_0_
  95.2 73.8 %shard_map.113 = (bf16[64,1,2,16,128]{4,3,2,1,0:T(8,128)(2,1)}, f32[64,16,512]{2,1,0:T(8,128)}) custom-call(bf16[64,1,2,16,128]{4,3,2,1,0:T(8,128)(2,1)} %maximum_bitcast_fusion.1.refs_0_, f32[64,16,512]{2,1,0:T(8,128)} %bitcast.52), custom_call_target="tpu_custom_call" | custom-call | tf_op jit(solution)/shard_map/pallas_call | solution.py:177
  168.9 1.1 copy.27
  170.0 0.8 copy-done.4
  170.8 0.7 slice_bitcast_fusion.1.ds_ref
  171.5 19.0 %shard_map.114 = f32[256,16,128]{2,1,0:T(8,128)} custom-call(s32[1024]{0:T(1024)} %reshape.53.ids_ref, s32[64]{0:T(128)} %cnt_ref.3, bf16[64,16,128]{2,1,0:T(8,128)(2,1)} %slice_bitcast_fusion.1.ds_ref, s32[64,16,8,128]{3,2,1,0:T(8,128)} %tiles_ref.3), custom_call_target="tpu_custom_call" | custom-call | tf_op jit(solution)/shard_map/pallas_call | solution.py:109
  190.6 1.6 copy-done.3
  192.3 17.5 %psum.7 = f32[16,512]{1,0:T(8,128)S(1)} all-reduce(f32[16,512]{1,0:T(8,128)S(1)} %reduce_sum.9), channel_id=1, replica_groups=mesh['feat'=64,'node'=4] {'node'}, use_global_device_ids=true, to_apply=%region_2.3 | all-reduce | flops 8192 | bytes 65536 | tf_op jit(solution)/shard_map/psum | solution.py:257
  210.4 12.3 %reduce-scatter.2.cloned.1.call-done = f32[64,16,128]{2,1,0:T(8,128)} async-done(((f32[256,16,128]{2,1,0:T(8,128)}), f32[64,16,128]{2,1,0:T(8,128)}) %reduce-scatter.2.cloned.1.call-update) | async-done | bytes 524304 | tf_op jit(solution)/shard_map/reduce_scatter | solution.py:263
  222.8 1.9 copy_bitcast_fusion.1
  (26 shorter events, 1.9 us)
Async XLA Ops:
  7.2 1.6 copy-start
  7.2 2.8 %copy-start.6 = (bf16[16,256]{1,0:T(8,128)(2,1)S(1)}, bf16[16,256]{1,0:T(8,128)(2,1)}, u32[]{:S(2)}) copy-start(bf16[16,256]{1,0:T(8,128)(2,1)} %param.10) | copy-start | bytes 24580
  7.2 2.8 %copy-start.7 = (bf16[16,256]{1,0:T(8,128)(2,1)S(1)}, bf16[16,256]{1,0:T(8,128)(2,1)}, u32[]{:S(2)}) copy-start(bf16[16,256]{1,0:T(8,128)(2,1)} %param.9) | copy-start | bytes 24580
  7.2 215.6 %reduce-scatter.2.cloned.1.call-start = ((), (), s32[]{:S(2)}) async-start(), calls=%async_computation.1 | async-start | bytes 2621440 | tf_op jit(solution)/shard_map/reduce_scatter | solution.py:263
  31.5 53.2 %copy-start.8 = (bf16[128,256]{1,0:T(8,128)(2,1)S(1)}, bf16[128,256]{1,0:T(8,128)(2,1)}, u32[]{:S(2)}) copy-start(bf16[128,256]{1,0:T(8,128)(2,1)} %param.12) | copy-start | bytes 196612
  31.5 53.2 %copy-start.9 = (f32[256]{0:T(256)S(1)}, f32[256]{0:T(256)}, u32[]{:S(2)}) copy-start(f32[256]{0:T(256)} %param.11) | copy-start | bytes 3076
  82.1 4.5 %copy-start.5 = (bf16[64,16,512]{2,1,0:T(8,128)(2,1)S(1)}, bf16[64,16,512]{2,1,0:T(8,128)(2,1)}, u32[]{:S(2)}) copy-start(bf16[64,16,512]{2,1,0:T(8,128)(2,1)} %get-tuple-element.12) | copy-start | bytes 3145732
  89.6 1.8 copy-start.1
  89.6 1.8 copy-start.2
  170.0 0.8 copy-start.4
  190.5 1.6 copy-start.3
Sparse Core Ops, SparseCore 0:
  190.7 32.0 reduce-scatter.1

commit v6 on v5

--- a/solution.py
+++ b/solution.py
@@ -243,21 +243,20 @@
         ],
         axis=1,
     )
+    part_got = lax.all_to_all(part.reshape(feat_parts, cols, 2 * hidden), "feat", 0, 0, tiled=True)
+    grads = lax.psum(jnp.sum(part_got, axis=0), "node")
+    grad_scale = 1.0 / math.sqrt(node_total)
+    grad_self = grads[:, :hidden] * grad_scale
+    grad_neigh = grads[:, hidden:] * grad_scale
+
     back = (
         jnp.stack([d_self_t, d_scaled_t], axis=0)
         .reshape(2, feat_parts, cols, per, block_size)
         .transpose(1, 3, 0, 2, 4)
     )
-    got_back, part_got = exchange(
-        [back, part.reshape(feat_parts, cols, 2 * hidden)], [False, False], feat_parts, 1
-    )
-    got_back = got_back.reshape(blocks_here, 2, cols, block_size)
+    got_back = lax.all_to_all(back, "feat", 0, 0, tiled=True).reshape(blocks_here, 2, cols, block_size)
     d_self_blocks = got_back[:, 0]
     d_scaled_blocks = got_back[:, 1]
-    grads = lax.psum(jnp.sum(part_got, axis=0), "node")
-    grad_scale = 1.0 / math.sqrt(node_total)
-    grad_self = grads[:, :hidden] * grad_scale
-    grad_neigh = grads[:, hidden:] * grad_scale
 
     grad_all = aggregate_backward(ids_flat, nbr_count, d_scaled_blocks, tiles, all_blocks)
     grad_group = lax.psum_scatter(grad_all, "node", scatter_dimension=0, tiled=True)

time: 233 us -> 201 us (0.86)
  Pallas kernels: 162 us -> 88.8 us
  waiting for transfers between devices: 12.3 us -> 41.8 us
  starting transfers between devices: 0.04 us -> 18.2 us
  matrix products: 7.27 us -> 4.56 us
    pallas_call x2 -> x1, Pallas kernels: 123 us -> 48.8 us  [exchange(): pl.pallas_call(functools.partial(exchange_kernel, parts, tuple(kinds)), o...]
    all_to_all x0 -> x2, waiting for transfers between devices: none -> 41.8 us  [the longest x1 27.9 us: shards(): lax.all_to_all(part.reshape(feat_parts, cols, 2 * hidden), 'feat', 0, 0,...]
    all_to_all x0 -> x2, starting transfers between devices: none -> 18.1 us  [the longest x1 11.2 us: shards(): lax.all_to_all(back, 'feat', 0, 0, tiled=True)]
    reduce_scatter x1, waiting for transfers between devices: 12.3 us -> 0.01 us  [shards(): lax.psum_scatter(grad_all, 'node', scatter_dimension=0, tiled=True)]
  transfers between devices with their start and end apart: 1 -> 3, of which waited for: 1 -> 2; matrix products, arithmetic and copies ran while one was open for 0% -> 3% of each run, Pallas kernels for 0% -> 10%
where the time goes in v6:
time: 201 us; the launch traced here: 200 us
  Pallas kernels  88.8 us (44%)
  waiting for transfers between devices  41.8 us (21%)
  starting transfers between devices  18.2 us (9%)
  blocking collectives  17.3 us (9%)
  between operations  14.2 us (7%)
  local copies, waits for them, and re-layouts  8.42 us (4%)
  other arithmetic  6.77 us (3%)
  matrix products  4.56 us (2%)
    pallas_call x1, Pallas kernels, exchange(): pl.pallas_call(functools.partial(exchange_kernel, parts, tuple(kinds)), o...  48.8 us
    all_to_all x1, waiting for transfers between devices, shards(): lax.all_to_all(part.reshape(feat_parts, cols, 2 * hidden), 'feat', 0, 0,...  27.9 us
    pallas_call x1, Pallas kernels, aggregate_forward(): pl.pallas_call(forward_kernel, grid_spec=pltpu.PrefetchScalarGridSpec(num...  20.9 us
    pallas_call x1, Pallas kernels, aggregate_backward(): pl.pallas_call(backward_kernel, grid_spec=pltpu.PrefetchScalarGridSpec(nu...  19 us
    psum x1, blocking collectives, shards(): grads = lax.psum(jnp.sum(part_got, axis=0), 'node')  17.3 us
    all_to_all x1, waiting for transfers between devices, shards(): lax.all_to_all(back, 'feat', 0, 0, tiled=True)  13.9 us
    all_to_all x1, starting transfers between devices, shards(): lax.all_to_all(back, 'feat', 0, 0, tiled=True)  11.2 us
    all_to_all x1, starting transfers between devices, shards(): lax.all_to_all(part.reshape(feat_parts, cols, 2 * hidden), 'feat', 0, 0,...  6.91 us
  transfers between devices with their start and end apart: 3, of which 2 were waited for; matrix products, arithmetic and copies ran while one was open for 3% of the time, Pallas kernels for 10%

profile of v6, /device:TPU:2, one launch (start us, length us, event | category | flops | bytes accessed | tf_op | source)
XLA Modules:
  0.0 200.0 jit_solution(1751819999327970478)
XLA Ops:
  7.2 0.9 copy.18
  8.1 0.7 reshape.53.ids_ref
  8.7 1.2 copy_bitcast_fusion
  10.0 20.9 %shard_map.111 = (bf16[64,16,128]{2,1,0:T(8,128)(2,1)}, f32[64,1,128]{2,1,0:T(1,128)}) custom-call(s32[1024]{0:T(1024)} %reshape.53.ids_ref, s32[64]{0:T(128)} %cnt_ref.3, bf16[256,16,128]{2,1,0:T(8,128)(2,1)} %get-tuple-element.13.feat_ref, s32[64,16,8,128]{3,2,1,0:T(8,128)} %tiles_ref.3), custom_call_target="tpu_custom_call" | custom-call | tf_op jit(solution)/shard_map/pallas_call | solution.py:83
  30.9 1.8 maximum_bitcast_fusion.refs_0_
  32.8 0.6 pad_maximum_fusion.1.refs_1_
  33.4 48.8 %shard_map.112 = (bf16[64,1,2,16,128]{4,3,2,1,0:T(8,128)(2,1)}, bf16[64,16,512]{2,1,0:T(8,128)(2,1)}) custom-call(bf16[64,1,2,16,128]{4,3,2,1,0:T(8,128)(2,1)} %maximum_bitcast_fusion.refs_0_, bf16[16,512]{1,0:T(8,128)(2,1)} %pad_maximum_fusion.1.refs_1_), custom_call_target="tpu_custom_call" | custom-call | tf_op jit(solution)/shard_map/pallas_call | solution.py:177
  82.2 1.2 fusion.15
  83.4 1.3 fusion.8
  84.7 2.0 %fusion.13 = (bf16[128,256]{1,0:T(8,128)(2,1)S(1)}, bf16[128,256]{1,0:T(8,128)(2,1)}) fusion(bf16[128,256]{1,0:T(8,128)(2,1)S(1)} %copy-done.5, f32[256]{0:T(256)S(1)} %copy-done.6, f32[128,256]{1,0:T(8,128)S(1)} %fusion.8, bf16[128,1024]{0,1:T(8,128)(2,1)S(1)} %bitcast.65, bf16[1024,512]{1,0:T(8,128)(2,1)} %bitcast.61), kind=kOutput, calls=%fused_computation.29 | convolution fusion | flops 67469312 | bytes 1115136 | tf_op jit(solution)/shard_map/dot_general | solution.py:221
  87.0 0.7 maximum_bitcast_fusion.2
  88.0 0.8 maximum_bitcast_fusion.1
  88.8 11.2 %all-to-all-start = ((bf16[64,1,2,16,128]{4,3,2,1,0:T(8,128)(2,1)}), bf16[64,1,2,16,128]{4,3,2,1,0:T(8,128)(2,1)}, u32[]{:S(2)}, u32[]{:S(2)}) async-start(bf16[64,1,2,16,128]{4,3,2,1,0:T(8,128)(2,1)} %maximum_bitcast_fusion.1), calls=%async_computation | async-start | bytes 1048576 | tf_op jit(solution)/shard_map/all_to_all | solution.py:257
  100.9 1.8 copy.24
  102.7 13.9 %all-to-all-done = bf16[64,1,2,16,128]{4,3,2,1,0:T(8,128)(2,1)} async-done(((bf16[64,1,2,16,128]{4,3,2,1,0:T(8,128)(2,1)}), bf16[64,1,2,16,128]{4,3,2,1,0:T(8,128)(2,1)}, u32[]{:S(2)}, u32[]{:S(2)}) %all-to-all-start) | async-done | bytes 524320 | tf_op jit(solution)/shard_map/all_to_all | solution.py:257
  116.7 6.9 %all-to-all-start.1 = ((f32[64,16,512]{2,1,0:T(8,128)}), f32[64,16,512]{2,1,0:T(8,128)S(1)}, u32[]{:S(2)}, u32[]{:S(2)}) async-start(f32[64,16,512]{2,1,0:T(8,128)} %bitcast.19), calls=%async_computation.2 | async-start | bytes 4194304 | tf_op jit(solution)/shard_map/all_to_all | solution.py:246
  123.6 1.1 copy.32
  124.7 0.8 copy-done.1
  125.5 0.7 slice_bitcast_fusion.1.ds_ref
  126.2 19.0 %shard_map.113 = f32[256,16,128]{2,1,0:T(8,128)} custom-call(s32[1024]{0:T(1024)} %reshape.53.ids_ref, s32[64]{0:T(128)} %cnt_ref.3, bf16[64,16,128]{2,1,0:T(8,128)(2,1)} %slice_bitcast_fusion.1.ds_ref, s32[64,16,8,128]{3,2,1,0:T(8,128)} %tiles_ref.3), custom_call_target="tpu_custom_call" | custom-call | tf_op jit(solution)/shard_map/pallas_call | solution.py:109
  145.3 27.9 %all-to-all-done.1 = f32[64,16,512]{2,1,0:T(8,128)S(1)} async-done(((f32[64,16,512]{2,1,0:T(8,128)}), f32[64,16,512]{2,1,0:T(8,128)S(1)}, u32[]{:S(2)}, u32[]{:S(2)}) %all-to-all-start.1) | async-done | bytes 2097184 | tf_op jit(solution)/shard_map/all_to_all | solution.py:246
  173.3 17.3 %psum.7 = f32[16,512]{1,0:T(8,128)S(1)} all-reduce(f32[16,512]{1,0:T(8,128)S(1)} %reduce_sum.9), channel_id=1, replica_groups=mesh['feat'=64,'node'=4] {'node'}, use_global_device_ids=true, to_apply=%region_2.3 | all-reduce | flops 8192 | bytes 65536 | tf_op jit(solution)/shard_map/psum | solution.py:247
  190.6 0.6 slice_multiply_fusion
  191.2 1.9 copy_bitcast_fusion.1
  (23 shorter events, 1.6 us)
Async XLA Ops:
  7.2 1.6 copy-start
  10.0 22.8 %copy-start.3 = (bf16[16,256]{1,0:T(8,128)(2,1)S(1)}, bf16[16,256]{1,0:T(8,128)(2,1)}, u32[]{:S(2)}) copy-start(bf16[16,256]{1,0:T(8,128)(2,1)} %param.10) | copy-start | bytes 24580
  10.0 22.8 %copy-start.4 = (bf16[16,256]{1,0:T(8,128)(2,1)S(1)}, bf16[16,256]{1,0:T(8,128)(2,1)}, u32[]{:S(2)}) copy-start(bf16[16,256]{1,0:T(8,128)(2,1)} %param.9) | copy-start | bytes 24580
  30.9 53.8 %copy-start.5 = (bf16[128,256]{1,0:T(8,128)(2,1)S(1)}, bf16[128,256]{1,0:T(8,128)(2,1)}, u32[]{:S(2)}) copy-start(bf16[128,256]{1,0:T(8,128)(2,1)} %param.12) | copy-start | bytes 196612
  30.9 53.8 %copy-start.6 = (f32[256]{0:T(256)S(1)}, f32[256]{0:T(256)}, u32[]{:S(2)}) copy-start(f32[256]{0:T(256)} %param.11) | copy-start | bytes 3076
  82.2 4.5 %copy-start.2 = (bf16[64,16,512]{2,1,0:T(8,128)(2,1)S(1)}, bf16[64,16,512]{2,1,0:T(8,128)(2,1)}, u32[]{:S(2)}) copy-start(bf16[64,16,512]{2,1,0:T(8,128)(2,1)} %get-tuple-element.10) | copy-start | bytes 3145732
  88.8 27.8 %all-to-all-start = ((bf16[64,1,2,16,128]{4,3,2,1,0:T(8,128)(2,1)}), bf16[64,1,2,16,128]{4,3,2,1,0:T(8,128)(2,1)}, u32[]{:S(2)}, u32[]{:S(2)}) async-start(bf16[64,1,2,16,128]{4,3,2,1,0:T(8,128)(2,1)} %maximum_bitcast_fusion.1), calls=%async_computation | async-start | bytes 1048576 | tf_op jit(solution)/shard_map/all_to_all | solution.py:257
  116.7 56.5 %all-to-all-start.1 = ((f32[64,16,512]{2,1,0:T(8,128)}), f32[64,16,512]{2,1,0:T(8,128)S(1)}, u32[]{:S(2)}, u32[]{:S(2)}) async-start(f32[64,16,512]{2,1,0:T(8,128)} %bitcast.19), calls=%async_computation.2 | async-start | bytes 4194304 | tf_op jit(solution)/shard_map/all_to_all | solution.py:246
  123.6 67.6 %reduce-scatter.2.cloned.1.call-start = ((), (), s32[]{:S(2)}) async-start(), calls=%async_computation.3 | async-start | bytes 2621440 | tf_op jit(solution)/shard_map/reduce_scatter | solution.py:262
  124.7 0.8 copy-start.1
Sparse Core Ops, SparseCore 0:
  145.4 33.5 reduce-scatter.1

commit v7 on v6

--- a/solution.py
+++ b/solution.py
@@ -187,6 +187,118 @@
     )(*arrays)
 
 
+def forward_exchange_kernel(
+    parts, ids_ref, cnt_ref, feat_ref, tiles_ref, w_ref,
+    feat_out, nm_out, w_out, deg_ref, nm_scr, send_sems, recv_sems,
+):
+    me = lax.axis_index("feat")
+    group = lax.axis_index("node")
+    blocks_here, slots = tiles_ref.shape[0], tiles_ref.shape[1]
+    cols, width = feat_ref.shape[1], feat_ref.shape[2]
+    per = blocks_here // parts
+    mesh_id = pl.DeviceIdType.MESH
+
+    barrier = pltpu.get_barrier_semaphore()
+
+    def greet(k, carry):
+        peer = lax.rem(me + k, parts)
+        pl.semaphore_signal(barrier, 1, device_id={"feat": peer}, device_id_type=mesh_id)
+        return carry
+
+    lax.fori_loop(1, parts, greet, 0)
+    pl.semaphore_wait(barrier, parts - 1)
+
+    def copy(i, k):
+        peer = lax.rem(me + k, parts)
+        if i == 0:
+            src, dst = w_ref, w_out
+        elif i == 1:
+            src, dst = feat_ref.at[pl.ds(group * blocks_here + peer * per, per)], feat_out
+        else:
+            src, dst = nm_scr.at[pl.ds(peer * per, per)], nm_out
+        return pltpu.make_async_remote_copy(
+            src_ref=src,
+            dst_ref=dst.at[me],
+            send_sem=send_sems.at[i, k],
+            recv_sem=recv_sems.at[i, k],
+            device_id={"feat": peer},
+            device_id_type=mesh_id,
+        )
+
+    def start_inputs(k, carry):
+        copy(0, k).start()
+        copy(1, k).start()
+        return carry
+
+    lax.fori_loop(1, parts, start_inputs, 0)
+    w_out[me] = w_ref[...]
+    feat_out[me] = feat_ref[pl.ds(group * blocks_here + me * per, per)]
+
+    def row(b, carry):
+        cnt = cnt_ref[b]
+        adjs, lhs = [], []
+        for s in range(slots):
+            live = jnp.where(s < cnt, 1.0, 0.0)
+            adjs.append(unpack_tile(tiles_ref[b, s]))
+            src = feat_ref[ids_ref[b * slots + s]].astype(jnp.float32) * live
+            lhs.append(
+                jnp.concatenate([src, jnp.full((cols, width), live, jnp.float32)], axis=0).astype(
+                    jnp.bfloat16
+                )
+            )
+        out = lax.dot_general(
+            jnp.concatenate(lhs, axis=1),
+            jnp.concatenate(adjs, axis=1),
+            (((1,), (1,)), ((), ())),
+            preferred_element_type=jnp.float32,
+        )
+        deg = out[cols : cols + 1, :]
+        nm_scr[b] = (out[:cols, :] / jnp.maximum(deg, 1.0)).astype(nm_scr.dtype)
+        deg_ref[b] = deg
+        return carry
+
+    lax.fori_loop(0, blocks_here, row, 0)
+
+    def start_result(k, carry):
+        copy(2, k).start()
+        return carry
+
+    lax.fori_loop(1, parts, start_result, 0)
+    nm_out[me] = nm_scr[pl.ds(me * per, per)]
+
+    def finish(k, carry):
+        for i in range(3):
+            copy(i, k).wait()
+        return carry
+
+    lax.fori_loop(1, parts, finish, 0)
+
+
+def forward_exchange(ids_flat, counts, feat_t, tiles, w_both, parts):
+    blocks_here, slots, nwords, width = tiles.shape
+    all_blocks, cols, _ = feat_t.shape
+    per = blocks_here // parts
+    vmem = pl.BlockSpec(memory_space=pltpu.VMEM)
+    smem = pl.BlockSpec(memory_space=pltpu.SMEM)
+    return pl.pallas_call(
+        functools.partial(forward_exchange_kernel, parts),
+        out_shape=[
+            jax.ShapeDtypeStruct((parts, per, cols, width), jnp.bfloat16),
+            jax.ShapeDtypeStruct((parts, per, cols, width), jnp.bfloat16),
+            jax.ShapeDtypeStruct((parts,) + w_both.shape, w_both.dtype),
+            jax.ShapeDtypeStruct((blocks_here, 1, width), jnp.float32),
+        ],
+        in_specs=[smem, smem, vmem, vmem, vmem],
+        out_specs=[vmem] * 4,
+        scratch_shapes=[
+            pltpu.VMEM((blocks_here, cols, width), jnp.bfloat16),
+            pltpu.SemaphoreType.DMA((3, parts)),
+            pltpu.SemaphoreType.DMA((3, parts)),
+        ],
+        compiler_params=pltpu.CompilerParams(collective_id=0, has_side_effects=True),
+    )(ids_flat, counts, feat_t, tiles, w_both)
+
+
 def shards(features, w_self, w_neigh, bias, d_out, nbr_ids, nbr_count, tiles):
     node_total, cols = features.shape
     hidden = w_self.shape[1]
@@ -202,19 +314,15 @@
     feat_t = features.reshape(all_blocks, block_size, cols).transpose(0, 2, 1)
     ids_flat = nbr_ids.reshape(-1)
 
-    nm_t, deg_blocks = aggregate_forward(ids_flat, nbr_count, feat_t, tiles)
-
     w_both = jnp.concatenate([w_self, w_neigh], axis=1)
-    group_t = lax.dynamic_slice_in_dim(feat_t, node_group * blocks_here, blocks_here, 0)
-    sent = jnp.stack([group_t, nm_t], axis=1).reshape(feat_parts, per, 2, cols, block_size)
-    got, w_all = exchange([sent, w_both], [False, True], feat_parts, 0)
+    feat_got, nm_got, w_all, deg_blocks = forward_exchange(
+        ids_flat, nbr_count, feat_t, tiles, w_both, feat_parts
+    )
     w_all = w_all.reshape(feat_parts * cols, 2 * hidden)
     w_self_all = w_all[:, :hidden]
     w_neigh_all = w_all[:, hidden:]
-
-    own = got.transpose(2, 1, 4, 0, 3).reshape(2, own_nodes, feat_parts * cols)
-    own_feat = own[0]
-    own_nm = own[1]
+    own_feat = feat_got.transpose(1, 3, 0, 2).reshape(own_nodes, feat_parts * cols)
+    own_nm = nm_got.transpose(1, 3, 0, 2).reshape(own_nodes, feat_parts * cols)
 
     pre_act = (
         jnp.dot(own_feat, w_self_all, preferred_element_type=jnp.float32)

time: 201 us -> 179 us (0.89)
  Pallas kernels: 88.8 us -> 71.4 us
    pallas_call x2 -> x1, Pallas kernels: 69.8 us -> 52.4 us  [forward_exchange(): pl.pallas_call(functools.partial(forward_exchange_kernel, parts), out_sha...]
  transfers between devices with their start and end apart: 3 -> 3, of which waited for: 2 -> 2; matrix products, arithmetic and copies ran while one was open for 3% -> 3% of each run, Pallas kernels for 10% -> 11%
where the time goes in v7:
time: 179 us; the launch traced here: 178 us
  Pallas kernels  71.4 us (40%)
  waiting for transfers between devices  41.8 us (23%)
  blocking collectives  17.3 us (10%)
  starting transfers between devices  16.5 us (9%)
  between operations  14.2 us (8%)
  local copies, waits for them, and re-layouts  7.18 us (4%)
  other arithmetic  4.96 us (3%)
  matrix products  4.82 us (3%)
    pallas_call x1, Pallas kernels, forward_exchange(): pl.pallas_call(functools.partial(forward_exchange_kernel, parts), out_sha...  52.4 us
    all_to_all x1, waiting for transfers between devices, shards(): lax.all_to_all(part.reshape(feat_parts, cols, 2 * hidden), 'feat', 0, 0,...  27.9 us
    pallas_call x1, Pallas kernels, aggregate_backward(): pl.pallas_call(backward_kernel, grid_spec=pltpu.PrefetchScalarGridSpec(nu...  19 us
    psum x1, blocking collectives, shards(): grads = lax.psum(jnp.sum(part_got, axis=0), 'node')  17.3 us
    all_to_all x1, waiting for transfers between devices, shards(): lax.all_to_all(back, 'feat', 0, 0, tiled=True)  13.9 us
    all_to_all x1, starting transfers between devices, shards(): lax.all_to_all(back, 'feat', 0, 0, tiled=True)  9.51 us
    all_to_all x1, starting transfers between devices, shards(): lax.all_to_all(part.reshape(feat_parts, cols, 2 * hidden), 'feat', 0, 0,...  6.91 us
  transfers between devices with their start and end apart: 3, of which 2 were waited for; matrix products, arithmetic and copies ran while one was open for 3% of the time, Pallas kernels for 11%

profile of v7, /device:TPU:2, one launch (start us, length us, event | category | flops | bytes accessed | tf_op | source)
XLA Modules:
  0.0 178.1 jit_solution(15595120843982322029)
XLA Ops:
  7.2 0.9 copy.16
  8.1 0.7 reshape.50.ids_ref
  8.7 1.2 bitcast_bitcast_fusion.feat_ref
  9.9 0.6 pad_maximum_fusion.1.w_ref
  10.5 52.4 %shard_map.111 = (bf16[64,1,16,128]{3,2,1,0:T(8,128)(2,1)}, bf16[64,1,16,128]{3,2,1,0:T(8,128)(2,1)}, bf16[64,16,512]{2,1,0:T(8,128)(2,1)}, f32[64,1,128]{2,1,0:T(1,128)}) custom-call(s32[1024]{0:T(1024)} %reshape.50.ids_ref, s32[64]{0:T(128)} %cnt_ref.3, bf16[256,16,128]{2,1,0:T(8,128)(2,1)} %bitcast_bitcast_fusion.feat_ref, s32[64,16,8,128]{3,2,1,0:T(8,128)} %tiles_ref.3, ...), custom_call_target="tpu_custom_call" | custom-call | tf_op jit(solution)/shard_map/pallas_call | solution.py:283
  62.9 1.5 fusion.8
  64.4 2.1 %fusion.13 = (bf16[128,256]{1,0:T(8,128)(2,1)S(1)}, bf16[128,256]{1,0:T(8,128)(2,1)}) fusion(bf16[128,256]{1,0:T(8,128)(2,1)S(1)} %copy-done.7, f32[256]{0:T(256)S(1)} %copy-done.8, f32[128,256]{1,0:T(8,128)S(1)} %fusion.8, bf16[128,1024]{0,1:T(8,128)(2,1)} %bitcast.59, bf16[1024,512]{1,0:T(8,128)(2,1)} %bitcast.53), kind=kOutput, calls=%fused_computation.27 | convolution fusion | flops 67469312 | bytes 1115136 | tf_op jit(solution)/shard_map/dot_general | solution.py:329
  66.8 0.7 maximum_bitcast_fusion.1
  67.5 0.3 fusion.2
  67.8 0.8 maximum_bitcast_fusion
  68.7 9.5 %all-to-all-start = ((bf16[64,1,2,16,128]{4,3,2,1,0:T(8,128)(2,1)}), bf16[64,1,2,16,128]{4,3,2,1,0:T(8,128)(2,1)}, u32[]{:S(2)}, u32[]{:S(2)}) async-start(bf16[64,1,2,16,128]{4,3,2,1,0:T(8,128)(2,1)} %maximum_bitcast_fusion), calls=%async_computation | async-start | bytes 1048576 | tf_op jit(solution)/shard_map/all_to_all | solution.py:365
  78.2 0.3 fusion.15
  78.5 0.3 fusion.14
  79.0 1.9 %copy.22 = f32[1024,512]{1,0:T(8,128)} copy(f32[1024,512]{0,1:T(8,128)S(1)} %pad_maximum_fusion) | data formatting | bytes 4194304 | tf_op jit(solution)/shard_map/concatenate | solution.py:347
  80.9 13.9 %all-to-all-done = bf16[64,1,2,16,128]{4,3,2,1,0:T(8,128)(2,1)} async-done(((bf16[64,1,2,16,128]{4,3,2,1,0:T(8,128)(2,1)}), bf16[64,1,2,16,128]{4,3,2,1,0:T(8,128)(2,1)}, u32[]{:S(2)}, u32[]{:S(2)}) %all-to-all-start) | async-done | bytes 524320 | tf_op jit(solution)/shard_map/all_to_all | solution.py:365
  94.8 6.9 %all-to-all-start.1 = ((f32[64,16,512]{2,1,0:T(8,128)}), f32[64,16,512]{2,1,0:T(8,128)S(1)}, u32[]{:S(2)}, u32[]{:S(2)}) async-start(f32[64,16,512]{2,1,0:T(8,128)} %bitcast.18), calls=%async_computation.2 | async-start | bytes 4194304 | tf_op jit(solution)/shard_map/all_to_all | solution.py:354
  101.8 1.1 copy.28
  102.8 0.8 copy-done.1
  103.6 0.7 slice_bitcast_fusion.1.ds_ref
  104.4 19.0 %shard_map.112 = f32[256,16,128]{2,1,0:T(8,128)} custom-call(s32[1024]{0:T(1024)} %reshape.50.ids_ref, s32[64]{0:T(128)} %cnt_ref.3, bf16[64,16,128]{2,1,0:T(8,128)(2,1)} %slice_bitcast_fusion.1.ds_ref, s32[64,16,8,128]{3,2,1,0:T(8,128)} %tiles_ref.3), custom_call_target="tpu_custom_call" | custom-call | tf_op jit(solution)/shard_map/pallas_call | solution.py:109
  123.4 27.9 %all-to-all-done.1 = f32[64,16,512]{2,1,0:T(8,128)S(1)} async-done(((f32[64,16,512]{2,1,0:T(8,128)}), f32[64,16,512]{2,1,0:T(8,128)S(1)}, u32[]{:S(2)}, u32[]{:S(2)}) %all-to-all-start.1) | async-done | bytes 2097184 | tf_op jit(solution)/shard_map/all_to_all | solution.py:354
  151.4 17.3 %psum.7 = f32[16,512]{1,0:T(8,128)S(1)} all-reduce(f32[16,512]{1,0:T(8,128)S(1)} %reduce_sum.9), channel_id=1, replica_groups=mesh['feat'=64,'node'=4] {'node'}, use_global_device_ids=true, to_apply=%region_2.3 | all-reduce | flops 8192 | bytes 65536 | tf_op jit(solution)/shard_map/psum | solution.py:355
  168.7 0.6 slice_multiply_fusion
  169.3 1.9 %copy_bitcast_fusion = f32[8192,16]{0,1:T(8,128)} fusion(f32[64,16,128]{2,1,0:T(8,128)} %reduce-scatter.2.cloned.1.call-done, bf16[64,2,16,128]{3,2,0,1:T(8,128)(2,1)} %bitcast.51), kind=kLoop, calls=%fused_computation.9 | loop fusion | flops 262144 | bytes 1310720 | tf_op jit(solution)/shard_map/reshape | solution.py:372
  (23 shorter events, 0.7 us)
Async XLA Ops:
  7.2 1.6 copy-start
  7.2 2.7 %copy-start.5 = (bf16[16,256]{1,0:T(8,128)(2,1)S(1)}, bf16[16,256]{1,0:T(8,128)(2,1)}, u32[]{:S(2)}) copy-start(bf16[16,256]{1,0:T(8,128)(2,1)} %param.10) | copy-start | bytes 24580
  7.2 2.7 %copy-start.6 = (bf16[16,256]{1,0:T(8,128)(2,1)S(1)}, bf16[16,256]{1,0:T(8,128)(2,1)}, u32[]{:S(2)}) copy-start(bf16[16,256]{1,0:T(8,128)(2,1)} %param.9) | copy-start | bytes 24580
  10.5 53.9 %copy-start.7 = (bf16[128,256]{1,0:T(8,128)(2,1)S(1)}, bf16[128,256]{1,0:T(8,128)(2,1)}, u32[]{:S(2)}) copy-start(bf16[128,256]{1,0:T(8,128)(2,1)} %param.12) | copy-start | bytes 196612
  10.5 53.9 %copy-start.8 = (f32[256]{0:T(256)S(1)}, f32[256]{0:T(256)}, u32[]{:S(2)}) copy-start(f32[256]{0:T(256)} %param.11) | copy-start | bytes 3076
  62.9 3.6 %copy-start.2 = (bf16[64,16,512]{2,1,0:T(8,128)(2,1)S(1)}, bf16[64,16,512]{2,1,0:T(8,128)(2,1)}, u32[]{:S(2)}) copy-start(bf16[64,16,512]{2,1,0:T(8,128)(2,1)} %get-tuple-element.9) | copy-start | bytes 3145732
  67.5 10.7 %copy-start.4 = (bf16[64,1,16,128]{3,2,1,0:T(8,128)(2,1)S(1)}, bf16[64,1,16,128]{3,2,1,0:T(8,128)(2,1)}, u32[]{:S(2)}) copy-start(bf16[64,1,16,128]{3,2,1,0:T(8,128)(2,1)} %get-tuple-element.10) | copy-start | bytes 786436
  67.8 10.7 %copy-start.3 = (bf16[64,1,16,128]{3,2,1,0:T(8,128)(2,1)S(1)}, bf16[64,1,16,128]{3,2,1,0:T(8,128)(2,1)}, u32[]{:S(2)}) copy-start(bf16[64,1,16,128]{3,2,1,0:T(8,128)(2,1)} %get-tuple-element.8) | copy-start | bytes 786436
  68.7 26.1 %all-to-all-start = ((bf16[64,1,2,16,128]{4,3,2,1,0:T(8,128)(2,1)}), bf16[64,1,2,16,128]{4,3,2,1,0:T(8,128)(2,1)}, u32[]{:S(2)}, u32[]{:S(2)}) async-start(bf16[64,1,2,16,128]{4,3,2,1,0:T(8,128)(2,1)} %maximum_bitcast_fusion), calls=%async_computation | async-start | bytes 1048576 | tf_op jit(solution)/shard_map/all_to_all | solution.py:365
  94.8 56.5 %all-to-all-start.1 = ((f32[64,16,512]{2,1,0:T(8,128)}), f32[64,16,512]{2,1,0:T(8,128)S(1)}, u32[]{:S(2)}, u32[]{:S(2)}) async-start(f32[64,16,512]{2,1,0:T(8,128)} %bitcast.18), calls=%async_computation.2 | async-start | bytes 4194304 | tf_op jit(solution)/shard_map/all_to_all | solution.py:354
  101.7 67.6 %reduce-scatter.2.cloned.1.call-start = ((), (), s32[]{:S(2)}) async-start(), calls=%async_computation.3 | async-start | bytes 2621440 | tf_op jit(solution)/shard_map/reduce_scatter | solution.py:370
  102.8 0.8 copy-start.1
Sparse Core Ops, SparseCore 0:
  123.5 33.4 reduce-scatter.1

commit v8 on v7

--- a/solution.py
+++ b/solution.py
@@ -351,20 +351,26 @@
         ],
         axis=1,
     )
-    part_got = lax.all_to_all(part.reshape(feat_parts, cols, 2 * hidden), "feat", 0, 0, tiled=True)
-    grads = lax.psum(jnp.sum(part_got, axis=0), "node")
-    grad_scale = 1.0 / math.sqrt(node_total)
-    grad_self = grads[:, :hidden] * grad_scale
-    grad_neigh = grads[:, hidden:] * grad_scale
-
+    lanes = part.shape[1] // block_size
     back = (
         jnp.stack([d_self_t, d_scaled_t], axis=0)
         .reshape(2, feat_parts, cols, per, block_size)
         .transpose(1, 3, 0, 2, 4)
-    )
-    got_back = lax.all_to_all(back, "feat", 0, 0, tiled=True).reshape(blocks_here, 2, cols, block_size)
-    d_self_blocks = got_back[:, 0]
-    d_scaled_blocks = got_back[:, 1]
+        .reshape(feat_parts, per * 2, cols, block_size)
+        .astype(jnp.float32)
+    )
+    part_tiles = part.reshape(feat_parts, cols, lanes, block_size).transpose(0, 2, 1, 3)
+    got_back = lax.all_to_all(
+        jnp.concatenate([back, part_tiles], axis=1), "feat", 0, 0, tiled=True
+    )
+    d_blocks = got_back[:, : per * 2].astype(jnp.bfloat16).reshape(blocks_here, 2, cols, block_size)
+    d_self_blocks = d_blocks[:, 0]
+    d_scaled_blocks = d_blocks[:, 1]
+    part_sum = jnp.sum(got_back[:, per * 2 :], axis=0).transpose(1, 0, 2).reshape(cols, lanes * block_size)
+    grads = lax.psum(part_sum, "node")
+    grad_scale = 1.0 / math.sqrt(node_total)
+    grad_self = grads[:, :hidden] * grad_scale
+    grad_neigh = grads[:, hidden:] * grad_scale
 
     grad_all = aggregate_backward(ids_flat, nbr_count, d_scaled_blocks, tiles, all_blocks)
     grad_group = lax.psum_scatter(grad_all, "node", scatter_dimension=0, tiled=True)

time: 179 us -> 227 us (1.27)
  blocking collectives: 17.3 us -> 98.9 us
  waiting for transfers between devices: 41.8 us -> 11 us
  starting transfers between devices: 16.5 us -> 0.04 us
  other arithmetic: 4.96 us -> 10 us
  local copies, waits for them, and re-layouts: 7.18 us -> 12.1 us
  matrix products: 4.82 us -> 7.92 us
    all_to_all x0 -> x1, blocking collectives: none -> 81.2 us  [shards(): lax.all_to_all(jnp.concatenate([back, part_tiles], axis=1), 'feat', 0, 0,...]
    all_to_all x2 -> x0, waiting for transfers between devices: 41.8 us -> none  [the longest x1 27.9 us: shards(): lax.all_to_all(part.reshape(feat_parts, cols, 2 * hidden), 'feat', 0, 0,...]
    all_to_all x2 -> x0, starting transfers between devices: 16.4 us -> none  [the longest x1 9.51 us: shards(): lax.all_to_all(back, 'feat', 0, 0, tiled=True)]
    reduce_scatter x1, waiting for transfers between devices: 0.01 us -> 11 us  [shards(): lax.psum_scatter(grad_all, 'node', scatter_dimension=0, tiled=True)]
    convert_element_type x0 -> x1, other arithmetic: none -> 2.42 us  [shards(): back = jnp.stack([d_self_t, d_scaled_t], axis=0).reshape(2, feat_parts, c...]
    another operation x0 -> x2, local copies, waits for them, and re-layouts: none -> 2.41 us  [shards(): jnp.stack([d_self_t, d_scaled_t], axis=0)]
  transfers between devices with their start and end apart: 3 -> 1, of which waited for: 2 -> 1; matrix products, arithmetic and copies ran while one was open for 3% -> 1% of each run, Pallas kernels for 11% -> 0%
where the time goes in v8:
time: 227 us; the launch traced here: 226 us
  blocking collectives  98.9 us (44%)
  Pallas kernels  71.4 us (31%)
  between operations  14.2 us (6%)
  local copies, waits for them, and re-layouts  12.1 us (5%)
  waiting for transfers between devices  11 us (5%)
  other arithmetic  10 us (4%)
  matrix products  7.92 us (3%)
    all_to_all x1, blocking collectives, shards(): lax.all_to_all(jnp.concatenate([back, part_tiles], axis=1), 'feat', 0, 0,...  81.2 us
    pallas_call x1, Pallas kernels, forward_exchange(): pl.pallas_call(functools.partial(forward_exchange_kernel, parts), out_sha...  52.4 us
    pallas_call x1, Pallas kernels, aggregate_backward(): pl.pallas_call(backward_kernel, grid_spec=pltpu.PrefetchScalarGridSpec(nu...  19 us
    psum x1, blocking collectives, shards(): grads = lax.psum(part_sum, 'node')  17.7 us
    reduce_scatter x1, waiting for transfers between devices, shards(): lax.psum_scatter(grad_all, 'node', scatter_dimension=0, tiled=True)  11 us
  transfers between devices with their start and end apart: 1, of which 1 were waited for; matrix products, arithmetic and copies ran while one was open for 1% of the time, Pallas kernels for 0%

profile of v8, /device:TPU:2, one launch (start us, length us, event | category | flops | bytes accessed | tf_op | source)
XLA Modules:
  0.0 225.6 jit_solution(18356034874322526659)
XLA Ops:
  7.2 0.9 copy.26
  8.8 1.2 bitcast_bitcast_fusion.feat_ref
  10.0 1.4 pad_maximum_fusion.2.w_ref
  11.3 52.4 %shard_map.111 = (bf16[64,1,16,128]{3,2,1,0:T(8,128)(2,1)}, bf16[64,1,16,128]{3,2,1,0:T(8,128)(2,1)}, bf16[64,16,512]{2,1,0:T(8,128)(2,1)}, f32[64,1,128]{2,1,0:T(1,128)}) custom-call(s32[1024]{0:T(1024)} %reshape.53.ids_ref, s32[64]{0:T(128)} %cnt_ref.3, bf16[256,16,128]{2,1,0:T(8,128)(2,1)} %bitcast_bitcast_fusion.feat_ref, s32[64,16,8,128]{3,2,1,0:T(8,128)} %tiles_ref.3, ...), custom_call_target="tpu_custom_call" | custom-call | tf_op jit(solution)/shard_map/pallas_call | solution.py:283
  63.8 1.5 fusion.8
  65.3 2.1 fusion.13
  67.4 1.3 convolution_convert_fusion.1
  68.7 1.4 fusion.15
  70.1 1.3 fusion.14
  71.4 0.8 maximum_bitcast_fusion
  72.5 1.2 copy.29
  73.7 1.2 copy.28
  75.1 1.9 copy.30
  77.0 1.9 reshape.58
  78.9 2.4 %convert_bitcast_fusion = f32[64,2,16,128]{3,1,2,0:T(2,128)S(1)} fusion(bf16[1,64,16,1,128]{4,0,2,1,3:T(2,128)(2,1)} %copy.29, bf16[1,64,16,1,128]{4,0,2,1,3:T(2,128)(2,1)} %copy.28), kind=kLoop, calls=%fused_computation.12 | loop fusion | flops 1048576 | bytes 1572864 | tf_op jit(solution)/shard_map/convert_element_type | solution.py:360
  81.3 0.9 pad_maximum_fusion
  82.9 81.2 %all_to_all.5 = f32[64,6,16,128]{3,2,1,0:T(8,128)S(1)} all-to-all(f32[64,6,16,128]{3,2,1,0:T(8,128)S(1)} %copy.31), channel_id=1, replica_groups=mesh['feat'=64,'node'=4] {'feat'}, dimensions={0} | all-to-all | bytes 6291456 | tf_op jit(solution)/shard_map/all_to_all | solution.py:363
  164.1 1.6 copy-done.1
  165.8 0.8 slice_bitcast_fusion.1.ds_ref
  166.5 19.0 %shard_map.112 = f32[256,16,128]{2,1,0:T(8,128)} custom-call(s32[1024]{0:T(1024)} %reshape.53.ids_ref, s32[64]{0:T(128)} %cnt_ref.3, bf16[64,16,128]{2,1,0:T(8,128)(2,1)} %slice_bitcast_fusion.1.ds_ref, s32[64,16,8,128]{3,2,1,0:T(8,128)} %tiles_ref.3), custom_call_target="tpu_custom_call" | custom-call | tf_op jit(solution)/shard_map/pallas_call | solution.py:109
  185.6 1.7 slice_reduce_fusion
  187.3 17.7 %psum.7 = f32[16,512]{1,0:T(8,128)S(1)} all-reduce(f32[16,512]{1,0:T(8,128)S(1)} %copy_bitcast_fusion.1), channel_id=1, replica_groups=mesh['feat'=64,'node'=4] {'node'}, use_global_device_ids=true, to_apply=%region_2.3 | all-reduce | flops 8192 | bytes 65536 | tf_op jit(solution)/shard_map/psum | solution.py:370
  205.7 11.0 %reduce-scatter.2.cloned.1.call-done = f32[64,16,128]{2,1,0:T(8,128)} async-done(((f32[256,16,128]{2,1,0:T(8,128)}), f32[64,16,128]{2,1,0:T(8,128)}) %reduce-scatter.2.cloned.1.call-update) | async-done | bytes 524304 | tf_op jit(solution)/shard_map/reduce_scatter | solution.py:376
  216.7 2.1 copy_bitcast_fusion
  (25 shorter events, 2.5 us)
Async XLA Ops:
  7.2 1.6 copy-start
  7.2 209.5 %reduce-scatter.2.cloned.1.call-start = ((), (), s32[]{:S(2)}) async-start(), calls=%async_computation.2 | async-start | bytes 2621440 | tf_op jit(solution)/shard_map/reduce_scatter | solution.py:376
  10.0 55.3 %copy-start.7 = (bf16[128,256]{1,0:T(8,128)(2,1)S(1)}, bf16[128,256]{1,0:T(8,128)(2,1)}, u32[]{:S(2)}) copy-start(bf16[128,256]{1,0:T(8,128)(2,1)} %param.12) | copy-start | bytes 196612
  10.0 55.3 %copy-start.8 = (f32[256]{0:T(256)S(1)}, f32[256]{0:T(256)}, u32[]{:S(2)}) copy-start(f32[256]{0:T(256)} %param.11) | copy-start | bytes 3076
  63.7 5.0 %copy-start.6 = (bf16[64,1,16,128]{3,2,1,0:T(8,128)(2,1)S(1)}, bf16[64,1,16,128]{3,2,1,0:T(8,128)(2,1)}, u32[]{:S(2)}) copy-start(bf16[64,1,16,128]{3,2,1,0:T(8,128)(2,1)} %get-tuple-element.10) | copy-start | bytes 786436
  63.7 6.4 %copy-start.5 = (bf16[64,1,16,128]{3,2,1,0:T(8,128)(2,1)S(1)}, bf16[64,1,16,128]{3,2,1,0:T(8,128)(2,1)}, u32[]{:S(2)}) copy-start(bf16[64,1,16,128]{3,2,1,0:T(8,128)(2,1)} %get-tuple-element.8) | copy-start | bytes 786436
  63.7 8.5 %copy-start.4 = (bf16[64,16,512]{2,1,0:T(8,128)(2,1)S(1)}, bf16[64,16,512]{2,1,0:T(8,128)(2,1)}, u32[]{:S(2)}) copy-start(bf16[64,16,512]{2,1,0:T(8,128)(2,1)} %get-tuple-element.9) | copy-start | bytes 3145732
  71.4 3.5 %copy-start.2 = (f32[1024,256]{0,1:T(8,128)S(1)}, f32[1024,256]{0,1:T(8,128)}, u32[]{:S(2)}) copy-start(f32[1024,256]{0,1:T(8,128)} %fusion.15) | copy-start | bytes 3145732
  71.4 3.5 %copy-start.3 = (f32[1024,256]{0,1:T(8,128)S(1)}, f32[1024,256]{0,1:T(8,128)}, u32[]{:S(2)}) copy-start(f32[1024,256]{0,1:T(8,128)} %fusion.14) | copy-start | bytes 3145732
  164.1 1.7 copy-start.1
Sparse Core Ops, SparseCore 0:
  185.7 30.9 reduce-scatter.1

commit v9 on v7

--- a/solution.py
+++ b/solution.py
@@ -208,30 +208,42 @@
     lax.fori_loop(1, parts, greet, 0)
     pl.semaphore_wait(barrier, parts - 1)
 
+    half = parts // 2
+    par = lax.rem(me, 2)
+    sibling = me + 1 - 2 * par
+
     def copy(i, k):
-        peer = lax.rem(me + k, parts)
         if i == 0:
-            src, dst = w_ref, w_out
+            peer = lax.rem(me + 2 * k, parts)
+            src, dst = w_ref, w_out.at[par, me // 2]
         elif i == 1:
-            src, dst = feat_ref.at[pl.ds(group * blocks_here + peer * per, per)], feat_out
+            peer = lax.rem(me + k, parts)
+            src = feat_ref.at[pl.ds(group * blocks_here + peer * per, per)]
+            dst = feat_out.at[me]
         else:
-            src, dst = nm_scr.at[pl.ds(peer * per, per)], nm_out
+            peer = lax.rem(me + k, parts)
+            src, dst = nm_scr.at[pl.ds(peer * per, per)], nm_out.at[me]
         return pltpu.make_async_remote_copy(
             src_ref=src,
-            dst_ref=dst.at[me],
+            dst_ref=dst,
             send_sem=send_sems.at[i, k],
             recv_sem=recv_sems.at[i, k],
             device_id={"feat": peer},
             device_id_type=mesh_id,
         )
 
-    def start_inputs(k, carry):
+    def start_weights(k, carry):
         copy(0, k).start()
+        return carry
+
+    def start_feat(k, carry):
         copy(1, k).start()
         return carry
 
-    lax.fori_loop(1, parts, start_inputs, 0)
-    w_out[me] = w_ref[...]
+    lax.fori_loop(1, half, start_weights, 0)
+    lax.fori_loop(1, parts, start_feat, 0)
+    own_w = pltpu.make_async_copy(w_ref, w_out.at[par, me // 2], send_sems.at[3, 0])
+    own_w.start()
     feat_out[me] = feat_ref[pl.ds(group * blocks_here + me * per, per)]
 
     def row(b, carry):
@@ -259,6 +271,22 @@
 
     lax.fori_loop(0, blocks_here, row, 0)
 
+    def finish_weights(k, carry):
+        copy(0, k).wait()
+        return carry
+
+    lax.fori_loop(1, half, finish_weights, 0)
+    own_w.wait()
+    to_sibling = pltpu.make_async_remote_copy(
+        src_ref=w_out.at[par],
+        dst_ref=w_out.at[par],
+        send_sem=send_sems.at[3, 1],
+        recv_sem=recv_sems.at[3, 1],
+        device_id={"feat": sibling},
+        device_id_type=mesh_id,
+    )
+    to_sibling.start()
+
     def start_result(k, carry):
         copy(2, k).start()
         return carry
@@ -267,11 +295,12 @@
     nm_out[me] = nm_scr[pl.ds(me * per, per)]
 
     def finish(k, carry):
-        for i in range(3):
-            copy(i, k).wait()
+        copy(1, k).wait()
+        copy(2, k).wait()
         return carry
 
     lax.fori_loop(1, parts, finish, 0)
+    to_sibling.wait()
 
 
 def forward_exchange(ids_flat, counts, feat_t, tiles, w_both, parts):
@@ -285,15 +314,15 @@
         out_shape=[
             jax.ShapeDtypeStruct((parts, per, cols, width), jnp.bfloat16),
             jax.ShapeDtypeStruct((parts, per, cols, width), jnp.bfloat16),
-            jax.ShapeDtypeStruct((parts,) + w_both.shape, w_both.dtype),
+            jax.ShapeDtypeStruct((2, parts // 2) + w_both.shape, w_both.dtype),
             jax.ShapeDtypeStruct((blocks_here, 1, width), jnp.float32),
         ],
         in_specs=[smem, smem, vmem, vmem, vmem],
         out_specs=[vmem] * 4,
         scratch_shapes=[
             pltpu.VMEM((blocks_here, cols, width), jnp.bfloat16),
-            pltpu.SemaphoreType.DMA((3, parts)),
-            pltpu.SemaphoreType.DMA((3, parts)),
+            pltpu.SemaphoreType.DMA((4, parts)),
+            pltpu.SemaphoreType.DMA((4, parts)),
         ],
         compiler_params=pltpu.CompilerParams(collective_id=0, has_side_effects=True),
     )(ids_flat, counts, feat_t, tiles, w_both)
@@ -318,7 +347,7 @@
     feat_got, nm_got, w_all, deg_blocks = forward_exchange(
         ids_flat, nbr_count, feat_t, tiles, w_both, feat_parts
     )
-    w_all = w_all.reshape(feat_parts * cols, 2 * hidden)
+    w_all = w_all.transpose(1, 0, 2, 3).reshape(feat_parts * cols, 2 * hidden)
     w_self_all = w_all[:, :hidden]
     w_neigh_all = w_all[:, hidden:]
     own_feat = feat_got.transpose(1, 3, 0, 2).reshape(own_nodes, feat_parts * cols)

time: 179 us -> 170 us (0.950)
  Pallas kernels: 71.4 us -> 63.7 us
  matrix products: 4.82 us -> 2.47 us
    pallas_call x1, Pallas kernels: 52.4 us -> 44.7 us  [forward_exchange(): pl.pallas_call(functools.partial(forward_exchange_kernel, parts), out_sha...]
where the time goes in v9:
time: 170 us; the launch traced here: 169 us
  Pallas kernels  63.7 us (37%)
  waiting for transfers between devices  41.8 us (25%)
  blocking collectives  17.4 us (10%)
  starting transfers between devices  16.4 us (10%)
  between operations  14.2 us (8%)
  local copies, waits for them, and re-layouts  8.54 us (5%)
  other arithmetic  4.89 us (3%)
  matrix products  2.47 us (1%)
    pallas_call x1, Pallas kernels, forward_exchange(): pl.pallas_call(functools.partial(forward_exchange_kernel, parts), out_sha...  44.7 us
    all_to_all x1, waiting for transfers between devices, shards(): lax.all_to_all(part.reshape(feat_parts, cols, 2 * hidden), 'feat', 0, 0,...  27.9 us
    pallas_call x1, Pallas kernels, aggregate_backward(): pl.pallas_call(backward_kernel, grid_spec=pltpu.PrefetchScalarGridSpec(nu...  19 us
    psum x1, blocking collectives, shards(): grads = lax.psum(jnp.sum(part_got, axis=0), 'node')  17.4 us
    all_to_all x1, waiting for transfers between devices, shards(): lax.all_to_all(back, 'feat', 0, 0, tiled=True)  13.9 us
    all_to_all x1, starting transfers between devices, shards(): lax.all_to_all(back, 'feat', 0, 0, tiled=True)  9.46 us
    all_to_all x1, starting transfers between devices, shards(): lax.all_to_all(part.reshape(feat_parts, cols, 2 * hidden), 'feat', 0, 0,...  6.91 us
  transfers between devices with their start and end apart: 3, of which 2 were waited for; matrix products, arithmetic and copies ran while one was open for 3% of the time, Pallas kernels for 11%

profile of v9, /device:TPU:2, one launch (start us, length us, event | category | flops | bytes accessed | tf_op | source)
XLA Modules:
  0.0 169.4 jit_solution(5310815912161315391)
XLA Ops:
  7.2 0.9 copy.17
  8.1 0.7 reshape.50.ids_ref
  8.7 1.1 bitcast_bitcast_fusion.feat_ref
  9.9 0.6 pad_maximum_fusion.1.w_ref
  10.5 44.7 %shard_map.111 = (bf16[64,1,16,128]{3,2,1,0:T(8,128)(2,1)}, bf16[64,1,16,128]{3,2,1,0:T(8,128)(2,1)}, bf16[2,32,16,512]{3,2,1,0:T(8,128)(2,1)}, f32[64,1,128]{2,1,0:T(1,128)}) custom-call(s32[1024]{0:T(1024)} %reshape.50.ids_ref, s32[64]{0:T(128)} %cnt_ref.3, bf16[256,16,128]{2,1,0:T(8,128)(2,1)} %bitcast_bitcast_fusion.feat_ref, ...), custom_call_target="tpu_custom_call" | custom-call | tf_op jit(solution)/shard_map/pallas_call | solution.py:312
  55.3 1.4 copy.19
  57.0 1.0 fusion.13
  58.2 0.6 maximum_bitcast_fusion.1
  58.8 0.3 fusion.2
  59.1 0.8 maximum_bitcast_fusion
  60.0 9.5 %all-to-all-start = ((bf16[64,1,2,16,128]{4,3,2,1,0:T(8,128)(2,1)}), bf16[64,1,2,16,128]{4,3,2,1,0:T(8,128)(2,1)}, u32[]{:S(2)}, u32[]{:S(2)}) async-start(bf16[64,1,2,16,128]{4,3,2,1,0:T(8,128)(2,1)} %maximum_bitcast_fusion), calls=%async_computation | async-start | bytes 1048576 | tf_op jit(solution)/shard_map/all_to_all | solution.py:394
  69.4 0.3 fusion.15
  69.8 0.3 fusion.14
  70.3 1.9 %copy.24 = f32[1024,512]{1,0:T(8,128)} copy(f32[1024,512]{0,1:T(8,128)S(1)} %pad_maximum_fusion) | data formatting | bytes 4194304 | tf_op jit(solution)/shard_map/concatenate | solution.py:376
  72.1 13.9 %all-to-all-done = bf16[64,1,2,16,128]{4,3,2,1,0:T(8,128)(2,1)} async-done(((bf16[64,1,2,16,128]{4,3,2,1,0:T(8,128)(2,1)}), bf16[64,1,2,16,128]{4,3,2,1,0:T(8,128)(2,1)}, u32[]{:S(2)}, u32[]{:S(2)}) %all-to-all-start) | async-done | bytes 524320 | tf_op jit(solution)/shard_map/all_to_all | solution.py:394
  86.0 6.9 %all-to-all-start.1 = ((f32[64,16,512]{2,1,0:T(8,128)}), f32[64,16,512]{2,1,0:T(8,128)S(1)}, u32[]{:S(2)}, u32[]{:S(2)}) async-start(f32[64,16,512]{2,1,0:T(8,128)} %bitcast.19), calls=%async_computation.2 | async-start | bytes 4194304 | tf_op jit(solution)/shard_map/all_to_all | solution.py:383
  93.0 1.1 copy.30
  94.1 0.8 copy-done.1
  94.9 0.7 slice_bitcast_fusion.1.ds_ref
  95.6 19.0 %shard_map.112 = f32[256,16,128]{2,1,0:T(8,128)} custom-call(s32[1024]{0:T(1024)} %reshape.50.ids_ref, s32[64]{0:T(128)} %cnt_ref.3, bf16[64,16,128]{2,1,0:T(8,128)(2,1)} %slice_bitcast_fusion.1.ds_ref, s32[64,16,8,128]{3,2,1,0:T(8,128)} %tiles_ref.3), custom_call_target="tpu_custom_call" | custom-call | tf_op jit(solution)/shard_map/pallas_call | solution.py:109
  114.7 27.9 %all-to-all-done.1 = f32[64,16,512]{2,1,0:T(8,128)S(1)} async-done(((f32[64,16,512]{2,1,0:T(8,128)}), f32[64,16,512]{2,1,0:T(8,128)S(1)}, u32[]{:S(2)}, u32[]{:S(2)}) %all-to-all-start.1) | async-done | bytes 2097184 | tf_op jit(solution)/shard_map/all_to_all | solution.py:383
  142.6 17.4 %psum.7 = f32[16,512]{1,0:T(8,128)S(1)} all-reduce(f32[16,512]{1,0:T(8,128)S(1)} %reduce_sum.9), channel_id=1, replica_groups=mesh['feat'=64,'node'=4] {'node'}, use_global_device_ids=true, to_apply=%region_2.3 | all-reduce | flops 8192 | bytes 65536 | tf_op jit(solution)/shard_map/psum | solution.py:384
  160.0 0.6 slice_multiply_fusion
  160.6 1.9 %copy_bitcast_fusion = f32[8192,16]{0,1:T(8,128)} fusion(f32[64,16,128]{2,1,0:T(8,128)} %reduce-scatter.2.cloned.1.call-done, bf16[64,2,16,128]{3,2,0,1:T(8,128)(2,1)} %bitcast.56), kind=kLoop, calls=%fused_computation.9 | loop fusion | flops 262144 | bytes 1310720 | tf_op jit(solution)/shard_map/reshape | solution.py:401
  (22 shorter events, 0.9 us)
Async XLA Ops:
  7.2 1.6 copy-start
  7.2 2.7 %copy-start.4 = (bf16[16,256]{1,0:T(8,128)(2,1)S(1)}, bf16[16,256]{1,0:T(8,128)(2,1)}, u32[]{:S(2)}) copy-start(bf16[16,256]{1,0:T(8,128)(2,1)} %param.10) | copy-start | bytes 24580
  7.2 2.7 %copy-start.5 = (bf16[16,256]{1,0:T(8,128)(2,1)S(1)}, bf16[16,256]{1,0:T(8,128)(2,1)}, u32[]{:S(2)}) copy-start(bf16[16,256]{1,0:T(8,128)(2,1)} %param.9) | copy-start | bytes 24580
  55.2 1.4 copy-start.2
  55.2 1.7 %copy-start.3 = (bf16[64,1,16,128]{3,2,1,0:T(8,128)(2,1)S(1)}, bf16[64,1,16,128]{3,2,1,0:T(8,128)(2,1)}, u32[]{:S(2)}) copy-start(bf16[64,1,16,128]{3,2,1,0:T(8,128)(2,1)} %get-tuple-element.10) | copy-start | bytes 786436
  55.3 1.7 %copy-start.6 = (bf16[128,256]{1,0:T(8,128)(2,1)S(1)}, bf16[128,256]{1,0:T(8,128)(2,1)}, u32[]{:S(2)}) copy-start(bf16[128,256]{1,0:T(8,128)(2,1)} %param.12) | copy-start | bytes 196612
  55.3 1.7 %copy-start.7 = (f32[256]{0:T(256)S(1)}, f32[256]{0:T(256)}, u32[]{:S(2)}) copy-start(f32[256]{0:T(256)} %param.11) | copy-start | bytes 3076
  60.0 26.1 %all-to-all-start = ((bf16[64,1,2,16,128]{4,3,2,1,0:T(8,128)(2,1)}), bf16[64,1,2,16,128]{4,3,2,1,0:T(8,128)(2,1)}, u32[]{:S(2)}, u32[]{:S(2)}) async-start(bf16[64,1,2,16,128]{4,3,2,1,0:T(8,128)(2,1)} %maximum_bitcast_fusion), calls=%async_computation | async-start | bytes 1048576 | tf_op jit(solution)/shard_map/all_to_all | solution.py:394
  86.0 56.5 %all-to-all-start.1 = ((f32[64,16,512]{2,1,0:T(8,128)}), f32[64,16,512]{2,1,0:T(8,128)S(1)}, u32[]{:S(2)}, u32[]{:S(2)}) async-start(f32[64,16,512]{2,1,0:T(8,128)} %bitcast.19), calls=%async_computation.2 | async-start | bytes 4194304 | tf_op jit(solution)/shard_map/all_to_all | solution.py:383
  93.0 67.7 %reduce-scatter.2.cloned.1.call-start = ((), (), s32[]{:S(2)}) async-start(), calls=%async_computation.3 | async-start | bytes 2621440 | tf_op jit(solution)/shard_map/reduce_scatter | solution.py:399
  94.1 0.8 copy-start.1
Sparse Core Ops, SparseCore 0:
  114.8 33.5 reduce-scatter.1

commit v10 on v9

--- a/solution.py
+++ b/solution.py
@@ -391,7 +391,8 @@
         .reshape(2, feat_parts, cols, per, block_size)
         .transpose(1, 3, 0, 2, 4)
     )
-    got_back = lax.all_to_all(back, "feat", 0, 0, tiled=True).reshape(blocks_here, 2, cols, block_size)
+    (got_back,) = exchange([back], [False], feat_parts, 1)
+    got_back = got_back.reshape(blocks_here, 2, cols, block_size)
     d_self_blocks = got_back[:, 0]
     d_scaled_blocks = got_back[:, 1]
 

time: 170 us -> 197 us (1.16)
  Pallas kernels: 63.7 us -> 123 us
  waiting for transfers between devices: 41.8 us -> 12 us
  starting transfers between devices: 16.4 us -> 9.29 us
  matrix products: 2.47 us -> 4.56 us
    pallas_call x0 -> x1, Pallas kernels: none -> 59.5 us  [exchange(): pl.pallas_call(functools.partial(exchange_kernel, parts, tuple(kinds)), o...]
    all_to_all x1, waiting for transfers between devices: 27.9 us -> 0.01 us  [shards(): lax.all_to_all(part.reshape(feat_parts, cols, 2 * hidden), 'feat', 0, 0,...]
    all_to_all x1 -> x0, waiting for transfers between devices: 13.9 us -> none  [shards(): lax.all_to_all(back, 'feat', 0, 0, tiled=True)]
    reduce_scatter x1, waiting for transfers between devices: 0.01 us -> 11.9 us  [shards(): lax.psum_scatter(grad_all, 'node', scatter_dimension=0, tiled=True)]
    all_to_all x1 -> x0, starting transfers between devices: 9.46 us -> none  [shards(): lax.all_to_all(back, 'feat', 0, 0, tiled=True)]
    all_to_all x1, starting transfers between devices: 6.91 us -> 9.24 us  [shards(): lax.all_to_all(part.reshape(feat_parts, cols, 2 * hidden), 'feat', 0, 0,...]
  transfers between devices with their start and end apart: 3 -> 2, of which waited for: 2 -> 1; matrix products, arithmetic and copies ran while one was open for 3% -> 4% of each run, Pallas kernels for 11% -> 40%
where the time goes in v10:
time: 197 us; the launch traced here: 195 us
  Pallas kernels  123 us (62%)
  blocking collectives  17.5 us (9%)
  between operations  14.2 us (7%)
  waiting for transfers between devices  12 us (6%)
  local copies, waits for them, and re-layouts  9.51 us (5%)
  starting transfers between devices  9.29 us (5%)
  other arithmetic  4.92 us (2%)
  matrix products  4.56 us (2%)
    pallas_call x1, Pallas kernels, exchange(): pl.pallas_call(functools.partial(exchange_kernel, parts, tuple(kinds)), o...  59.5 us
    pallas_call x1, Pallas kernels, forward_exchange(): pl.pallas_call(functools.partial(forward_exchange_kernel, parts), out_sha...  44.7 us
    pallas_call x1, Pallas kernels, aggregate_backward(): pl.pallas_call(backward_kernel, grid_spec=pltpu.PrefetchScalarGridSpec(nu...  19 us
    psum x1, blocking collectives, shards(): grads = lax.psum(jnp.sum(part_got, axis=0), 'node')  17.5 us
    reduce_scatter x1, waiting for transfers between devices, shards(): lax.psum_scatter(grad_all, 'node', scatter_dimension=0, tiled=True)  11.9 us
    all_to_all x1, starting transfers between devices, shards(): lax.all_to_all(part.reshape(feat_parts, cols, 2 * hidden), 'feat', 0, 0,...  9.24 us
  transfers between devices with their start and end apart: 2, of which 1 were waited for; matrix products, arithmetic and copies ran while one was open for 4% of the time, Pallas kernels for 40%

profile of v10, /device:TPU:2, one launch (start us, length us, event | category | flops | bytes accessed | tf_op | source)
XLA Modules:
  0.0 195.2 jit_solution(8873657033381485318)
XLA Ops:
  7.2 0.9 copy.13
  8.1 0.7 reshape.50.ids_ref
  8.7 1.1 bitcast_bitcast_fusion.feat_ref
  9.9 0.6 pad_maximum_fusion.1.w_ref
  10.5 44.7 %shard_map.111 = (bf16[64,1,16,128]{3,2,1,0:T(8,128)(2,1)}, bf16[64,1,16,128]{3,2,1,0:T(8,128)(2,1)}, bf16[2,32,16,512]{3,2,1,0:T(8,128)(2,1)}, f32[64,1,128]{2,1,0:T(1,128)}) custom-call(s32[1024]{0:T(1024)} %reshape.50.ids_ref, s32[64]{0:T(128)} %cnt_ref.3, bf16[256,16,128]{2,1,0:T(8,128)(2,1)} %bitcast_bitcast_fusion.feat_ref, ...), custom_call_target="tpu_custom_call" | custom-call | tf_op jit(solution)/shard_map/pallas_call | solution.py:312
  55.3 1.4 copy.15
  56.7 0.3 fusion.8
  57.0 1.0 fusion.13
  57.9 0.3 fusion.15
  58.3 0.3 fusion.14
  58.8 1.9 copy.18
  60.6 9.2 %all-to-all-start = ((f32[64,16,512]{2,1,0:T(8,128)}), f32[64,16,512]{2,1,0:T(8,128)S(1)}, u32[]{:S(2)}, u32[]{:S(2)}) async-start(f32[64,16,512]{2,1,0:T(8,128)} %bitcast.47), calls=%async_computation.1 | async-start | bytes 4194304 | tf_op jit(solution)/shard_map/all_to_all | solution.py:383
  69.9 1.3 convolution_convert_fusion.1
  71.3 0.6 maximum_bitcast_fusion.1
  71.9 1.3 fusion.2
  73.3 0.8 maximum_bitcast_fusion.refs_0_
  74.1 59.5 %shard_map.112 = bf16[64,1,2,16,128]{4,3,2,1,0:T(8,128)(2,1)} custom-call(bf16[64,1,2,16,128]{4,3,2,1,0:T(8,128)(2,1)} %maximum_bitcast_fusion.refs_0_), custom_call_target="tpu_custom_call" | custom-call | tf_op jit(solution)/shard_map/pallas_call | solution.py:177
  133.6 1.9 copy.24
  135.5 1.7 slice_bitcast_fusion.1.ds_ref
  137.1 19.0 %shard_map.113 = f32[256,16,128]{2,1,0:T(8,128)} custom-call(s32[1024]{0:T(1024)} %reshape.50.ids_ref, s32[64]{0:T(128)} %cnt_ref.3, bf16[64,16,128]{2,1,0:T(8,128)(2,1)} %slice_bitcast_fusion.1.ds_ref, s32[64,16,8,128]{3,2,1,0:T(8,128)} %tiles_ref.3), custom_call_target="tpu_custom_call" | custom-call | tf_op jit(solution)/shard_map/pallas_call | solution.py:109
  156.3 17.5 %psum.7 = f32[16,512]{1,0:T(8,128)S(1)} all-reduce(f32[16,512]{1,0:T(8,128)S(1)} %reduce_sum.9), channel_id=1, replica_groups=mesh['feat'=64,'node'=4] {'node'}, use_global_device_ids=true, to_apply=%region_2.3 | all-reduce | flops 8192 | bytes 65536 | tf_op jit(solution)/shard_map/psum | solution.py:384
  173.9 0.6 slice_multiply_fusion
  174.5 11.9 %reduce-scatter.2.cloned.1.call-done = f32[64,16,128]{2,1,0:T(8,128)} async-done(((f32[256,16,128]{2,1,0:T(8,128)}), f32[64,16,128]{2,1,0:T(8,128)}) %reduce-scatter.2.cloned.1.call-update) | async-done | bytes 524304 | tf_op jit(solution)/shard_map/reduce_scatter | solution.py:400
  186.4 1.9 copy_bitcast_fusion
  (21 shorter events, 0.4 us)
Async XLA Ops:
  7.2 1.6 copy-start
  7.2 2.7 %copy-start.4 = (bf16[16,256]{1,0:T(8,128)(2,1)S(1)}, bf16[16,256]{1,0:T(8,128)(2,1)}, u32[]{:S(2)}) copy-start(bf16[16,256]{1,0:T(8,128)(2,1)} %param.10) | copy-start | bytes 24580
  7.2 2.7 %copy-start.5 = (bf16[16,256]{1,0:T(8,128)(2,1)S(1)}, bf16[16,256]{1,0:T(8,128)(2,1)}, u32[]{:S(2)}) copy-start(bf16[16,256]{1,0:T(8,128)(2,1)} %param.9) | copy-start | bytes 24580
  55.2 1.4 copy-start.2
  55.2 1.7 copy-start.3
  55.2 1.7 copy-start.6
  55.3 1.7 copy-start.7
  56.6 1.6 copy-start.1
  60.6 95.5 %all-to-all-start = ((f32[64,16,512]{2,1,0:T(8,128)}), f32[64,16,512]{2,1,0:T(8,128)S(1)}, u32[]{:S(2)}, u32[]{:S(2)}) async-start(f32[64,16,512]{2,1,0:T(8,128)} %bitcast.47), calls=%async_computation.1 | async-start | bytes 4194304 | tf_op jit(solution)/shard_map/all_to_all | solution.py:383
  69.9 116.5 %reduce-scatter.2.cloned.1.call-start = ((), (), s32[]{:S(2)}) async-start(), calls=%async_computation.2 | async-start | bytes 2621440 | tf_op jit(solution)/shard_map/reduce_scatter | solution.py:400
Sparse Core Ops, SparseCore 0:
  156.3 30.0 reduce-scatter.1

commit v11 on v9

--- a/solution.py
+++ b/solution.py
@@ -8,7 +8,7 @@
 from jax.experimental.pallas import tpu as pltpu
 from jax.sharding import PartitionSpec as P
 
-ROWS_PER_STEP = 8
+ROWS_PER_STEP = 16
 
 
 def unpack_tile(words):

time: 170 us -> 170 us (level)
  no operation moved by 1% of the time
where the time goes in v11:
time: 170 us; the launch traced here: 169 us
  Pallas kernels  63.9 us (38%)
  waiting for transfers between devices  41.7 us (25%)
  blocking collectives  17.3 us (10%)
  starting transfers between devices  16.4 us (10%)
  between operations  14.2 us (8%)
  local copies, waits for them, and re-layouts  8.54 us (5%)
  other arithmetic  4.89 us (3%)
  matrix products  2.49 us (1%)
    pallas_call x1, Pallas kernels, forward_exchange(): pl.pallas_call(functools.partial(forward_exchange_kernel, parts), out_sha...  44.7 us
    all_to_all x1, waiting for transfers between devices, shards(): lax.all_to_all(part.reshape(feat_parts, cols, 2 * hidden), 'feat', 0, 0,...  27.7 us
    pallas_call x1, Pallas kernels, aggregate_backward(): pl.pallas_call(backward_kernel, grid_spec=pltpu.PrefetchScalarGridSpec(nu...  19.1 us
    psum x1, blocking collectives, shards(): grads = lax.psum(jnp.sum(part_got, axis=0), 'node')  17.3 us
    all_to_all x1, waiting for transfers between devices, shards(): lax.all_to_all(back, 'feat', 0, 0, tiled=True)  13.9 us
    all_to_all x1, starting transfers between devices, shards(): lax.all_to_all(back, 'feat', 0, 0, tiled=True)  9.46 us
    all_to_all x1, starting transfers between devices, shards(): lax.all_to_all(part.reshape(feat_parts, cols, 2 * hidden), 'feat', 0, 0,...  6.91 us
  transfers between devices with their start and end apart: 3, of which 2 were waited for; matrix products, arithmetic and copies ran while one was open for 3% of the time, Pallas kernels for 11%

profile of v11, /device:TPU:2, one launch (start us, length us, event | category | flops | bytes accessed | tf_op | source)
XLA Modules:
  0.0 169.4 jit_solution(2060339110320178694)
XLA Ops:
  7.2 0.9 copy.17
  8.1 0.7 reshape.50.ids_ref
  8.7 1.1 bitcast_bitcast_fusion.feat_ref
  9.9 0.6 pad_maximum_fusion.1.w_ref
  10.5 44.7 %shard_map.111 = (bf16[64,1,16,128]{3,2,1,0:T(8,128)(2,1)}, bf16[64,1,16,128]{3,2,1,0:T(8,128)(2,1)}, bf16[2,32,16,512]{3,2,1,0:T(8,128)(2,1)}, f32[64,1,128]{2,1,0:T(1,128)}) custom-call(s32[1024]{0:T(1024)} %reshape.50.ids_ref, s32[64]{0:T(128)} %cnt_ref.3, bf16[256,16,128]{2,1,0:T(8,128)(2,1)} %bitcast_bitcast_fusion.feat_ref, ...), custom_call_target="tpu_custom_call" | custom-call | tf_op jit(solution)/shard_map/pallas_call | solution.py:312
  55.3 1.4 copy.19
  57.0 1.0 fusion.13
  58.2 0.6 maximum_bitcast_fusion.1
  58.8 0.3 fusion.2
  59.1 0.8 maximum_bitcast_fusion
  60.0 9.5 %all-to-all-start = ((bf16[64,1,2,16,128]{4,3,2,1,0:T(8,128)(2,1)}), bf16[64,1,2,16,128]{4,3,2,1,0:T(8,128)(2,1)}, u32[]{:S(2)}, u32[]{:S(2)}) async-start(bf16[64,1,2,16,128]{4,3,2,1,0:T(8,128)(2,1)} %maximum_bitcast_fusion), calls=%async_computation | async-start | bytes 1048576 | tf_op jit(solution)/shard_map/all_to_all | solution.py:394
  69.5 0.3 fusion.15
  69.8 0.3 fusion.14
  70.3 1.9 %copy.24 = f32[1024,512]{1,0:T(8,128)} copy(f32[1024,512]{0,1:T(8,128)S(1)} %pad_maximum_fusion) | data formatting | bytes 4194304 | tf_op jit(solution)/shard_map/concatenate | solution.py:376
  72.1 13.9 %all-to-all-done = bf16[64,1,2,16,128]{4,3,2,1,0:T(8,128)(2,1)} async-done(((bf16[64,1,2,16,128]{4,3,2,1,0:T(8,128)(2,1)}), bf16[64,1,2,16,128]{4,3,2,1,0:T(8,128)(2,1)}, u32[]{:S(2)}, u32[]{:S(2)}) %all-to-all-start) | async-done | bytes 524320 | tf_op jit(solution)/shard_map/all_to_all | solution.py:394
  86.1 6.9 %all-to-all-start.1 = ((f32[64,16,512]{2,1,0:T(8,128)}), f32[64,16,512]{2,1,0:T(8,128)S(1)}, u32[]{:S(2)}, u32[]{:S(2)}) async-start(f32[64,16,512]{2,1,0:T(8,128)} %bitcast.19), calls=%async_computation.2 | async-start | bytes 4194304 | tf_op jit(solution)/shard_map/all_to_all | solution.py:383
  93.0 1.1 copy.30
  94.1 0.8 copy-done.1
  94.9 0.7 slice_bitcast_fusion.1.ds_ref
  95.6 19.1 %shard_map.112 = f32[256,16,128]{2,1,0:T(8,128)} custom-call(s32[1024]{0:T(1024)} %reshape.50.ids_ref, s32[64]{0:T(128)} %cnt_ref.3, bf16[64,16,128]{2,1,0:T(8,128)(2,1)} %slice_bitcast_fusion.1.ds_ref, s32[64,16,8,128]{3,2,1,0:T(8,128)} %tiles_ref.3), custom_call_target="tpu_custom_call" | custom-call | tf_op jit(solution)/shard_map/pallas_call | solution.py:109
  114.8 27.7 %all-to-all-done.1 = f32[64,16,512]{2,1,0:T(8,128)S(1)} async-done(((f32[64,16,512]{2,1,0:T(8,128)}), f32[64,16,512]{2,1,0:T(8,128)S(1)}, u32[]{:S(2)}, u32[]{:S(2)}) %all-to-all-start.1) | async-done | bytes 2097184 | tf_op jit(solution)/shard_map/all_to_all | solution.py:383
  142.7 17.3 %psum.7 = f32[16,512]{1,0:T(8,128)S(1)} all-reduce(f32[16,512]{1,0:T(8,128)S(1)} %reduce_sum.9), channel_id=1, replica_groups=mesh['feat'=64,'node'=4] {'node'}, use_global_device_ids=true, to_apply=%region_2.3 | all-reduce | flops 8192 | bytes 65536 | tf_op jit(solution)/shard_map/psum | solution.py:384
  160.0 0.6 slice_multiply_fusion
  160.6 1.9 %copy_bitcast_fusion = f32[8192,16]{0,1:T(8,128)} fusion(f32[64,16,128]{2,1,0:T(8,128)} %reduce-scatter.2.cloned.1.call-done, bf16[64,2,16,128]{3,2,0,1:T(8,128)(2,1)} %bitcast.56), kind=kLoop, calls=%fused_computation.9 | loop fusion | flops 262144 | bytes 1310720 | tf_op jit(solution)/shard_map/reshape | solution.py:401
  (22 shorter events, 0.9 us)
Async XLA Ops:
  7.2 1.6 copy-start
  7.2 2.7 %copy-start.4 = (bf16[16,256]{1,0:T(8,128)(2,1)S(1)}, bf16[16,256]{1,0:T(8,128)(2,1)}, u32[]{:S(2)}) copy-start(bf16[16,256]{1,0:T(8,128)(2,1)} %param.10) | copy-start | bytes 24580
  7.2 2.7 %copy-start.5 = (bf16[16,256]{1,0:T(8,128)(2,1)S(1)}, bf16[16,256]{1,0:T(8,128)(2,1)}, u32[]{:S(2)}) copy-start(bf16[16,256]{1,0:T(8,128)(2,1)} %param.9) | copy-start | bytes 24580
  55.2 1.4 copy-start.2
  55.2 1.7 %copy-start.3 = (bf16[64,1,16,128]{3,2,1,0:T(8,128)(2,1)S(1)}, bf16[64,1,16,128]{3,2,1,0:T(8,128)(2,1)}, u32[]{:S(2)}) copy-start(bf16[64,1,16,128]{3,2,1,0:T(8,128)(2,1)} %get-tuple-element.10) | copy-start | bytes 786436
  55.3 1.7 %copy-start.6 = (bf16[128,256]{1,0:T(8,128)(2,1)S(1)}, bf16[128,256]{1,0:T(8,128)(2,1)}, u32[]{:S(2)}) copy-start(bf16[128,256]{1,0:T(8,128)(2,1)} %param.12) | copy-start | bytes 196612
  55.3 1.7 %copy-start.7 = (f32[256]{0:T(256)S(1)}, f32[256]{0:T(256)}, u32[]{:S(2)}) copy-start(f32[256]{0:T(256)} %param.11) | copy-start | bytes 3076
  60.0 26.1 %all-to-all-start = ((bf16[64,1,2,16,128]{4,3,2,1,0:T(8,128)(2,1)}), bf16[64,1,2,16,128]{4,3,2,1,0:T(8,128)(2,1)}, u32[]{:S(2)}, u32[]{:S(2)}) async-start(bf16[64,1,2,16,128]{4,3,2,1,0:T(8,128)(2,1)} %maximum_bitcast_fusion), calls=%async_computation | async-start | bytes 1048576 | tf_op jit(solution)/shard_map/all_to_all | solution.py:394
  86.1 56.5 %all-to-all-start.1 = ((f32[64,16,512]{2,1,0:T(8,128)}), f32[64,16,512]{2,1,0:T(8,128)S(1)}, u32[]{:S(2)}, u32[]{:S(2)}) async-start(f32[64,16,512]{2,1,0:T(8,128)} %bitcast.19), calls=%async_computation.2 | async-start | bytes 4194304 | tf_op jit(solution)/shard_map/all_to_all | solution.py:383
  93.0 67.6 %reduce-scatter.2.cloned.1.call-start = ((), (), s32[]{:S(2)}) async-start(), calls=%async_computation.3 | async-start | bytes 2621440 | tf_op jit(solution)/shard_map/reduce_scatter | solution.py:399
  94.1 0.8 copy-start.1
Sparse Core Ops, SparseCore 0:
  114.9 33.4 reduce-scatter.1

commit v12 on v11

--- a/solution.py
+++ b/solution.py
@@ -267,6 +267,12 @@
         deg = out[cols : cols + 1, :]
         nm_scr[b] = (out[:cols, :] / jnp.maximum(deg, 1.0)).astype(nm_scr.dtype)
         deg_ref[b] = deg
+        k = lax.rem(b // per - me + parts, parts)
+
+        @pl.when(jnp.logical_and(k != 0, lax.rem(b + 1, per) == 0))
+        def _():
+            copy(2, k).start()
+
         return carry
 
     lax.fori_loop(0, blocks_here, row, 0)
@@ -287,11 +293,6 @@
     )
     to_sibling.start()
 
-    def start_result(k, carry):
-        copy(2, k).start()
-        return carry
-
-    lax.fori_loop(1, parts, start_result, 0)
     nm_out[me] = nm_scr[pl.ds(me * per, per)]
 
     def finish(k, carry):

time: 170 us -> 167 us (0.982)
  Pallas kernels: 63.9 us -> 59.9 us
    pallas_call x1, Pallas kernels: 44.7 us -> 40.7 us  [forward_exchange(): pl.pallas_call(functools.partial(forward_exchange_kernel, parts), out_sha...]
where the time goes in v12:
time: 167 us
  Pallas kernels  59.9 us (36%)
  waiting for transfers between devices  41.7 us (25%)
  starting transfers between devices  17.9 us (11%)
  blocking collectives  17.3 us (10%)
  between operations  14.2 us (9%)
  local copies, waits for them, and re-layouts  8.54 us (5%)
  other arithmetic  4.89 us (3%)
  matrix products  2.49 us (1%)
    pallas_call x1, Pallas kernels, forward_exchange(): pl.pallas_call(functools.partial(forward_exchange_kernel, parts), out_sha...  40.7 us
    all_to_all x1, waiting for transfers between devices, shards(): lax.all_to_all(part.reshape(feat_parts, cols, 2 * hidden), 'feat', 0, 0,...  27.7 us
    pallas_call x1, Pallas kernels, aggregate_backward(): pl.pallas_call(backward_kernel, grid_spec=pltpu.PrefetchScalarGridSpec(nu...  19.1 us
    psum x1, blocking collectives, shards(): grads = lax.psum(jnp.sum(part_got, axis=0), 'node')  17.3 us
    all_to_all x1, waiting for transfers between devices, shards(): lax.all_to_all(back, 'feat', 0, 0, tiled=True)  13.9 us
    all_to_all x1, starting transfers between devices, shards(): lax.all_to_all(back, 'feat', 0, 0, tiled=True)  11 us
    all_to_all x1, starting transfers between devices, shards(): lax.all_to_all(part.reshape(feat_parts, cols, 2 * hidden), 'feat', 0, 0,...  6.91 us
  transfers between devices with their start and end apart: 3, of which 2 were waited for; matrix products, arithmetic and copies ran while one was open for 3% of the time, Pallas kernels for 11%

profile of v12, /device:TPU:2, one launch (start us, length us, event | category | flops | bytes accessed | tf_op | source)
XLA Modules:
  0.0 166.9 jit_solution(15620131450932723957)
XLA Ops:
  7.2 0.9 copy.17
  8.1 0.7 reshape.50.ids_ref
  8.7 1.1 bitcast_bitcast_fusion.feat_ref
  9.9 0.6 pad_maximum_fusion.1.w_ref
  10.5 40.7 %shard_map.111 = (bf16[64,1,16,128]{3,2,1,0:T(8,128)(2,1)}, bf16[64,1,16,128]{3,2,1,0:T(8,128)(2,1)}, bf16[2,32,16,512]{3,2,1,0:T(8,128)(2,1)}, f32[64,1,128]{2,1,0:T(1,128)}) custom-call(s32[1024]{0:T(1024)} %reshape.50.ids_ref, s32[64]{0:T(128)} %cnt_ref.3, bf16[256,16,128]{2,1,0:T(8,128)(2,1)} %bitcast_bitcast_fusion.feat_ref, ...), custom_call_target="tpu_custom_call" | custom-call | tf_op jit(solution)/shard_map/pallas_call | solution.py:313
  51.3 1.4 copy.19
  53.0 1.0 fusion.13
  54.2 0.6 maximum_bitcast_fusion.1
  54.8 0.3 fusion.2
  55.1 0.8 maximum_bitcast_fusion
  56.0 11.0 %all-to-all-start = ((bf16[64,1,2,16,128]{4,3,2,1,0:T(8,128)(2,1)}), bf16[64,1,2,16,128]{4,3,2,1,0:T(8,128)(2,1)}, u32[]{:S(2)}, u32[]{:S(2)}) async-start(bf16[64,1,2,16,128]{4,3,2,1,0:T(8,128)(2,1)} %maximum_bitcast_fusion), calls=%async_computation | async-start | bytes 1048576 | tf_op jit(solution)/shard_map/all_to_all | solution.py:395
  67.0 0.3 fusion.15
  67.3 0.3 fusion.14
  67.8 1.9 %copy.24 = f32[1024,512]{1,0:T(8,128)} copy(f32[1024,512]{0,1:T(8,128)S(1)} %pad_maximum_fusion) | data formatting | bytes 4194304 | tf_op jit(solution)/shard_map/concatenate | solution.py:377
  69.7 13.9 %all-to-all-done = bf16[64,1,2,16,128]{4,3,2,1,0:T(8,128)(2,1)} async-done(((bf16[64,1,2,16,128]{4,3,2,1,0:T(8,128)(2,1)}), bf16[64,1,2,16,128]{4,3,2,1,0:T(8,128)(2,1)}, u32[]{:S(2)}, u32[]{:S(2)}) %all-to-all-start) | async-done | bytes 524320 | tf_op jit(solution)/shard_map/all_to_all | solution.py:395
  83.6 6.9 %all-to-all-start.1 = ((f32[64,16,512]{2,1,0:T(8,128)}), f32[64,16,512]{2,1,0:T(8,128)S(1)}, u32[]{:S(2)}, u32[]{:S(2)}) async-start(f32[64,16,512]{2,1,0:T(8,128)} %bitcast.19), calls=%async_computation.2 | async-start | bytes 4194304 | tf_op jit(solution)/shard_map/all_to_all | solution.py:384
  90.5 1.1 copy.30
  91.6 0.8 copy-done.1
  92.4 0.7 slice_bitcast_fusion.1.ds_ref
  93.2 19.1 %shard_map.112 = f32[256,16,128]{2,1,0:T(8,128)} custom-call(s32[1024]{0:T(1024)} %reshape.50.ids_ref, s32[64]{0:T(128)} %cnt_ref.3, bf16[64,16,128]{2,1,0:T(8,128)(2,1)} %slice_bitcast_fusion.1.ds_ref, s32[64,16,8,128]{3,2,1,0:T(8,128)} %tiles_ref.3), custom_call_target="tpu_custom_call" | custom-call | tf_op jit(solution)/shard_map/pallas_call | solution.py:109
  112.3 27.7 %all-to-all-done.1 = f32[64,16,512]{2,1,0:T(8,128)S(1)} async-done(((f32[64,16,512]{2,1,0:T(8,128)}), f32[64,16,512]{2,1,0:T(8,128)S(1)}, u32[]{:S(2)}, u32[]{:S(2)}) %all-to-all-start.1) | async-done | bytes 2097184 | tf_op jit(solution)/shard_map/all_to_all | solution.py:384
  140.2 17.3 %psum.7 = f32[16,512]{1,0:T(8,128)S(1)} all-reduce(f32[16,512]{1,0:T(8,128)S(1)} %reduce_sum.9), channel_id=1, replica_groups=mesh['feat'=64,'node'=4] {'node'}, use_global_device_ids=true, to_apply=%region_2.3 | all-reduce | flops 8192 | bytes 65536 | tf_op jit(solution)/shard_map/psum | solution.py:385
  157.5 0.6 slice_multiply_fusion
  158.1 1.9 %copy_bitcast_fusion = f32[8192,16]{0,1:T(8,128)} fusion(f32[64,16,128]{2,1,0:T(8,128)} %reduce-scatter.2.cloned.1.call-done, bf16[64,2,16,128]{3,2,0,1:T(8,128)(2,1)} %bitcast.56), kind=kLoop, calls=%fused_computation.9 | loop fusion | flops 262144 | bytes 1310720 | tf_op jit(solution)/shard_map/reshape | solution.py:402
  (22 shorter events, 0.9 us)
Async XLA Ops:
  7.2 1.6 copy-start
  7.2 2.7 %copy-start.4 = (bf16[16,256]{1,0:T(8,128)(2,1)S(1)}, bf16[16,256]{1,0:T(8,128)(2,1)}, u32[]{:S(2)}) copy-start(bf16[16,256]{1,0:T(8,128)(2,1)} %param.10) | copy-start | bytes 24580
  7.2 2.7 %copy-start.5 = (bf16[16,256]{1,0:T(8,128)(2,1)S(1)}, bf16[16,256]{1,0:T(8,128)(2,1)}, u32[]{:S(2)}) copy-start(bf16[16,256]{1,0:T(8,128)(2,1)} %param.9) | copy-start | bytes 24580
  51.2 1.4 copy-start.2
  51.2 1.7 %copy-start.3 = (bf16[64,1,16,128]{3,2,1,0:T(8,128)(2,1)S(1)}, bf16[64,1,16,128]{3,2,1,0:T(8,128)(2,1)}, u32[]{:S(2)}) copy-start(bf16[64,1,16,128]{3,2,1,0:T(8,128)(2,1)} %get-tuple-element.10) | copy-start | bytes 786436
  51.2 1.7 %copy-start.6 = (bf16[128,256]{1,0:T(8,128)(2,1)S(1)}, bf16[128,256]{1,0:T(8,128)(2,1)}, u32[]{:S(2)}) copy-start(bf16[128,256]{1,0:T(8,128)(2,1)} %param.12) | copy-start | bytes 196612
  51.3 1.7 %copy-start.7 = (f32[256]{0:T(256)S(1)}, f32[256]{0:T(256)}, u32[]{:S(2)}) copy-start(f32[256]{0:T(256)} %param.11) | copy-start | bytes 3076
  56.0 27.6 %all-to-all-start = ((bf16[64,1,2,16,128]{4,3,2,1,0:T(8,128)(2,1)}), bf16[64,1,2,16,128]{4,3,2,1,0:T(8,128)(2,1)}, u32[]{:S(2)}, u32[]{:S(2)}) async-start(bf16[64,1,2,16,128]{4,3,2,1,0:T(8,128)(2,1)} %maximum_bitcast_fusion), calls=%async_computation | async-start | bytes 1048576 | tf_op jit(solution)/shard_map/all_to_all | solution.py:395
  83.6 56.5 %all-to-all-start.1 = ((f32[64,16,512]{2,1,0:T(8,128)}), f32[64,16,512]{2,1,0:T(8,128)S(1)}, u32[]{:S(2)}, u32[]{:S(2)}) async-start(f32[64,16,512]{2,1,0:T(8,128)} %bitcast.19), calls=%async_computation.2 | async-start | bytes 4194304 | tf_op jit(solution)/shard_map/all_to_all | solution.py:384
  90.5 67.6 %reduce-scatter.2.cloned.1.call-start = ((), (), s32[]{:S(2)}) async-start(), calls=%async_computation.3 | async-start | bytes 2621440 | tf_op jit(solution)/shard_map/reduce_scatter | solution.py:400
  91.6 0.8 copy-start.1
Sparse Core Ops, SparseCore 0:
  112.4 33.4 reduce-scatter.1

commit v13 on v12

--- a/solution.py
+++ b/solution.py
@@ -382,7 +382,7 @@
         axis=1,
     )
     part_got = lax.all_to_all(part.reshape(feat_parts, cols, 2 * hidden), "feat", 0, 0, tiled=True)
-    grads = lax.psum(jnp.sum(part_got, axis=0), "node")
+    grads = jnp.sum(lax.all_gather(jnp.sum(part_got, axis=0), "node"), axis=0)
     grad_scale = 1.0 / math.sqrt(node_total)
     grad_self = grads[:, :hidden] * grad_scale
     grad_neigh = grads[:, hidden:] * grad_scale

time: 167 us -> 164 us (0.982); the launches traced: 167 us -> 162 us
  blocking collectives: 17.3 us -> 12.5 us
    psum x1 -> x0, blocking collectives: 17.3 us -> none  [shards(): grads = lax.psum(jnp.sum(part_got, axis=0), 'node')]
    all_gather x0 -> x1, blocking collectives: none -> 12.5 us  [shards(): grads = jnp.sum(lax.all_gather(jnp.sum(part_got, axis=0), 'node'), axis=0)]
  transfers between devices with their start and end apart: 3 -> 3, of which waited for: 2 -> 2; matrix products, arithmetic and copies ran while one was open for 3% -> 4% of each run, Pallas kernels for 11% -> 12%
where the time goes in v13:
time: 164 us; the launch traced here: 162 us
  Pallas kernels  59.9 us (37%)
  waiting for transfers between devices  40.7 us (25%)
  starting transfers between devices  17.9 us (11%)
  between operations  14.2 us (9%)
  blocking collectives  12.5 us (8%)
  local copies, waits for them, and re-layouts  9.51 us (6%)
  other arithmetic  4.98 us (3%)
  matrix products  2.48 us (2%)
    pallas_call x1, Pallas kernels, forward_exchange(): pl.pallas_call(functools.partial(forward_exchange_kernel, parts), out_sha...  40.7 us
    all_to_all x1, waiting for transfers between devices, shards(): lax.all_to_all(part.reshape(feat_parts, cols, 2 * hidden), 'feat', 0, 0,...  26.8 us
    pallas_call x1, Pallas kernels, aggregate_backward(): pl.pallas_call(backward_kernel, grid_spec=pltpu.PrefetchScalarGridSpec(nu...  19.1 us
    all_to_all x1, waiting for transfers between devices, shards(): lax.all_to_all(back, 'feat', 0, 0, tiled=True)  13.9 us
    all_gather x1, blocking collectives, shards(): grads = jnp.sum(lax.all_gather(jnp.sum(part_got, axis=0), 'node'), axis=0)  12.5 us
    all_to_all x1, starting transfers between devices, shards(): lax.all_to_all(back, 'feat', 0, 0, tiled=True)  11 us
    all_to_all x1, starting transfers between devices, shards(): lax.all_to_all(part.reshape(feat_parts, cols, 2 * hidden), 'feat', 0, 0,...  6.91 us
  transfers between devices with their start and end apart: 3, of which 2 were waited for; matrix products, arithmetic and copies ran while one was open for 4% of the time, Pallas kernels for 12%

profile of v13, /device:TPU:2, one launch (start us, length us, event | category | flops | bytes accessed | tf_op | source)
XLA Modules:
  0.0 162.2 jit_solution(12356000374260675475)
XLA Ops:
  7.2 0.9 copy.25
  8.1 0.7 reshape.50.ids_ref
  8.7 1.1 bitcast_bitcast_fusion.feat_ref
  9.9 0.6 pad_maximum_fusion.1.w_ref
  10.5 40.7 %shard_map.111 = (bf16[64,1,16,128]{3,2,1,0:T(8,128)(2,1)}, bf16[64,1,16,128]{3,2,1,0:T(8,128)(2,1)}, bf16[2,32,16,512]{3,2,1,0:T(8,128)(2,1)}, f32[64,1,128]{2,1,0:T(1,128)}) custom-call(s32[1024]{0:T(1024)} %reshape.50.ids_ref, s32[64]{0:T(128)} %cnt_ref.3, bf16[256,16,128]{2,1,0:T(8,128)(2,1)} %bitcast_bitcast_fusion.feat_ref, ...), custom_call_target="tpu_custom_call" | custom-call | tf_op jit(solution)/shard_map/pallas_call | solution.py:313
  51.3 1.4 copy.27
  53.0 1.0 fusion.13
  53.9 0.3 convolution_convert_fusion.1
  54.2 0.7 maximum_bitcast_fusion.1
  54.9 0.3 fusion.2
  55.2 0.8 maximum_bitcast_fusion
  56.1 11.0 %all-to-all-start = ((bf16[64,1,2,16,128]{4,3,2,1,0:T(8,128)(2,1)}), bf16[64,1,2,16,128]{4,3,2,1,0:T(8,128)(2,1)}, u32[]{:S(2)}, u32[]{:S(2)}) async-start(bf16[64,1,2,16,128]{4,3,2,1,0:T(8,128)(2,1)} %maximum_bitcast_fusion), calls=%async_computation | async-start | bytes 1048576 | tf_op jit(solution)/shard_map/all_to_all | solution.py:395
  67.0 0.3 fusion.15
  67.4 0.3 fusion.14
  67.9 1.9 %copy.32 = f32[1024,512]{1,0:T(8,128)} copy(f32[1024,512]{0,1:T(8,128)S(1)} %pad_maximum_fusion) | data formatting | bytes 4194304 | tf_op jit(solution)/shard_map/concatenate | solution.py:377
  69.7 13.9 %all-to-all-done = bf16[64,1,2,16,128]{4,3,2,1,0:T(8,128)(2,1)} async-done(((bf16[64,1,2,16,128]{4,3,2,1,0:T(8,128)(2,1)}), bf16[64,1,2,16,128]{4,3,2,1,0:T(8,128)(2,1)}, u32[]{:S(2)}, u32[]{:S(2)}) %all-to-all-start) | async-done | bytes 524320 | tf_op jit(solution)/shard_map/all_to_all | solution.py:395
  83.6 6.9 %all-to-all-start.1 = ((f32[64,16,512]{2,1,0:T(8,128)}), f32[64,16,512]{2,1,0:T(8,128)S(1)}, u32[]{:S(2)}, u32[]{:S(2)}) async-start(f32[64,16,512]{2,1,0:T(8,128)} %bitcast.19), calls=%async_computation.2 | async-start | bytes 4194304 | tf_op jit(solution)/shard_map/all_to_all | solution.py:384
  90.6 1.9 %copy.38 = bf16[64,1,2,16,128]{4,3,0,2,1:T(8,128)(2,1)} copy(bf16[64,1,2,16,128]{4,3,2,1,0:T(8,128)(2,1)} %all-to-all-done) | data formatting | bytes 1048576 | tf_op jit(solution)/shard_map/all_to_all | solution.py:395
  92.5 1.7 %slice_bitcast_fusion.1.ds_ref = bf16[64,16,128]{2,1,0:T(8,128)(2,1)} fusion(bf16[64,2,16,128]{3,2,0,1:T(8,128)(2,1)} %bitcast.51), kind=kLoop, calls=%fused_computation.20 | loop fusion | bytes 524288 | tf_op jit(solution)/shard_map/squeeze | solution.py:397
  94.2 19.1 %shard_map.112 = f32[256,16,128]{2,1,0:T(8,128)} custom-call(s32[1024]{0:T(1024)} %reshape.50.ids_ref, s32[64]{0:T(128)} %cnt_ref.3, bf16[64,16,128]{2,1,0:T(8,128)(2,1)} %slice_bitcast_fusion.1.ds_ref, s32[64,16,8,128]{3,2,1,0:T(8,128)} %tiles_ref.3), custom_call_target="tpu_custom_call" | custom-call | tf_op jit(solution)/shard_map/pallas_call | solution.py:109
  113.3 26.8 %all-to-all-done.1 = f32[64,16,512]{2,1,0:T(8,128)S(1)} async-done(((f32[64,16,512]{2,1,0:T(8,128)}), f32[64,16,512]{2,1,0:T(8,128)S(1)}, u32[]{:S(2)}, u32[]{:S(2)}) %all-to-all-start.1) | async-done | bytes 2097184 | tf_op jit(solution)/shard_map/all_to_all | solution.py:384
  140.2 12.5 %all-gather = f32[64,512]{1,0:T(8,128)S(1)} all-gather(f32[16,512]{1,0:T(8,128)S(1)} %reduce_sum.18), channel_id=2, replica_groups=mesh['feat'=64,'node'=4] {'node'}, dimensions={0}, use_global_device_ids=true | all-gather | bytes 163840 | tf_op jit(solution)/shard_map/all_gather | solution.py:385
  152.8 0.6 slice_multiply_fusion
  153.4 1.9 %copy_bitcast_fusion = f32[8192,16]{0,1:T(8,128)} fusion(f32[64,16,128]{2,1,0:T(8,128)} %reduce-scatter.2.cloned.1.call-done, bf16[64,2,16,128]{3,2,0,1:T(8,128)(2,1)} %bitcast.51), kind=kLoop, calls=%fused_computation.9 | loop fusion | flops 262144 | bytes 1310720 | tf_op jit(solution)/shard_map/reshape | solution.py:402
  (21 shorter events, 0.7 us)
Async XLA Ops:
  7.2 1.6 copy-start
  7.2 2.7 %copy-start.3 = (bf16[16,256]{1,0:T(8,128)(2,1)S(1)}, bf16[16,256]{1,0:T(8,128)(2,1)}, u32[]{:S(2)}) copy-start(bf16[16,256]{1,0:T(8,128)(2,1)} %param.10) | copy-start | bytes 24580
  7.2 2.7 %copy-start.4 = (bf16[16,256]{1,0:T(8,128)(2,1)S(1)}, bf16[16,256]{1,0:T(8,128)(2,1)}, u32[]{:S(2)}) copy-start(bf16[16,256]{1,0:T(8,128)(2,1)} %param.9) | copy-start | bytes 24580
  51.2 1.4 copy-start.1
  51.3 1.7 %copy-start.2 = (bf16[64,1,16,128]{3,2,1,0:T(8,128)(2,1)S(1)}, bf16[64,1,16,128]{3,2,1,0:T(8,128)(2,1)}, u32[]{:S(2)}) copy-start(bf16[64,1,16,128]{3,2,1,0:T(8,128)(2,1)} %get-tuple-element.10) | copy-start | bytes 786436
  51.3 1.7 %copy-start.5 = (bf16[128,256]{1,0:T(8,128)(2,1)S(1)}, bf16[128,256]{1,0:T(8,128)(2,1)}, u32[]{:S(2)}) copy-start(bf16[128,256]{1,0:T(8,128)(2,1)} %param.12) | copy-start | bytes 196612
  51.3 1.7 %copy-start.6 = (f32[256]{0:T(256)S(1)}, f32[256]{0:T(256)}, u32[]{:S(2)}) copy-start(f32[256]{0:T(256)} %param.11) | copy-start | bytes 3076
  56.1 27.6 %all-to-all-start = ((bf16[64,1,2,16,128]{4,3,2,1,0:T(8,128)(2,1)}), bf16[64,1,2,16,128]{4,3,2,1,0:T(8,128)(2,1)}, u32[]{:S(2)}, u32[]{:S(2)}) async-start(bf16[64,1,2,16,128]{4,3,2,1,0:T(8,128)(2,1)} %maximum_bitcast_fusion), calls=%async_computation | async-start | bytes 1048576 | tf_op jit(solution)/shard_map/all_to_all | solution.py:395
  83.6 56.5 %all-to-all-start.1 = ((f32[64,16,512]{2,1,0:T(8,128)}), f32[64,16,512]{2,1,0:T(8,128)S(1)}, u32[]{:S(2)}, u32[]{:S(2)}) async-start(f32[64,16,512]{2,1,0:T(8,128)} %bitcast.19), calls=%async_computation.2 | async-start | bytes 4194304 | tf_op jit(solution)/shard_map/all_to_all | solution.py:384
  90.6 62.8 %reduce-scatter.2.cloned.1.call-start = ((), (), s32[]{:S(2)}) async-start(), calls=%async_computation.3 | async-start | bytes 2621440 | tf_op jit(solution)/shard_map/reduce_scatter | solution.py:400
Sparse Core Ops, SparseCore 0:
  113.4 33.4 reduce-scatter.1

commit v14 on v13

--- a/solution.py
+++ b/solution.py
@@ -392,6 +392,7 @@
         .reshape(2, feat_parts, cols, per, block_size)
         .transpose(1, 3, 0, 2, 4)
     )
+    back = back.reshape(feat_parts, per * 2 * cols, block_size)
     got_back = lax.all_to_all(back, "feat", 0, 0, tiled=True).reshape(blocks_here, 2, cols, block_size)
     d_self_blocks = got_back[:, 0]
     d_scaled_blocks = got_back[:, 1]

time: 164 us -> 164 us (level)
  local copies, waits for them, and re-layouts: 9.51 us -> 7.58 us
  waiting for transfers between devices: 40.7 us -> 42.6 us
    all_to_all x1 -> x0, local copies, waits for them, and re-layouts: 1.89 us -> none  [shards(): lax.all_to_all(back, 'feat', 0, 0, tiled=True)]
    all_to_all x1, waiting for transfers between devices: 26.8 us -> 28.6 us  [shards(): lax.all_to_all(part.reshape(feat_parts, cols, 2 * hidden), 'feat', 0, 0,...]
  transfers between devices with their start and end apart: 3 -> 3, of which waited for: 2 -> 2; matrix products, arithmetic and copies ran while one was open for 4% -> 3% of each run, Pallas kernels for 12% -> 12%
where the time goes in v14:
time: 164 us; the launch traced here: 162 us
  Pallas kernels  59.9 us (37%)
  waiting for transfers between devices  42.6 us (26%)
  starting transfers between devices  17.9 us (11%)
  between operations  14.2 us (9%)
  blocking collectives  12.5 us (8%)
  local copies, waits for them, and re-layouts  7.58 us (5%)
  other arithmetic  4.98 us (3%)
  matrix products  2.48 us (2%)
    pallas_call x1, Pallas kernels, forward_exchange(): pl.pallas_call(functools.partial(forward_exchange_kernel, parts), out_sha...  40.7 us
    all_to_all x1, waiting for transfers between devices, shards(): lax.all_to_all(part.reshape(feat_parts, cols, 2 * hidden), 'feat', 0, 0,...  28.6 us
    pallas_call x1, Pallas kernels, aggregate_backward(): pl.pallas_call(backward_kernel, grid_spec=pltpu.PrefetchScalarGridSpec(nu...  19.2 us
    all_to_all x1, waiting for transfers between devices, shards(): lax.all_to_all(back, 'feat', 0, 0, tiled=True)  14 us
    all_gather x1, blocking collectives, shards(): grads = jnp.sum(lax.all_gather(jnp.sum(part_got, axis=0), 'node'), axis=0)  12.5 us
    all_to_all x1, starting transfers between devices, shards(): lax.all_to_all(back, 'feat', 0, 0, tiled=True)  11 us
    all_to_all x1, starting transfers between devices, shards(): lax.all_to_all(part.reshape(feat_parts, cols, 2 * hidden), 'feat', 0, 0,...  6.91 us
  transfers between devices with their start and end apart: 3, of which 2 were waited for; matrix products, arithmetic and copies ran while one was open for 3% of the time, Pallas kernels for 12%

profile of v14, /device:TPU:2, one launch (start us, length us, event | category | flops | bytes accessed | tf_op | source)
XLA Modules:
  0.0 162.2 jit_solution(6275193144454947222)
XLA Ops:
  7.2 0.9 copy.21
  8.1 0.7 reshape.53.ids_ref
  8.7 1.1 bitcast_bitcast_fusion.feat_ref
  9.9 0.6 pad_maximum_fusion.2.w_ref
  10.5 40.7 %shard_map.111 = (bf16[64,1,16,128]{3,2,1,0:T(8,128)(2,1)}, bf16[64,1,16,128]{3,2,1,0:T(8,128)(2,1)}, bf16[2,32,16,512]{3,2,1,0:T(8,128)(2,1)}, f32[64,1,128]{2,1,0:T(1,128)}) custom-call(s32[1024]{0:T(1024)} %reshape.53.ids_ref, s32[64]{0:T(128)} %cnt_ref.3, bf16[256,16,128]{2,1,0:T(8,128)(2,1)} %bitcast_bitcast_fusion.feat_ref, ...), custom_call_target="tpu_custom_call" | custom-call | tf_op jit(solution)/shard_map/pallas_call | solution.py:313
  51.3 1.4 copy.23
  52.7 0.3 fusion.8
  53.0 1.0 fusion.13
  53.9 0.3 convolution_convert_fusion.1
  54.2 0.7 maximum_bitcast_fusion
  54.9 0.3 fusion.2
  55.2 0.8 pad_maximum_fusion.1
  56.1 11.0 %all-to-all-start = ((bf16[64,32,128]{2,1,0:T(8,128)(2,1)}), bf16[64,32,128]{2,1,0:T(8,128)(2,1)}, u32[]{:S(2)}, u32[]{:S(2)}) async-start(bf16[64,32,128]{2,1,0:T(8,128)(2,1)} %bitcast.13), calls=%async_computation | async-start | bytes 1048576 | tf_op jit(solution)/shard_map/all_to_all | solution.py:396
  67.0 0.3 fusion.15
  67.4 0.3 fusion.14
  67.9 1.8 %copy.29 = f32[1024,512]{1,0:T(8,128)} copy(f32[1024,512]{0,1:T(8,128)S(1)} %pad_maximum_fusion) | data formatting | bytes 4194304 | tf_op jit(solution)/shard_map/concatenate | solution.py:377
  69.7 14.0 %all-to-all-done = bf16[64,32,128]{2,1,0:T(8,128)(2,1)} async-done(((bf16[64,32,128]{2,1,0:T(8,128)(2,1)}), bf16[64,32,128]{2,1,0:T(8,128)(2,1)}, u32[]{:S(2)}, u32[]{:S(2)}) %all-to-all-start) | async-done | bytes 524320 | tf_op jit(solution)/shard_map/all_to_all | solution.py:396
  83.6 6.9 %all-to-all-start.1 = ((f32[64,16,512]{2,1,0:T(8,128)}), f32[64,16,512]{2,1,0:T(8,128)S(1)}, u32[]{:S(2)}, u32[]{:S(2)}) async-start(f32[64,16,512]{2,1,0:T(8,128)} %bitcast.20), calls=%async_computation.2 | async-start | bytes 4194304 | tf_op jit(solution)/shard_map/all_to_all | solution.py:384
  90.6 1.7 %slice_bitcast_fusion.1.ds_ref = bf16[64,16,128]{2,1,0:T(8,128)(2,1)} fusion(bf16[64,2,16,128]{3,2,1,0:T(8,128)(2,1)} %bitcast.14), kind=kLoop, calls=%fused_computation.19 | loop fusion | bytes 524288 | tf_op jit(solution)/shard_map/squeeze | solution.py:398
  92.3 19.2 %shard_map.112 = f32[256,16,128]{2,1,0:T(8,128)} custom-call(s32[1024]{0:T(1024)} %reshape.53.ids_ref, s32[64]{0:T(128)} %cnt_ref.3, bf16[64,16,128]{2,1,0:T(8,128)(2,1)} %slice_bitcast_fusion.1.ds_ref, s32[64,16,8,128]{3,2,1,0:T(8,128)} %tiles_ref.3), custom_call_target="tpu_custom_call" | custom-call | tf_op jit(solution)/shard_map/pallas_call | solution.py:109
  111.5 28.6 %all-to-all-done.1 = f32[64,16,512]{2,1,0:T(8,128)S(1)} async-done(((f32[64,16,512]{2,1,0:T(8,128)}), f32[64,16,512]{2,1,0:T(8,128)S(1)}, u32[]{:S(2)}, u32[]{:S(2)}) %all-to-all-start.1) | async-done | bytes 2097184 | tf_op jit(solution)/shard_map/all_to_all | solution.py:384
  140.2 12.5 %all-gather = f32[64,512]{1,0:T(8,128)S(1)} all-gather(f32[16,512]{1,0:T(8,128)S(1)} %reduce_sum.18), channel_id=2, replica_groups=mesh['feat'=64,'node'=4] {'node'}, dimensions={0}, use_global_device_ids=true | all-gather | bytes 163840 | tf_op jit(solution)/shard_map/all_gather | solution.py:385
  152.8 0.6 slice_multiply_fusion
  153.4 1.9 %copy_bitcast_fusion = f32[8192,16]{0,1:T(8,128)} fusion(f32[64,16,128]{2,1,0:T(8,128)} %reduce-scatter.2.cloned.1.call-done, bf16[64,2,16,128]{3,2,1,0:T(8,128)(2,1)} %bitcast.14), kind=kLoop, calls=%fused_computation.9 | loop fusion | flops 262144 | bytes 1310720 | tf_op jit(solution)/shard_map/reshape | solution.py:403
  (20 shorter events, 0.4 us)
Async XLA Ops:
  7.2 1.6 copy-start
  7.2 2.7 %copy-start.3 = (bf16[16,256]{1,0:T(8,128)(2,1)S(1)}, bf16[16,256]{1,0:T(8,128)(2,1)}, u32[]{:S(2)}) copy-start(bf16[16,256]{1,0:T(8,128)(2,1)} %param.10) | copy-start | bytes 24580
  7.2 2.7 %copy-start.4 = (bf16[16,256]{1,0:T(8,128)(2,1)S(1)}, bf16[16,256]{1,0:T(8,128)(2,1)}, u32[]{:S(2)}) copy-start(bf16[16,256]{1,0:T(8,128)(2,1)} %param.9) | copy-start | bytes 24580
  51.2 1.4 copy-start.1
  51.3 1.7 %copy-start.2 = (bf16[64,1,16,128]{3,2,1,0:T(8,128)(2,1)S(1)}, bf16[64,1,16,128]{3,2,1,0:T(8,128)(2,1)}, u32[]{:S(2)}) copy-start(bf16[64,1,16,128]{3,2,1,0:T(8,128)(2,1)} %get-tuple-element.10) | copy-start | bytes 786436
  51.3 1.7 %copy-start.5 = (bf16[128,256]{1,0:T(8,128)(2,1)S(1)}, bf16[128,256]{1,0:T(8,128)(2,1)}, u32[]{:S(2)}) copy-start(bf16[128,256]{1,0:T(8,128)(2,1)} %param.12) | copy-start | bytes 196612
  51.3 1.7 %copy-start.6 = (f32[256]{0:T(256)S(1)}, f32[256]{0:T(256)}, u32[]{:S(2)}) copy-start(f32[256]{0:T(256)} %param.11) | copy-start | bytes 3076
  56.1 27.6 %all-to-all-start = ((bf16[64,32,128]{2,1,0:T(8,128)(2,1)}), bf16[64,32,128]{2,1,0:T(8,128)(2,1)}, u32[]{:S(2)}, u32[]{:S(2)}) async-start(bf16[64,32,128]{2,1,0:T(8,128)(2,1)} %bitcast.13), calls=%async_computation | async-start | bytes 1048576 | tf_op jit(solution)/shard_map/all_to_all | solution.py:396
  83.6 56.5 %all-to-all-start.1 = ((f32[64,16,512]{2,1,0:T(8,128)}), f32[64,16,512]{2,1,0:T(8,128)S(1)}, u32[]{:S(2)}, u32[]{:S(2)}) async-start(f32[64,16,512]{2,1,0:T(8,128)} %bitcast.20), calls=%async_computation.2 | async-start | bytes 4194304 | tf_op jit(solution)/shard_map/all_to_all | solution.py:384
  90.6 62.8 %reduce-scatter.2.cloned.1.call-start = ((), (), s32[]{:S(2)}) async-start(), calls=%async_computation.3 | async-start | bytes 2621440 | tf_op jit(solution)/shard_map/reduce_scatter | solution.py:401
Sparse Core Ops, SparseCore 0:
  111.6 33.4 reduce-scatter.1

commit v15 on v13

--- a/solution.py
+++ b/solution.py
@@ -381,20 +381,26 @@
         ],
         axis=1,
     )
-    part_got = lax.all_to_all(part.reshape(feat_parts, cols, 2 * hidden), "feat", 0, 0, tiled=True)
+    d_self_rows = d_self_t.astype(jnp.float32).reshape(feat_parts, cols, own_nodes)
+    late = jnp.concatenate([part.reshape(feat_parts, cols, 2 * hidden), d_self_rows], axis=2)
+    late_got = lax.all_to_all(late, "feat", 0, 0, tiled=True)
+    part_got = late_got[:, :, : 2 * hidden]
+    d_self_blocks = (
+        late_got[:, :, 2 * hidden :]
+        .astype(jnp.bfloat16)
+        .reshape(feat_parts, cols, per, block_size)
+        .transpose(0, 2, 1, 3)
+        .reshape(blocks_here, cols, block_size)
+    )
     grads = jnp.sum(lax.all_gather(jnp.sum(part_got, axis=0), "node"), axis=0)
     grad_scale = 1.0 / math.sqrt(node_total)
     grad_self = grads[:, :hidden] * grad_scale
     grad_neigh = grads[:, hidden:] * grad_scale
 
-    back = (
-        jnp.stack([d_self_t, d_scaled_t], axis=0)
-        .reshape(2, feat_parts, cols, per, block_size)
-        .transpose(1, 3, 0, 2, 4)
-    )
-    got_back = lax.all_to_all(back, "feat", 0, 0, tiled=True).reshape(blocks_here, 2, cols, block_size)
-    d_self_blocks = got_back[:, 0]
-    d_scaled_blocks = got_back[:, 1]
+    back = d_scaled_t.reshape(feat_parts, cols, per, block_size).transpose(0, 2, 1, 3)
+    d_scaled_blocks = lax.all_to_all(back, "feat", 0, 0, tiled=True).reshape(
+        blocks_here, cols, block_size
+    )
 
     grad_all = aggregate_backward(ids_flat, nbr_count, d_scaled_blocks, tiles, all_blocks)
     grad_group = lax.psum_scatter(grad_all, "node", scatter_dimension=0, tiled=True)

time: 164 us -> 173 us (1.055)
  other arithmetic: 4.98 us -> 10.9 us
  waiting for transfers between devices: 40.7 us -> 45.8 us
  local copies, waits for them, and re-layouts: 9.51 us -> 6.61 us
    all_to_all x1, waiting for transfers between devices: 26.8 us -> 41.6 us  [shards(): late_got = lax.all_to_all(late, 'feat', 0, 0, tiled=True)]
    all_to_all x1, waiting for transfers between devices: 13.9 us -> 4.21 us  [shards(): lax.all_to_all(back, 'feat', 0, 0, tiled=True)]
    concatenate x0 -> x1, other arithmetic: none -> 3.54 us  [shards(): jnp.concatenate([part.reshape(feat_parts, cols, 2 * hidden), d_self_rows]...]
    all_to_all x1 -> x0, local copies, waits for them, and re-layouts: 1.89 us -> none  [shards(): lax.all_to_all(back, 'feat', 0, 0, tiled=True)]
  transfers between devices with their start and end apart: 3 -> 3, of which waited for: 2 -> 2; matrix products, arithmetic and copies ran while one was open for 4% -> 6% of each run, Pallas kernels for 12% -> 11%
where the time goes in v15:
time: 173 us; the launch traced here: 171 us
  Pallas kernels  59.9 us (35%)
  waiting for transfers between devices  45.8 us (26%)
  starting transfers between devices  17.4 us (10%)
  between operations  14.2 us (8%)
  blocking collectives  12.5 us (7%)
  other arithmetic  10.9 us (6%)
  local copies, waits for them, and re-layouts  6.61 us (4%)
  matrix products  4.16 us (2%)
    all_to_all x1, waiting for transfers between devices, shards(): late_got = lax.all_to_all(late, 'feat', 0, 0, tiled=True)  41.6 us
    pallas_call x1, Pallas kernels, forward_exchange(): pl.pallas_call(functools.partial(forward_exchange_kernel, parts), out_sha...  40.7 us
    pallas_call x1, Pallas kernels, aggregate_backward(): pl.pallas_call(backward_kernel, grid_spec=pltpu.PrefetchScalarGridSpec(nu...  19.2 us
    all_gather x1, blocking collectives, shards(): grads = jnp.sum(lax.all_gather(jnp.sum(part_got, axis=0), 'node'), axis=0)  12.5 us
    all_to_all x1, starting transfers between devices, shards(): lax.all_to_all(back, 'feat', 0, 0, tiled=True)  10.7 us
    all_to_all x1, starting transfers between devices, shards(): late_got = lax.all_to_all(late, 'feat', 0, 0, tiled=True)  6.65 us
    all_to_all x1, waiting for transfers between devices, shards(): lax.all_to_all(back, 'feat', 0, 0, tiled=True)  4.21 us
    concatenate x1, other arithmetic, shards(): jnp.concatenate([part.reshape(feat_parts, cols, 2 * hidden), d_self_rows]...  3.54 us
  transfers between devices with their start and end apart: 3, of which 2 were waited for; matrix products, arithmetic and copies ran while one was open for 6% of the time, Pallas kernels for 11%

profile of v15, /device:TPU:2, one launch (start us, length us, event | category | flops | bytes accessed | tf_op | source)
XLA Modules:
  0.0 171.5 jit_solution(8562436611764401287)
XLA Ops:
  7.2 0.9 copy.24
  8.1 0.7 reshape.49.ids_ref
  8.7 1.1 bitcast_bitcast_fusion.feat_ref
  9.9 1.3 pad_maximum_fusion.2.w_ref
  11.2 40.7 %shard_map.111 = (bf16[64,1,16,128]{3,2,1,0:T(8,128)(2,1)}, bf16[64,1,16,128]{3,2,1,0:T(8,128)(2,1)}, bf16[2,32,16,512]{3,2,1,0:T(8,128)(2,1)}, f32[64,1,128]{2,1,0:T(1,128)}) custom-call(s32[1024]{0:T(1024)} %reshape.49.ids_ref, s32[64]{0:T(128)} %cnt_ref.3, bf16[256,16,128]{2,1,0:T(8,128)(2,1)} %bitcast_bitcast_fusion.feat_ref, ...), custom_call_target="tpu_custom_call" | custom-call | tf_op jit(solution)/shard_map/pallas_call | solution.py:313
  52.0 1.4 copy.26
  53.3 0.7 maximum_bitcast_fusion
  54.0 1.2 fusion.7
  55.2 1.0 fusion.12
  56.2 1.0 fusion.2
  57.2 10.7 %all-to-all-start = ((bf16[64,1,16,128]{3,2,1,0:T(8,128)(2,1)}), bf16[64,1,16,128]{3,2,1,0:T(8,128)(2,1)S(1)}, u32[]{:S(2)}, u32[]{:S(2)}) async-start(bf16[64,1,16,128]{3,2,1,0:T(8,128)(2,1)} %bitcast.9), calls=%async_computation | async-start | bytes 524288 | tf_op jit(solution)/shard_map/all_to_all | solution.py:401
  68.3 0.3 fusion.14
  68.6 0.8 convert.5
  69.9 1.8 %copy.28 = f32[1024,512]{1,0:T(8,128)} copy(f32[1024,512]{0,1:T(8,128)S(1)} %pad_maximum_fusion.1) | data formatting | bytes 4194304 | tf_op jit(solution)/shard_map/concatenate | solution.py:377
  71.8 3.5 %pad_maximum_fusion = f32[64,16,640]{2,1,0:T(8,128)} fusion(f32[64,16,128]{2,1,0:T(8,128)} %convert.5, f32[64,16,512]{2,1,0:T(8,128)} %bitcast.39), kind=kLoop, calls=%fused_computation | loop fusion | flops 655360 | bytes 5242880 | tf_op jit(solution)/shard_map/concatenate | solution.py:385
  75.3 4.2 %all-to-all-done = bf16[64,1,16,128]{3,2,1,0:T(8,128)(2,1)S(1)} async-done(((bf16[64,1,16,128]{3,2,1,0:T(8,128)(2,1)}), bf16[64,1,16,128]{3,2,1,0:T(8,128)(2,1)S(1)}, u32[]{:S(2)}, u32[]{:S(2)}) %all-to-all-start) | async-done | bytes 262176 | tf_op jit(solution)/shard_map/all_to_all | solution.py:401
  79.5 0.7 copy-done.1
  80.2 6.7 %all-to-all-start.1 = ((f32[64,16,640]{2,1,0:T(8,128)}), f32[64,16,640]{2,1,0:T(8,128)}, u32[]{:S(2)}, u32[]{:S(2)}) async-start(f32[64,16,640]{2,1,0:T(8,128)} %pad_maximum_fusion), calls=%async_computation.2 | async-start | bytes 5242880 | tf_op jit(solution)/shard_map/all_to_all | solution.py:386
  86.9 19.2 %shard_map.112 = f32[256,16,128]{2,1,0:T(8,128)} custom-call(s32[1024]{0:T(1024)} %reshape.49.ids_ref, s32[64]{0:T(128)} %cnt_ref.3, bf16[64,16,128]{2,1,0:T(8,128)(2,1)} %bitcast.44, s32[64,16,8,128]{3,2,1,0:T(8,128)} %tiles_ref.3), custom_call_target="tpu_custom_call" | custom-call | tf_op jit(solution)/shard_map/pallas_call | solution.py:109
  106.1 41.6 %all-to-all-done.1 = f32[64,16,640]{2,1,0:T(8,128)} async-done(((f32[64,16,640]{2,1,0:T(8,128)}), f32[64,16,640]{2,1,0:T(8,128)}, u32[]{:S(2)}, u32[]{:S(2)}) %all-to-all-start.1) | async-done | bytes 2621472 | tf_op jit(solution)/shard_map/all_to_all | solution.py:386
  147.7 1.7 %slice_reduce_fusion = f32[16,512]{1,0:T(8,128)S(1)} fusion(f32[64,16,640]{2,1,0:T(8,128)} %all-to-all-done.1), kind=kLoop, calls=%fused_computation.1 | loop fusion | flops 516096 | bytes 2129920 | tf_op jit(solution)/shard_map/reduce_sum | solution.py:395
  149.4 12.5 %all-gather = f32[64,512]{1,0:T(8,128)S(1)} all-gather(f32[16,512]{1,0:T(8,128)S(1)} %slice_reduce_fusion), channel_id=2, replica_groups=mesh['feat'=64,'node'=4] {'node'}, dimensions={0}, use_global_device_ids=true | all-gather | bytes 163840 | tf_op jit(solution)/shard_map/all_gather | solution.py:395
  162.0 0.6 slice_multiply_fusion
  162.6 2.0 %copy_bitcast_fusion = f32[8192,16]{0,1:T(8,128)} fusion(f32[64,16,128]{2,1,0:T(8,128)} %reduce-scatter.2.cloned.1.call-done, f32[64,16,640]{2,1,0:T(8,128)} %all-to-all-done.1), kind=kLoop, calls=%fused_computation.11 | loop fusion | flops 262144 | bytes 1310720 | tf_op jit(solution)/shard_map/reshape | solution.py:408
  (18 shorter events, 0.9 us)
Async XLA Ops:
  7.2 1.6 copy-start
  51.9 3.3 %copy-start.3 = (bf16[64,1,16,128]{3,2,1,0:T(8,128)(2,1)S(1)}, bf16[64,1,16,128]{3,2,1,0:T(8,128)(2,1)}, u32[]{:S(2)}) copy-start(bf16[64,1,16,128]{3,2,1,0:T(8,128)(2,1)} %get-tuple-element.10) | copy-start | bytes 786436
  51.9 3.3 %copy-start.4 = (bf16[128,256]{1,0:T(8,128)(2,1)S(1)}, bf16[128,256]{1,0:T(8,128)(2,1)}, u32[]{:S(2)}) copy-start(bf16[128,256]{1,0:T(8,128)(2,1)} %param.12) | copy-start | bytes 196612
  51.9 3.3 %copy-start.5 = (f32[256]{0:T(256)S(1)}, f32[256]{0:T(256)}, u32[]{:S(2)}) copy-start(f32[256]{0:T(256)} %param.11) | copy-start | bytes 3076
  56.2 13.2 %copy-start.2 = (bf16[64,1,16,128]{3,2,1,0:T(8,128)(2,1)S(1)}, bf16[64,1,16,128]{3,2,1,0:T(8,128)(2,1)}, u32[]{:S(2)}) copy-start(bf16[64,1,16,128]{3,2,1,0:T(8,128)(2,1)} %get-tuple-element.8) | copy-start | bytes 786436
  57.2 22.3 %all-to-all-start = ((bf16[64,1,16,128]{3,2,1,0:T(8,128)(2,1)}), bf16[64,1,16,128]{3,2,1,0:T(8,128)(2,1)S(1)}, u32[]{:S(2)}, u32[]{:S(2)}) async-start(bf16[64,1,16,128]{3,2,1,0:T(8,128)(2,1)} %bitcast.9), calls=%async_computation | async-start | bytes 524288 | tf_op jit(solution)/shard_map/all_to_all | solution.py:401
  79.5 0.7 copy-start.1
  80.2 67.5 %all-to-all-start.1 = ((f32[64,16,640]{2,1,0:T(8,128)}), f32[64,16,640]{2,1,0:T(8,128)}, u32[]{:S(2)}, u32[]{:S(2)}) async-start(f32[64,16,640]{2,1,0:T(8,128)} %pad_maximum_fusion), calls=%async_computation.2 | async-start | bytes 5242880 | tf_op jit(solution)/shard_map/all_to_all | solution.py:386
  86.9 75.7 %reduce-scatter.2.cloned.1.call-start = ((), (), s32[]{:S(2)}) async-start(), calls=%async_computation.3 | async-start | bytes 2621440 | tf_op jit(solution)/shard_map/reduce_scatter | solution.py:406
Sparse Core Ops, SparseCore 0:
  106.3 33.4 reduce-scatter.1
